TPU v7x, 32 devices: a whole 2x2x4 slice. The times are simulated.
32 devices in a mesh: fsdp: 16 (over z, y, core), tp: 2 (over x).
Axes of the slice: x: 2, y: 2, z: 4, core: 2. Of those that a mesh axis runs over, the one named last changes fastest.
Arguments:
- tokens: bfloat16 [32768, 768], P(('fsdp', 'tp')), may hold values from -6 to 6
- lengths: int32 [64], P('fsdp'), may hold values from 32 to 512, as said below
- cotangent: bfloat16 [32768, 768], P(('fsdp', 'tp')), may hold values from -6 to 6
- w_query: float32 [768, 768], P('fsdp', 'tp'), may hold values from -0.21875 to 0.21875
- w_key: float32 [768, 768], P('fsdp', 'tp'), may hold values from -0.21875 to 0.21875
- w_value: float32 [768, 768], P('fsdp', 'tp'), may hold values from -0.21875 to 0.21875
- w_output: float32 [768, 768], P('tp', 'fsdp'), may hold values from -1.75 to 1.75
- w_inner: float32 [768, 3072], P('fsdp', 'tp'), may hold values from -0.21875 to 0.21875
- w_outer: float32 [3072, 768], P('tp', 'fsdp'), may hold values from -0.109375 to 0.109375
- bias_query: float32 [768], P('tp'), may hold values from -3 to 3
- bias_value: float32 [768], P('tp'), may hold values from -3 to 3
- bias_output: float32 [768], replicated, may hold values from -3 to 3
- norm1_gain: float32 [768], replicated, may hold values from 0.25 to 1.75
- norm1_bias: float32 [768], replicated, may hold values from -3 to 3
- bias_inner: float32 [3072], P('tp'), may hold values from -3 to 3
- bias_outer: float32 [768], replicated, may hold values from -3 to 3
- norm2_gain: float32 [768], replicated, may hold values from 0.25 to 1.75
- norm2_bias: float32 [768], replicated, may hold values from -3 to 3
Outputs:
- mixed_out: bfloat16 [32768, 768], P(('fsdp', 'tp'))
- grad_tokens: float32 [32768, 768], P(('fsdp', 'tp'))
- grad_w_query: float32 [768, 768], P('fsdp', 'tp')
- grad_w_key: float32 [768, 768], P('fsdp', 'tp')
- grad_w_value: float32 [768, 768], P('fsdp', 'tp')
- grad_w_output: float32 [768, 768], P('tp', 'fsdp')
- grad_w_inner: float32 [768, 3072], P('fsdp', 'tp')
- grad_w_outer: float32 [3072, 768], P('tp', 'fsdp')
- grad_bias_query: float32 [768], P('tp')
- grad_bias_value: float32 [768], P('tp')
- grad_bias_output: float32 [768], replicated
- grad_norm1_gain: float32 [768], replicated
- grad_norm1_bias: float32 [768], replicated
- grad_bias_inner: float32 [3072], P('tp')
- grad_bias_outer: float32 [768], replicated
- grad_norm2_gain: float32 [768], replicated
- grad_norm2_bias: float32 [768], replicated
Inputs may be any that keep to these rules, and one draw needn't show every extreme that they name: `lengths`: the number of leading tokens of each sequence that are not padding; keys at later positions are masked for every query.
All inputs are finite; a program needn't handle non-finite values.
Results may differ from a plain program's by a relative error of at most 0.014.
The roundings to bfloat16 on the way count: a program that leaves them out, or rounds other values in their place, can miss the bound.
Values may be sent and summed in bfloat16 or wider, within the bound.
No kernel may reach another device: no remote copies, remote signals or barrier semaphores. Data moves between devices by JAX's collectives and lax.ppermute only.
A program may use at most 192 MiB of HBM per device.

v0:
```python
import jax
import jax.numpy as jnp
from jax import lax
from jax.sharding import PartitionSpec as P

DH = 64
SEQ = 512


norm_eps = 1e-12
masked_score = -1000000000.0


def norm_rows(values, gain, shift):
    row_mean = jnp.mean(values, axis=-1, keepdims=True)
    centred = values - row_mean
    row_var = jnp.mean(centred * centred, axis=-1, keepdims=True)
    return centred * lax.rsqrt(row_var + norm_eps) * gain + shift


def exact_gelu(values):
    return jax.nn.gelu(values, approximate=False)


def matmul(left, right):
    return jnp.dot(left, right, preferred_element_type=jnp.float32)


def matmul_tn(left, right):
    return lax.dot_general(
        left, right, (((0,), (0,)), ((), ())), preferred_element_type=jnp.float32
    )


def matmul_nt(left, right):
    return lax.dot_general(
        left, right, (((1,), (1,)), ((), ())), preferred_element_type=jnp.float32
    )


def head_scores(query, key_rows, length):
    seq_len = query.shape[0]
    head_count = query.shape[1] // DH
    scores = jnp.einsum(
        "qhd,khd->hqk",
        query.reshape(seq_len, head_count, DH),
        key_rows.reshape(seq_len, head_count, DH),
        preferred_element_type=jnp.float32,
    ) * DH ** (-0.5)
    key_live = jnp.arange(seq_len) < length
    return jnp.where(key_live[None, None, :], scores, masked_score)


def attend_forward(pieces):
    query, key_rows, value, length = pieces
    seq_len = query.shape[0]
    head_count = query.shape[1] // DH
    scores = head_scores(query, key_rows, length)
    row_max = jnp.max(scores, axis=-1, keepdims=True)
    expo = jnp.exp(scores - row_max)
    row_sum = jnp.sum(expo, axis=-1, keepdims=True)
    probs = (expo / row_sum).astype(jnp.bfloat16)
    context = jnp.einsum(
        "hqk,khd->qhd",
        probs,
        value.reshape(seq_len, head_count, DH),
        preferred_element_type=jnp.float32,
    )
    log_total = (row_max + jnp.log(row_sum))[:, :, 0]
    return (context.reshape(seq_len, head_count * DH).astype(jnp.bfloat16), log_total)


def attend_backward(pieces):
    query, key_rows, value, d_context, log_total, length = pieces
    seq_len = query.shape[0]
    head_count = query.shape[1] // DH
    scores = head_scores(query, key_rows, length)
    probs = jnp.exp(scores - log_total[:, :, None])
    query_three = query.reshape(seq_len, head_count, DH)
    key_three = key_rows.reshape(seq_len, head_count, DH)
    value_three = value.reshape(seq_len, head_count, DH)
    dctx_three = d_context.reshape(seq_len, head_count, DH)
    d_probs = jnp.einsum(
        "qhd,khd->hqk", dctx_three, value_three, preferred_element_type=jnp.float32
    )
    row_dot = jnp.sum(d_probs * probs, axis=-1, keepdims=True)
    d_scores = (probs * (d_probs - row_dot)).astype(jnp.bfloat16)
    d_query = (
        jnp.einsum("hqk,khd->qhd", d_scores, key_three, preferred_element_type=jnp.float32)
        * DH ** (-0.5)
    ).astype(jnp.bfloat16)
    d_key = (
        jnp.einsum("hqk,qhd->khd", d_scores, query_three, preferred_element_type=jnp.float32)
        * DH ** (-0.5)
    ).astype(jnp.bfloat16)
    d_value = jnp.einsum(
        "hqk,qhd->khd", probs.astype(jnp.bfloat16), dctx_three, preferred_element_type=jnp.float32
    ).astype(jnp.bfloat16)
    width = head_count * DH
    return (
        d_query.reshape(seq_len, width),
        d_key.reshape(seq_len, width),
        d_value.reshape(seq_len, width),
    )


def rows_times(grads, weight):
    return matmul_nt(grads, weight)


def shards(
    tokens,
    lengths,
    cotangent,
    w_query,
    w_key,
    w_value,
    w_output,
    w_inner,
    w_outer,
    bias_query,
    bias_value,
    bias_output,
    norm1_gain,
    norm1_bias,
    bias_inner,
    bias_outer,
    norm2_gain,
    norm2_bias,
):
    low_weights = (
        w_query.astype(jnp.bfloat16),
        w_key.astype(jnp.bfloat16),
        w_value.astype(jnp.bfloat16),
        w_output.astype(jnp.bfloat16),
        w_inner.astype(jnp.bfloat16),
        w_outer.astype(jnp.bfloat16),
    )
    tp_index = lax.axis_index("tp")
    tp_count = lax.axis_size("tp")
    query_shift, value_shift, inner_shift = (bias_query, bias_value, bias_inner)
    wq, wk, wv, wo, wi, wu = (
        lax.all_gather(low_weights[0], "fsdp", axis=0, tiled=True),
        lax.all_gather(low_weights[1], "fsdp", axis=0, tiled=True),
        lax.all_gather(low_weights[2], "fsdp", axis=0, tiled=True),
        lax.all_gather(low_weights[3], "fsdp", axis=1, tiled=True),
        lax.all_gather(low_weights[4], "fsdp", axis=0, tiled=True),
        lax.all_gather(low_weights[5], "fsdp", axis=1, tiled=True),
    )
    every_row = lax.all_gather(tokens, "tp", axis=0, tiled=True)
    query = (matmul(every_row, wq) + query_shift).astype(jnp.bfloat16)
    key_rows = matmul(every_row, wk).astype(jnp.bfloat16)
    value = (matmul(every_row, wv) + value_shift).astype(jnp.bfloat16)
    seq_count = every_row.shape[0] // SEQ
    width = query.shape[1]
    query_seq = query.reshape(seq_count, SEQ, width)
    key_seq = key_rows.reshape(seq_count, SEQ, width)
    value_seq = value.reshape(seq_count, SEQ, width)
    context, log_total = lax.map(attend_forward, (query_seq, key_seq, value_seq, lengths))
    context = context.reshape(seq_count * SEQ, width)
    attention = lax.psum_scatter(matmul(context, wo), "tp", scatter_dimension=0, tiled=True)
    summed = attention + bias_output + tokens.astype(jnp.float32)
    normed, norm1_pull = jax.vjp(norm_rows, summed, norm1_gain, norm1_bias)
    all_normed = lax.all_gather(normed.astype(jnp.bfloat16), "tp", axis=0, tiled=True)
    inner = matmul(all_normed, wi) + inner_shift
    hidden, gelu_pull = jax.vjp(exact_gelu, inner)
    hidden16 = hidden.astype(jnp.bfloat16)
    ffn_out = lax.psum_scatter(matmul(hidden16, wu), "tp", scatter_dimension=0, tiled=True)
    before_norm = ffn_out + bias_outer + normed
    mixed, norm2_pull = jax.vjp(norm_rows, before_norm, norm2_gain, norm2_bias)
    wq, wk, wv, wo, wi, wu = (
        lax.all_gather(low_weights[0], "fsdp", axis=0, tiled=True),
        lax.all_gather(low_weights[1], "fsdp", axis=0, tiled=True),
        lax.all_gather(low_weights[2], "fsdp", axis=0, tiled=True),
        lax.all_gather(low_weights[3], "fsdp", axis=1, tiled=True),
        lax.all_gather(low_weights[4], "fsdp", axis=0, tiled=True),
        lax.all_gather(low_weights[5], "fsdp", axis=1, tiled=True),
    )
    d_before, grad_gain_two, grad_shift_two = norm2_pull(cotangent.astype(jnp.float32))
    grad_outer_bias = jnp.sum(d_before, axis=0)
    all_dffn = lax.all_gather(d_before.astype(jnp.bfloat16), "tp", axis=0, tiled=True)
    grad_outer = matmul_tn(hidden16, all_dffn)
    d_hidden = matmul_nt(all_dffn, wu)
    d_inner = gelu_pull(d_hidden)[0].astype(jnp.bfloat16)
    grad_inner_bias = jnp.sum(d_inner.astype(jnp.float32), axis=0)
    grad_inner = matmul_tn(all_normed, d_inner)
    d_normed = d_before + lax.psum_scatter(
        rows_times(d_inner, wi), "tp", scatter_dimension=0, tiled=True
    )
    d_summed, grad_gain_one, grad_shift_one = norm1_pull(d_normed)
    grad_output_bias = jnp.sum(d_summed, axis=0)
    all_dattn = lax.all_gather(d_summed.astype(jnp.bfloat16), "tp", axis=0, tiled=True)
    grad_output = matmul_tn(context, all_dattn)
    d_context = matmul_nt(all_dattn, wo).astype(jnp.bfloat16)
    d_query, d_key, d_value = lax.map(
        attend_backward,
        (
            query_seq,
            key_seq,
            value_seq,
            d_context.reshape(seq_count, SEQ, width),
            log_total,
            lengths,
        ),
    )
    d_query = d_query.reshape(seq_count * SEQ, width)
    d_key = d_key.reshape(seq_count * SEQ, width)
    d_value = d_value.reshape(seq_count * SEQ, width)
    grad_query_bias = jnp.sum(d_query.astype(jnp.float32), axis=0)
    grad_value_bias = jnp.sum(d_value.astype(jnp.float32), axis=0)
    grad_query = matmul_tn(every_row, d_query)
    grad_key = matmul_tn(every_row, d_key)
    grad_value = matmul_tn(every_row, d_value)
    grad_tokens = d_summed + lax.psum_scatter(
        (rows_times(d_query, wq) + rows_times(d_key, wk) + rows_times(d_value, wv)).astype(
            jnp.bfloat16
        ),
        "tp",
        scatter_dimension=0,
        tiled=True,
    ).astype(jnp.float32)
    weight_terms = (grad_query, grad_key, grad_value, grad_output, grad_inner, grad_outer)
    sum_query, sum_key, sum_value, sum_output, sum_inner, sum_outer = (
        lax.psum_scatter(weight_terms[0], "fsdp", scatter_dimension=0, tiled=True),
        lax.psum_scatter(weight_terms[1], "fsdp", scatter_dimension=0, tiled=True),
        lax.psum_scatter(weight_terms[2], "fsdp", scatter_dimension=0, tiled=True),
        lax.psum_scatter(weight_terms[3], "fsdp", scatter_dimension=1, tiled=True),
        lax.psum_scatter(weight_terms[4], "fsdp", scatter_dimension=0, tiled=True),
        lax.psum_scatter(weight_terms[5], "fsdp", scatter_dimension=1, tiled=True),
    )

    def widen(piece):
        spread_out = jnp.zeros((piece.shape[0] * tp_count,), jnp.float32)
        return lax.dynamic_update_slice_in_dim(spread_out, piece, tp_index * piece.shape[0], 0)

    def narrow(whole_vec, piece_len):
        return lax.dynamic_slice_in_dim(whole_vec, tp_index * piece_len, piece_len, 0)

    sliced_terms = (widen(grad_query_bias), widen(grad_value_bias), widen(grad_inner_bias))
    small_sums = lax.psum(
        (
            sliced_terms[0],
            sliced_terms[1],
            sliced_terms[2],
            grad_output_bias,
            grad_gain_one,
            grad_shift_one,
            grad_outer_bias,
            grad_gain_two,
            grad_shift_two,
        ),
        ("fsdp", "tp"),
    )
    query_bias_sum = narrow(small_sums[0], bias_query.shape[0])
    value_bias_sum = narrow(small_sums[1], bias_value.shape[0])
    inner_bias_sum = narrow(small_sums[2], bias_inner.shape[0])
    return (
        mixed.astype(jnp.bfloat16),
        grad_tokens,
        sum_query,
        sum_key,
        sum_value,
        sum_output,
        sum_inner,
        sum_outer,
        query_bias_sum,
        value_bias_sum,
        small_sums[3],
        small_sums[4],
        small_sums[5],
        inner_bias_sum,
        small_sums[6],
        small_sums[7],
        small_sums[8],
    )


def solution(mesh):
    return jax.shard_map(
        shards,
        mesh=mesh,
        in_specs=(
            P(("fsdp", "tp"), None),
            P("fsdp"),
            P(("fsdp", "tp"), None),
            P("fsdp", "tp"),
            P("fsdp", "tp"),
            P("fsdp", "tp"),
            P("tp", "fsdp"),
            P("fsdp", "tp"),
            P("tp", "fsdp"),
            P("tp"),
            P("tp"),
            P(),
            P(),
            P(),
            P("tp"),
            P(),
            P(),
            P(),
        ),
        out_specs=(
            P(("fsdp", "tp"), None),
            P(("fsdp", "tp"), None),
            P("fsdp", "tp"),
            P("fsdp", "tp"),
            P("fsdp", "tp"),
            P("tp", "fsdp"),
            P("fsdp", "tp"),
            P("tp", "fsdp"),
            P("tp"),
            P("tp"),
            P(),
            P(),
            P(),
            P("tp"),
            P(),
            P(),
            P(),
        ),
        check_vma=False,
    )
```

profile of v0, /device:TPU:0, one launch (start us, length us, event | category | flops | bytes accessed | tf_op | source)
XLA Modules:
  0.0 1212.2 jit_solution(4693354683763853291)
XLA Ops:
  12.4 24.9 %all_gather.37 = bf16[768,384]{1,0:T(8,128)(2,1)S(1)} all-gather(bf16[48,384]{1,0:T(8,128)(2,1)S(1)} %convert_element_type.114), channel_id=1, replica_groups=mesh['fsdp'=16,'tp'=2] {'fsdp'}, dimensions={0}, use_global_device_ids=true | all-gather | bytes 626688 | tf_op jit(solution)/shard_map/all_gather | solution.py:145
  37.2 19.0 %all_gather.38 = bf16[768,384]{1,0:T(8,128)(2,1)S(1)} all-gather(bf16[48,384]{1,0:T(8,128)(2,1)S(1)} %convert_element_type.116), channel_id=1, replica_groups=mesh['fsdp'=16,'tp'=2] {'fsdp'}, dimensions={0}, use_global_device_ids=true | all-gather | bytes 626688 | tf_op jit(solution)/shard_map/all_gather | solution.py:143
  56.3 21.8 %all_gather.39 = bf16[768,384]{1,0:T(8,128)(2,1)} all-gather(bf16[48,384]{1,0:T(8,128)(2,1)S(1)} %convert_element_type.118), channel_id=1, replica_groups=mesh['fsdp'=16,'tp'=2] {'fsdp'}, dimensions={0}, use_global_device_ids=true | all-gather | bytes 626688 | tf_op jit(solution)/shard_map/all_gather | solution.py:144
  78.0 20.4 %all_gather.40 = bf16[384,768]{0,1:T(8,128)(2,1)} all-gather(bf16[384,48]{0,1:T(8,128)(2,1)S(1)} %convert_element_type.120), channel_id=1, replica_groups=mesh['fsdp'=16,'tp'=2] {'fsdp'}, dimensions={1}, use_global_device_ids=true | all-gather | bytes 626688 | tf_op jit(solution)/shard_map/all_gather | solution.py:146
  98.5 4.8 add_convert_fusion.4
  111.8 5.0 convolution_convert_fusion.1
  120.6 41.6 %while.26 = (s32[]{:T(128)}, bf16[4,512,384]{2,1,0:T(8,128)(2,1)}, f32[4,6,512]{2,1,0:T(8,128)}, bf16[4,512,384]{1,2,0:T(8,128)(2,1)S(1)}, s32[4]{0:T(128)S(1)},...) while((s32[]{:T(128)}, bf16[4,512,384]{2,1,0:T(8,128)(2,1)}, ...), condition=%wide.region_3.4_spmd, body=%wide.region_0.3_spmd.sunk | while | flops 421721600 | bytes 24484972 | solution.py:159
  162.2 7.2 fusion.36
  171.3 73.9 %reduce-scatter.17.cloned.1.call-done = f32[1024,768]{1,0:T(8,128)} async-done(((f32[2048,768]{1,0:T(8,128)}), f32[1024,768]{1,0:T(8,128)}) %reduce-scatter.17.cloned.1.call-update) | async-done | bytes 3145744 | tf_op jit(solution)/shard_map/reduce_scatter | solution.py:161
  251.7 44.0 %all-gather.9.cloned.1.call-done = bf16[2048,768]{1,0:T(8,128)(2,1)} async-done(((bf16[1024,768]{1,0:T(8,128)(2,1)}), bf16[2048,768]{1,0:T(8,128)(2,1)}) %all-gather.9.cloned.1.call-update) | async-done | bytes 3145744 | tf_op jit(solution)/shard_map/all_gather | solution.py:164
  295.7 34.9 %multiply_convert_fusion.1 = (bf16[2048,1536]{1,0:T(8,128)(2,1)}, f32[2048,1536]{1,0:T(8,128)}, f32[2048,1536]{1,0:T(8,128)}) fusion(f32[1536]{0:T(1024)S(1)} %copy-done.26, bf16[2048,768]{1,0:T(8,128)(2,1)} %all-gather.9.cloned.1.call-done, bf16[768,1536]{1,0:T(8,128)(2,1)} %all-gather.11.cloned.1.call-done), kind=kOutput, calls=%fused_computation.41 | convolution fusion | flops 5039456256 | bytes 36968448 | tf_op jit(solution)/shard_map/dot_general | solution.py:26
  330.6 10.5 all-gather.13.cloned.1.call-done
  341.1 9.7 fusion.37
  351.2 75.1 %reduce-scatter.19.cloned.1.call-done = f32[1024,768]{1,0:T(8,128)} async-done(((f32[2048,768]{1,0:T(8,128)}), f32[1024,768]{1,0:T(8,128)}) %reduce-scatter.19.cloned.1.call-update) | async-done | bytes 3145744 | tf_op jit(solution)/shard_map/reduce_scatter | solution.py:168
  438.9 45.0 %all-gather.15.cloned.1.call-done = bf16[2048,768]{1,0:T(8,128)(2,1)} async-done(((bf16[1024,768]{1,0:T(8,128)(2,1)}), bf16[2048,768]{1,0:T(8,128)(2,1)}) %all-gather.15.cloned.1.call-update) | async-done | bytes 3145744 | tf_op jit(solution)/shard_map/all_gather | solution.py:181
  483.9 17.6 %convert_reduce_fusion = (f32[1536]{0:T(1024)}, bf16[2048,1536]{1,0:T(8,128)(2,1)S(1)}) fusion(f32[2048,1536]{1,0:T(8,128)} %get-tuple-element.273, bf16[2048,768]{1,0:T(8,128)(2,1)} %all-gather.15.cloned.1.call-done, bf16[1536,768]{0,1:T(8,128)(2,1)} %all-gather.13.cloned.1.call-done, f32[2048,1536]{1,0:T(8,128)} %get-tuple-element.289, ...), kind=kOutput, calls=%fused_computation.39 | convolution fusion | flops 4885314048 | bytes 36974592 | tf_op jit(solution)/shard_map/dot_general | solution.py:36
  504.2 6.9 fusion.38
  511.2 77.2 %reduce-scatter.21.cloned.1.call-done = f32[1024,768]{1,0:T(8,128)} async-done(((f32[2048,768]{1,0:T(8,128)}), f32[1024,768]{1,0:T(8,128)}) %reduce-scatter.21.cloned.1.call-update) | async-done | bytes 3145744 | tf_op jit(solution)/shard_map/reduce_scatter | solution.py:187
  597.0 44.6 %all-gather.17.cloned.1.call-done = bf16[2048,768]{1,0:T(8,128)(2,1)} async-done(((bf16[1024,768]{1,0:T(8,128)(2,1)}), bf16[2048,768]{1,0:T(8,128)(2,1)}) %all-gather.17.cloned.1.call-update) | async-done | bytes 3145744 | tf_op jit(solution)/shard_map/all_gather | solution.py:192
  646.6 85.8 %while.27 = (s32[]{:T(128)}, bf16[4,512,384]{1,2,0:T(8,128)(2,1)}, bf16[4,512,384]{2,1,0:T(8,128)(2,1)S(1)}, bf16[4,512,384]{1,2,0:T(8,128)(2,1)}, bf16[4,512,38...) while((s32[]{:T(128)}, bf16[4,512,384]{1,2,0:T(8,128)(2,1)}, ...), condition=%wide.region_17.18_spmd, body=%wide.region_15.17_spmd.sunk | while | flops 1031206400 | bytes 77159104 | solution.py:195
  734.4 5.6 fusion.39
  747.0 8.8 add_convert_fusion.1
  755.8 10.3 fusion.43
  766.2 9.7 fusion.42
  775.9 5.2 fusion.41
  806.3 42.1 %all-reduce = (f32[768]{0:T(1024)S(1)}, f32[768]{0:T(1024)S(1)}, f32[768]{0:T(1024)}, f32[768]{0:T(1024)}, f32[768]{0:T(1024)}, /*index=5*/f32[3072]{0:T(1024)S(1)}, f32[768]{0:T(1024)}, f32[768]{0:T(1024)}, f32[768]{0:T(1024)}) all-reduce(f32[768]{0:T(1024)S(1)} %dynamic_update_slice.26, ...), channel_id=1, replica_groups=mesh['fsdp'=16,'tp'=2] {'fsdp','tp'}, use_global_device_ids=true, to_apply=%region_26.27 | all-reduce | flops 9216 | bytes 73728 | tf_op jit(solution)/shard_map/psum | solution.py:240
  853.9 25.9 %reduce-scatter.29.cloned.1.call-done = f32[1536,48]{0,1:T(8,128)} async-done(((f32[1536,768]{0,1:T(8,128)}), f32[1536,48]{0,1:T(8,128)}) %reduce-scatter.29.cloned.1.call-update) | async-done | bytes 294928 | tf_op jit(solution)/shard_map/reduce_scatter | solution.py:229
  879.8 79.1 %reduce-scatter.27.cloned.1.call-done = f32[48,1536]{1,0:T(8,128)} async-done(((f32[768,1536]{1,0:T(8,128)}), f32[48,1536]{1,0:T(8,128)}) %reduce-scatter.27.cloned.1.call-update) | async-done | bytes 294928 | tf_op jit(solution)/shard_map/reduce_scatter | solution.py:228
  958.8 61.6 %reduce-scatter.25.cloned.1.call-done = f32[384,48]{0,1:T(8,128)} async-done(((f32[384,768]{0,1:T(8,128)}), f32[384,48]{0,1:T(8,128)}) %reduce-scatter.25.cloned.1.call-update) | async-done | bytes 73744 | tf_op jit(solution)/shard_map/reduce_scatter | solution.py:227
  1020.4 61.6 %reduce-scatter.31.cloned.1.call-done = f32[48,384]{1,0:T(8,128)} async-done(((f32[768,384]{1,0:T(8,128)}), f32[48,384]{1,0:T(8,128)}) %reduce-scatter.31.cloned.1.call-update) | async-done | bytes 73744
  1082.0 61.4 %reduce-scatter.35.cloned.1.call-done = f32[48,384]{1,0:T(8,128)} async-done(((f32[768,384]{1,0:T(8,128)}), f32[48,384]{1,0:T(8,128)}) %reduce-scatter.35.cloned.1.call-update) | async-done | bytes 73744
  1143.3 61.5 %reduce-scatter.33.cloned.1.call-done = f32[48,384]{1,0:T(8,128)} async-done(((f32[768,384]{1,0:T(8,128)}), f32[48,384]{1,0:T(8,128)}) %reduce-scatter.33.cloned.1.call-update) | async-done | bytes 73744
  (282 shorter events, 220.6 us)
Async XLA Ops:
  8.0 90.5 %copy-start.27 = (f32[384]{0:T(512)S(1)}, f32[384]{0:T(512)}, u32[]{:S(2)}) copy-start(f32[384]{0:T(512)} %param.32) | copy-start | bytes 4612
  8.0 90.4 %all-gather.7.cloned.1.call-start = ((), (), s32[]{:S(2)}) async-start(), calls=%async_computation.10 | async-start | bytes 4718592 | tf_op jit(solution)/shard_map/all_gather | solution.py:150
  8.8 236.4 %reduce-scatter.17.cloned.1.call-start = ((), (), s32[]{:S(2)}) async-start(), calls=%async_computation.11 | async-start | bytes 9437184 | tf_op jit(solution)/shard_map/reduce_scatter | solution.py:161
  37.2 66.1 %copy-start.7 = (bf16[768,384]{1,0:T(8,128)(2,1)}, bf16[768,384]{1,0:T(8,128)(2,1)S(1)}, u32[]{:S(2)}) copy-start(bf16[768,384]{1,0:T(8,128)(2,1)S(1)} %all_gather.37) | copy-start | bytes 1769476
  56.3 48.9 %copy-start.8 = (bf16[768,384]{1,0:T(8,128)(2,1)}, bf16[768,384]{1,0:T(8,128)(2,1)S(1)}, u32[]{:S(2)}) copy-start(bf16[768,384]{1,0:T(8,128)(2,1)S(1)} %all_gather.38) | copy-start | bytes 1769476
  162.2 7.2 copy-start.3
  162.2 7.2 copy-start.4
  169.3 75.8 %copy-start.22 = (f32[768]{0:T(1024)S(1)}, f32[768]{0:T(1024)}, u32[]{:S(2)}) copy-start(f32[768]{0:T(1024)} %param.33) | copy-start | bytes 9220
  169.4 82.3 %all-gather.11.cloned.1.call-start = ((), (), s32[]{:S(2)}) async-start(), calls=%async_computation.13 | async-start | bytes 2506752 | tf_op jit(solution)/shard_map/all_gather | solution.py:147
  171.0 124.7 %all-gather.9.cloned.1.call-start = ((), (), s32[]{:S(2)}) async-start(), calls=%async_computation.12 | async-start | bytes 4718592 | tf_op jit(solution)/shard_map/all_gather | solution.py:164
  249.1 46.6 %copy-start.26 = (f32[1536]{0:T(1024)S(1)}, f32[1536]{0:T(1024)}, u32[]{:S(2)}) copy-start(f32[1536]{0:T(1024)} %param.36) | copy-start | bytes 18436
  250.8 90.2 %all-gather.13.cloned.1.call-start = ((), (), s32[]{:S(2)}) async-start(), calls=%async_computation.14 | async-start | bytes 2506752 | tf_op jit(solution)/shard_map/all_gather | solution.py:148
  251.6 174.7 %reduce-scatter.19.cloned.1.call-start = ((), (), s32[]{:S(2)}) async-start(), calls=%async_computation.15 | async-start | bytes 9437184 | tf_op jit(solution)/shard_map/reduce_scatter | solution.py:168
  350.7 75.6 %copy-start.23 = (f32[768]{0:T(1024)S(1)}, f32[768]{0:T(1024)}, u32[]{:S(2)}) copy-start(f32[768]{0:T(1024)} %param.37) | copy-start | bytes 9220
  350.8 133.2 %all-gather.15.cloned.1.call-start = ((), (), s32[]{:S(2)}) async-start(), calls=%async_computation.16 | async-start | bytes 4718592 | tf_op jit(solution)/shard_map/all_gather | solution.py:181
  438.9 149.6 %reduce-scatter.21.cloned.1.call-start = ((), (), s32[]{:S(2)}) async-start(), calls=%async_computation.17 | async-start | bytes 9437184 | tf_op jit(solution)/shard_map/reduce_scatter | solution.py:187
  483.9 20.2 %copy-start.25 = (bf16[768,1536]{1,0:T(8,128)(2,1)S(1)}, bf16[768,1536]{1,0:T(8,128)(2,1)}, u32[]{:S(2)}) copy-start(bf16[768,1536]{1,0:T(8,128)(2,1)} %all-gather.11.cloned.1.call-done) | copy-start | bytes 7077892
  511.1 81.0 %copy-start.15 = (f32[1024]{0:T(1024)S(1)}, f32[1024]{0:T(1024)}, u32[]{:S(2)}) copy-start(f32[1024]{0:T(1024)} %copy-done.14) | copy-start | bytes 12292
  511.1 130.5 %all-gather.17.cloned.1.call-start = ((), (), s32[]{:S(2)}) async-start(), calls=%async_computation.18 | async-start | bytes 4718592 | tf_op jit(solution)/shard_map/all_gather | solution.py:192
  595.3 46.4 %copy-start.10 = (bf16[384,768]{0,1:T(8,128)(2,1)S(1)}, bf16[384,768]{0,1:T(8,128)(2,1)}, u32[]{:S(2)}) copy-start(bf16[384,768]{0,1:T(8,128)(2,1)} %all_gather.40) | copy-start | bytes 1769476
  596.7 253.6 %reduce-scatter.23.cloned.1.call-start = ((), (), s32[]{:S(2)}) async-start(), calls=%async_computation.19 | async-start | bytes 4718592 | tf_op jit(solution)/shard_map/reduce_scatter | solution.py:214
  597.0 49.6 %copy-start.30 = (s32[4]{0:T(128)S(1)}, s32[4]{0:T(128)}, u32[]{:S(2)}) copy-start(s32[4]{0:T(128)} %param.23) | copy-start | bytes 52
  755.8 124.0 %reduce-scatter.29.cloned.1.call-start = ((), (), s32[]{:S(2)}) async-start(), calls=%async_computation.22 | async-start | bytes 5013504 | tf_op jit(solution)/shard_map/reduce_scatter | solution.py:229
  766.1 192.7 %reduce-scatter.27.cloned.1.call-start = ((), (), s32[]{:S(2)}) async-start(), calls=%async_computation.21 | async-start | bytes 5013504 | tf_op jit(solution)/shard_map/reduce_scatter | solution.py:228
  775.9 244.5 %reduce-scatter.25.cloned.1.call-start = ((), (), s32[]{:S(2)}) async-start(), calls=%async_computation.20 | async-start | bytes 1253376 | tf_op jit(solution)/shard_map/reduce_scatter | solution.py:227
  781.2 300.7 %reduce-scatter.31.cloned.1.call-start = ((), (), s32[]{:S(2)}) async-start(), calls=%async_computation.23 | async-start | bytes 1253376
  788.5 354.8 %reduce-scatter.35.cloned.1.call-start = ((), (), s32[]{:S(2)}) async-start(), calls=%async_computation.25 | async-start | bytes 1253376
  795.6 409.2 %reduce-scatter.33.cloned.1.call-start = ((), (), s32[]{:S(2)}) async-start(), calls=%async_computation.24 | async-start | bytes 1253376
  800.0 6.3 copy-start.18
  800.0 6.3 copy-start.19
  800.0 6.3 copy-start.20
  800.0 50.4 %copy-start.1 = (f32[1024,768]{1,0:T(8,128)S(1)}, f32[1024,768]{1,0:T(8,128)}, u32[]{:S(2)}) copy-start(f32[1024,768]{1,0:T(8,128)} %copy-done) | copy-start | bytes 9437188
  (24 other events, 71.3 us)
Sparse Core Ops, SparseCore 0:
  10.4 47.6 all-gather.6
  169.5 75.5 reduce-scatter.16
  439.0 44.8 all-gather.14
  511.2 77.1 reduce-scatter.20
Sparse Core Ops, SparseCore 1:
  172.7 40.8 all-gather.10
  250.9 44.7 all-gather.8
  298.5 42.6 all-gather.12
  350.8 75.4 reduce-scatter.18
  596.8 44.7 all-gather.16
  755.8 43.3 reduce-scatter.22
  803.5 76.2 reduce-scatter.28
  884.1 74.7 reduce-scatter.26
  962.9 57.4 reduce-scatter.24
  1024.6 57.3 reduce-scatter.30
  1086.0 57.3 reduce-scatter.34
  1147.6 57.2 reduce-scatter.32
where the time goes:
time: 1220 us; the launch traced here: 1210 us
  waiting for transfers between devices  722 us (59%)
  matrix products  215 us (18%)
  blocking collectives  128 us (10%)
  local copies, waits for them, and re-layouts  74.5 us (6%)
  other arithmetic  54.2 us (4%)
  between operations  16.1 us (1%)
    unnamed x19, waiting for transfers between devices  185 us
    reduce_scatter x1, waiting for transfers between devices, shards(): lax.psum_scatter(weight_terms[4], 'fsdp', scatter_dimension=0, tiled=True)  79.1 us
    reduce_scatter x1, waiting for transfers between devices, shards(): lax.psum_scatter(rows_times(d_inner, wi), 'tp', scatter_dimension=0, tile...  77.2 us
    reduce_scatter x1, waiting for transfers between devices, shards(): lax.psum_scatter(matmul(hidden16, wu), 'tp', scatter_dimension=0, tiled=T...  75.1 us
    reduce_scatter x1, waiting for transfers between devices, shards(): lax.psum_scatter(matmul(context, wo), 'tp', scatter_dimension=0, tiled=True)  73.9 us
    dot_general x6, matrix products, matmul(): return jnp.dot(left, right, preferred_element_type=jnp.float32)  66.3 us
    reduce_scatter x1, waiting for transfers between devices, shards(): lax.psum_scatter(weight_terms[3], 'fsdp', scatter_dimension=1, tiled=True)  61.6 us
    dot_general x6, matrix products, matmul_nt(): lax.dot_general(left, right, (((1,), (1,)), ((), ())), preferred_element_...  48.1 us
  transfers between devices with their start and end apart: 16, of which 13 were waited for; matrix products, arithmetic and copies ran while one was open for 8% of the time, Pallas kernels for 0%

commit v1 on v0

v1 whole, which is shorter than its diff:
```python
import functools

import jax
import jax.numpy as jnp
import numpy as np
from jax import lax
from jax.experimental import pallas as pl
from jax.experimental.pallas import tpu as pltpu
from jax.sharding import PartitionSpec as P

DH = 64
SEQ = 512
PAIR = 2 * DH
norm_eps = 1e-12
masked_score = -1000000000.0
bf16 = jnp.bfloat16
f32 = jnp.float32


def dot_nn(left, right):
    return lax.dot_general(left, right, (((1,), (0,)), ((), ())), preferred_element_type=f32)


def dot_nt(left, right):
    return lax.dot_general(left, right, (((1,), (1,)), ((), ())), preferred_element_type=f32)


def dot_tn(left, right):
    return lax.dot_general(left, right, (((0,), (0,)), ((), ())), preferred_element_type=f32)


def head_slice(block, head):
    return block[:, head * DH : (head + 1) * DH]


def live_rows(lengths_ref):
    rows = lax.broadcasted_iota(jnp.int32, (SEQ, 1), 0)
    return rows < lengths_ref[pl.program_id(0)]


def attend_forward_kernel(pairs, lengths_ref, qkv_ref, context_ref, lse_ref):
    live = live_rows(lengths_ref)
    width = pairs * PAIR

    def one_pair(index, carry):
        at = pl.multiple_of(index * PAIR, PAIR)
        query = qkv_ref[:, pl.ds(at, PAIR)] * jnp.asarray(DH ** (-0.5), bf16)
        keys = qkv_ref[:, pl.ds(width + at, PAIR)]
        values = qkv_ref[:, pl.ds(2 * width + at, PAIR)]
        turned = []
        for head in range(2):
            scores = dot_nt(head_slice(keys, head), head_slice(query, head))
            scores = jnp.where(live, scores, masked_score)
            top = jnp.max(scores, axis=0, keepdims=True)
            expo = jnp.exp(scores - top)
            total = jnp.sum(expo, axis=0, keepdims=True)
            probs = (expo * (1.0 / total)).astype(bf16)
            turned.append(dot_tn(head_slice(values, head), probs))
            lse_ref[0, pl.ds(index * 2 + head, 1), :] = top + jnp.log(total)
        context_ref[:, pl.ds(at, PAIR)] = jnp.concatenate(turned, axis=0).T.astype(bf16)
        return carry

    lax.fori_loop(0, pairs, one_pair, 0)


def attend_forward(qkv, lengths):
    rows, triple = qkv.shape
    width = triple // 3
    seqs, pairs = rows // SEQ, width // PAIR
    heads = 2 * pairs
    return pl.pallas_call(
        functools.partial(attend_forward_kernel, pairs),
        grid_spec=pltpu.PrefetchScalarGridSpec(
            num_scalar_prefetch=1,
            grid=(seqs,),
            in_specs=[pl.BlockSpec((SEQ, triple), lambda s, n: (s, 0))],
            out_specs=[
                pl.BlockSpec((SEQ, width), lambda s, n: (s, 0)),
                pl.BlockSpec((1, heads, SEQ), lambda s, n: (s, 0, 0)),
            ],
        ),
        out_shape=[
            jax.ShapeDtypeStruct((rows, width), bf16),
            jax.ShapeDtypeStruct((seqs, heads, SEQ), f32),
        ],
        compiler_params=pltpu.CompilerParams(vmem_limit_bytes=20 << 20),
        cost_estimate=pl.CostEstimate(
            flops=8 * rows * SEQ * width, bytes_accessed=rows * width * 8, transcendentals=rows * SEQ * heads
        ),
        name="attend_forward",
    )(lengths, qkv)


def attend_backward_kernel(pairs, lengths_ref, qkv_ref, context_ref, d_context_ref, lse_ref, out_ref):
    live = live_rows(lengths_ref)
    width = pairs * PAIR
    scale = DH ** (-0.5)

    def one_pair(index, carry):
        at = pl.multiple_of(index * PAIR, PAIR)
        query = qkv_ref[:, pl.ds(at, PAIR)] * jnp.asarray(scale, bf16)
        keys = qkv_ref[:, pl.ds(width + at, PAIR)]
        values = qkv_ref[:, pl.ds(2 * width + at, PAIR)]
        d_context = d_context_ref[:, pl.ds(at, PAIR)]
        weighed = (context_ref[:, pl.ds(at, PAIR)].astype(f32) * d_context.astype(f32)).T
        d_query, d_key, d_value = [], [], []
        for head in range(2):
            q_h, k_h, v_h = head_slice(query, head), head_slice(keys, head), head_slice(values, head)
            g_h = head_slice(d_context, head)
            row_dot = jnp.sum(weighed[head * DH : (head + 1) * DH], axis=0, keepdims=True)
            scores = jnp.where(live, dot_nt(k_h, q_h), masked_score)
            probs = jnp.exp(scores - lse_ref[0, pl.ds(index * 2 + head, 1), :])
            d_probs = dot_nt(v_h, g_h)
            d_scores = (probs * (d_probs - row_dot)).astype(bf16)
            d_value.append(dot_nn(probs.astype(bf16), g_h))
            d_key.append(dot_nn(d_scores, q_h))
            d_query.append(dot_tn(k_h, d_scores))
        turned = jnp.concatenate(d_query, axis=0).T * scale
        out_ref[:, pl.ds(at, PAIR)] = turned.astype(bf16)
        out_ref[:, pl.ds(width + at, PAIR)] = jnp.concatenate(d_key, axis=1).astype(bf16)
        out_ref[:, pl.ds(2 * width + at, PAIR)] = jnp.concatenate(d_value, axis=1).astype(bf16)
        return carry

    lax.fori_loop(0, pairs, one_pair, 0)


def attend_backward(qkv, context, d_context, lse, lengths):
    rows, triple = qkv.shape
    width = triple // 3
    seqs, pairs = rows // SEQ, width // PAIR
    heads = 2 * pairs
    return pl.pallas_call(
        functools.partial(attend_backward_kernel, pairs),
        grid_spec=pltpu.PrefetchScalarGridSpec(
            num_scalar_prefetch=1,
            grid=(seqs,),
            in_specs=[
                pl.BlockSpec((SEQ, triple), lambda s, n: (s, 0)),
                pl.BlockSpec((SEQ, width), lambda s, n: (s, 0)),
                pl.BlockSpec((SEQ, width), lambda s, n: (s, 0)),
                pl.BlockSpec((1, heads, SEQ), lambda s, n: (s, 0, 0)),
            ],
            out_specs=pl.BlockSpec((SEQ, triple), lambda s, n: (s, 0)),
        ),
        out_shape=jax.ShapeDtypeStruct((rows, triple), bf16),
        compiler_params=pltpu.CompilerParams(vmem_limit_bytes=24 << 20),
        cost_estimate=pl.CostEstimate(
            flops=20 * rows * SEQ * width, bytes_accessed=rows * width * 16, transcendentals=rows * SEQ * heads
        ),
        name="attend_backward",
    )(lengths, qkv, context, d_context, lse)


class Exchange:
    def __init__(self, fsdp):
        self.fsdp = fsdp
        bits = [1 << i for i in range(fsdp.bit_length() - 1)]
        self.far = [bit for bit in bits if bit > 2]
        self.stages = self.far + [bit for bit in (2, 1) if bit in bits]
        self.masks = [0]
        for bit in self.stages:
            self.masks = self.masks + [mask ^ bit for mask in self.masks]

    def flip(self, array, bit):
        return lax.ppermute(array, "fsdp", [(i, i ^ bit) for i in range(self.fsdp)])

    def cross(self, array):
        return lax.ppermute(array, "tp", [(0, 1), (1, 0)])

    def gather(self, shard, cross_first):
        own = shard
        for bit in self.far:
            own = jnp.concatenate([own, self.flip(own, bit)], axis=0)
        if cross_first:
            other = self.cross(own)
            own = jnp.concatenate([own, self.flip(own, 2)], axis=0)
            other = jnp.concatenate([other, self.flip(other, 2)], axis=0)
        else:
            own = jnp.concatenate([own, self.flip(own, 2)], axis=0)
            other = self.cross(own)
        own = jnp.concatenate([own, self.flip(own, 1)], axis=0)
        other = jnp.concatenate([other, self.flip(other, 1)], axis=0)
        return own, other

    def halves(self, array):
        half = array.shape[0] // 2
        return array[:half], array[half:]

    def merge(self, keep, send, bit):
        return keep + self.flip(send.astype(bf16), bit).astype(f32)

    def scatter(self, own_keep, own_send, other_keep, other_send, cross_first):
        own = self.merge(own_keep, own_send, 1)
        other = self.merge(other_keep, other_send, 1)
        if cross_first:
            own = own + self.cross(other.astype(bf16)).astype(f32)
            own = self.merge(*self.halves(own), 2)
        else:
            own = self.merge(*self.halves(own), 2)
            other = self.merge(*self.halves(other), 2)
            own = own + self.cross(other.astype(bf16)).astype(f32)
        for bit in reversed(self.far):
            own = self.merge(*self.halves(own), bit)
        return own

    def total(self, array):
        for bit in reversed(self.stages):
            array = array + self.flip(array, bit)
        return array


ERF_P = 0.3275911
ERF_A = (0.254829592, -0.284496736, 1.421413741, -1.453152027, 1.061405429)


def gelu_parts(values):
    size = jnp.abs(values)
    t = 1.0 / (1.0 + (ERF_P * 2**-0.5) * size)
    expo = jnp.exp(-0.5 * values * values)
    poly = ERF_A[4]
    for coefficient in ERF_A[3::-1]:
        poly = poly * t + coefficient
    tail = (0.5 * poly) * (t * expo)
    phi = jnp.where(values < 0, tail, 1.0 - tail)
    return values * phi, phi + values * (expo * (2 * np.pi) ** -0.5)


def norm_parts(values):
    centred = values - jnp.mean(values, axis=-1, keepdims=True)
    scale = lax.rsqrt(jnp.mean(centred * centred, axis=-1, keepdims=True) + norm_eps)
    return centred * scale, scale


def norm_pull(grads, gain, normal, scale):
    inner = grads * gain
    return scale * (
        inner
        - jnp.mean(inner, axis=-1, keepdims=True)
        - normal * jnp.mean(inner * normal, axis=-1, keepdims=True)
    )


def shards(
    tokens,
    lengths,
    cotangent,
    w_query,
    w_key,
    w_value,
    w_output,
    w_inner,
    w_outer,
    bias_query,
    bias_value,
    bias_output,
    norm1_gain,
    norm1_bias,
    bias_inner,
    bias_outer,
    norm2_gain,
    norm2_bias,
):
    fsdp = lax.axis_size("fsdp")
    exchange = Exchange(fsdp)
    rows, model = tokens.shape
    seqs = rows // SEQ
    block = w_query.shape[0]
    width = w_query.shape[1]
    half = model // 2

    here = lax.axis_index("fsdp")
    masks = jnp.repeat(jnp.asarray(exchange.masks, jnp.int32), block)
    inside = jnp.tile(jnp.arange(block, dtype=jnp.int32), fsdp)
    source = (here ^ masks) * block + inside
    place = jnp.arange(model, dtype=jnp.int32)[:, None] == source[None, :]
    place16 = place.astype(bf16)
    place32 = place.astype(f32)

    shard_qkv = jnp.concatenate([w_query, w_key, w_value], axis=1).astype(bf16)
    qkv_own, qkv_other = exchange.gather(shard_qkv, False)
    out_own, out_other = exchange.gather(w_output.T.astype(bf16), True)
    inner_own, inner_other = exchange.gather(w_inner.astype(bf16), False)
    outer_own, outer_other = exchange.gather(w_outer.T.astype(bf16), True)

    biases_own = jnp.concatenate([bias_query, bias_value, bias_inner])
    biases_other = exchange.cross(biases_own)
    zero = jnp.zeros((width,), f32)

    def qkv_bias(biases):
        return jnp.concatenate([biases[:width], zero, biases[width : 2 * width]])

    def inner_bias(biases):
        return biases[2 * width :]

    vectors = jnp.stack([bias_output, norm1_gain, norm1_bias, bias_outer, norm2_gain, norm2_bias])
    vectors = lax.dot_general(
        vectors, place32, (((1,), (0,)), ((), ())), precision=lax.Precision.HIGHEST, preferred_element_type=f32
    )
    output_shift, gain_one, shift_one, outer_shift, gain_two, shift_two = [vectors[i] for i in range(6)]

    lengths_here = lax.dynamic_slice_in_dim(lengths, lax.axis_index("tp") * seqs, seqs, 0)

    inputs = dot_nn(tokens, place16).astype(bf16)
    cotan = dot_nn(cotangent, place16)
    proj_own = (dot_nn(inputs, qkv_own) + qkv_bias(biases_own)).astype(bf16)
    context_own, lse_own = attend_forward(proj_own, lengths_here)
    proj_other = (dot_nn(inputs, qkv_other) + qkv_bias(biases_other)).astype(bf16)
    context_other, lse_other = attend_forward(proj_other, lengths_here)
    attention = dot_nt(context_own, out_own) + dot_nt(context_other, out_other)
    normal_one, scale_one = norm_parts(attention + output_shift + inputs.astype(f32))
    normed = normal_one * gain_one + shift_one
    normed16 = normed.astype(bf16)
    hidden_own, slope_own = gelu_parts(dot_nn(normed16, inner_own) + inner_bias(biases_own))
    hidden_other, slope_other = gelu_parts(dot_nn(normed16, inner_other) + inner_bias(biases_other))
    hidden_own, hidden_other = hidden_own.astype(bf16), hidden_other.astype(bf16)
    ffn = dot_nt(hidden_own, outer_own) + dot_nt(hidden_other, outer_other)
    normal_two, scale_two = norm_parts(ffn + outer_shift + normed)
    mixed = dot_nt((normal_two * gain_two + shift_two).astype(bf16), place16).astype(bf16)

    d_before = norm_pull(cotan, gain_two, normal_two, scale_two)
    grad_gain_two = jnp.sum(cotan * normal_two, axis=0)
    grad_shift_two = jnp.sum(cotan, axis=0)
    grad_outer_bias = jnp.sum(d_before, axis=0)
    d_ffn = d_before.astype(bf16)

    def weight_grads(left, own, other):
        own_send = dot_tn(left[:, half:], own).astype(bf16)
        other_send = dot_tn(left[:, half:], other).astype(bf16)
        own_keep = dot_tn(left[:, :half], own)
        other_keep = dot_tn(left[:, :half], other)
        return own_keep, own_send, other_keep, other_send

    sum_outer = exchange.scatter(*weight_grads(d_ffn, hidden_own, hidden_other), True)
    d_inner_own = (dot_nn(d_ffn, outer_own) * slope_own).astype(bf16)
    d_inner_other = (dot_nn(d_ffn, outer_other) * slope_other).astype(bf16)
    grad_inner_bias_own = jnp.sum(d_inner_own.astype(f32), axis=0)
    grad_inner_bias_other = jnp.sum(d_inner_other.astype(f32), axis=0)
    sum_inner = exchange.scatter(*weight_grads(normed16, d_inner_own, d_inner_other), False)
    d_normed = d_before + dot_nt(d_inner_own, inner_own) + dot_nt(d_inner_other, inner_other)
    d_summed = norm_pull(d_normed, gain_one, normal_one, scale_one)
    grad_gain_one = jnp.sum(d_normed * normal_one, axis=0)
    grad_shift_one = jnp.sum(d_normed, axis=0)
    grad_output_bias = jnp.sum(d_summed, axis=0)
    d_attn = d_summed.astype(bf16)
    sum_output = exchange.scatter(*weight_grads(d_attn, context_own, context_other), True)
    d_context_own = dot_nn(d_attn, out_own).astype(bf16)
    d_context_other = dot_nn(d_attn, out_other).astype(bf16)
    d_proj_own = attend_backward(proj_own, context_own, d_context_own, lse_own, lengths_here)
    d_proj_other = attend_backward(proj_other, context_other, d_context_other, lse_other, lengths_here)
    sum_qkv = exchange.scatter(*weight_grads(inputs, d_proj_own, d_proj_other), False)
    grad_inputs = d_summed + dot_nt(d_proj_own, qkv_own) + dot_nt(d_proj_other, qkv_other)
    high = lax.reduce_precision(grad_inputs, 8, 7)
    grad_tokens = dot_nt(high.astype(bf16), place16) + dot_nt((grad_inputs - high).astype(bf16), place16)

    def sliced(d_proj, inner_part):
        summed = jnp.sum(d_proj.astype(f32), axis=0)
        return jnp.concatenate([summed[:width], summed[2 * width :], inner_part])

    whole = jnp.stack(
        [grad_output_bias, grad_gain_one, grad_shift_one, grad_outer_bias, grad_gain_two, grad_shift_two]
    )
    whole = lax.dot_general(
        whole, place32, (((1,), (1,)), ((), ())), precision=lax.Precision.HIGHEST, preferred_element_type=f32
    ).reshape(-1)
    small_own = jnp.concatenate([sliced(d_proj_own, grad_inner_bias_own), whole])
    small_other = jnp.concatenate([sliced(d_proj_other, grad_inner_bias_other), whole])
    small = exchange.total(small_own + exchange.cross(small_other))
    inner_width = bias_inner.shape[0]
    cuts = np.cumsum([width, width, inner_width] + [model] * 6)
    query_bias, value_bias, inner_bias_sum, *rest = jnp.split(small, cuts[:-1])

    return (
        mixed,
        grad_tokens,
        sum_qkv[:, :width],
        sum_qkv[:, width : 2 * width],
        sum_qkv[:, 2 * width :],
        sum_output.T,
        sum_inner,
        sum_outer.T,
        query_bias,
        value_bias,
        rest[0],
        rest[1],
        rest[2],
        inner_bias_sum,
        rest[3],
        rest[4],
        rest[5],
    )


def solution(mesh):
    both = P(("fsdp", "tp"), None)
    cols, rows = P("fsdp", "tp"), P("tp", "fsdp")
    return jax.shard_map(
        shards,
        mesh=mesh,
        in_specs=(both, P("fsdp"), both, cols, cols, cols, rows, cols, rows)
        + (P("tp"), P("tp"), P(), P(), P(), P("tp"), P(), P(), P()),
        out_specs=(both, both, cols, cols, cols, rows, cols, rows)
        + (P("tp"), P("tp"), P(), P(), P(), P("tp"), P(), P(), P()),
        check_vma=False,
    )
```

time: 1220 us -> 417 us (0.34)
  waiting for transfers between devices: 722 us -> 164 us
  blocking collectives: 128 us -> 0 us
  matrix products: 215 us -> 107 us
  local copies, waits for them, and re-layouts: 74.5 us -> 20.2 us
  starting transfers between devices: 1.48 us -> 53.9 us
  Pallas kernels: 0 us -> 39.4 us
  other arithmetic: 54.2 us -> 23.2 us
  between operations: 16.1 us -> 2.37 us
    reduce_scatter x7 -> x0, waiting for transfers between devices: 393 us -> none  [the longest x1 79.1 us: shards(): lax.psum_scatter(weight_terms[4], 'fsdp', scatter_dimension=0, tiled=True)]
    unnamed x19 -> x0, waiting for transfers between devices: 185 us -> none
    ppermute x0 -> x58, waiting for transfers between devices: none -> 164 us  [the longest x48 128 us: flip(): return lax.ppermute(array, 'fsdp', [(i, i ^ bit) for i in range(self.fsdp)])]
    all_gather x6 -> x0, waiting for transfers between devices: 144 us -> none  [the longest x1 45 us: shards(): lax.all_gather(d_before.astype(jnp.bfloat16), 'tp', axis=0, tiled=True)]
    dot_general x46 -> x39, matrix products: 215 us -> 107 us  [the longest x10 49.4 us: dot_nn(): lax.dot_general(left, right, (((1,), (0,)), ((), ())), preferred_element_...]
    all_gather x4 -> x0, blocking collectives: 86.1 us -> none  [the longest x1 24.9 us: shards(): lax.all_gather(low_weights[2], 'fsdp', axis=0, tiled=True)]
    ppermute x0 -> x58, starting transfers between devices: none -> 53.9 us  [the longest x48 43.2 us: flip(): return lax.ppermute(array, 'fsdp', [(i, i ^ bit) for i in range(self.fsdp)])]
    psum x1 -> x0, blocking collectives: 42.1 us -> none  [shards(): lax.psum((sliced_terms[0], sliced_terms[1], sliced_terms[2], grad_output_...]
  transfers between devices with their start and end apart: 16 -> 58, of which waited for: 13 -> 22; matrix products, arithmetic and copies ran while one was open for 8% -> 16% of each run, Pallas kernels for 0% -> 4%
where the time goes in v1:
time: 417 us; the launch traced here: 410 us
  waiting for transfers between devices  164 us (39%)
  matrix products  107 us (26%)
  starting transfers between devices  53.9 us (13%)
  Pallas kernels  39.4 us (9%)
  other arithmetic  23.2 us (6%)
  local copies, waits for them, and re-layouts  20.2 us (5%)
    ppermute x48, waiting for transfers between devices, flip(): return lax.ppermute(array, 'fsdp', [(i, i ^ bit) for i in range(self.fsdp)])  128 us
    dot_general x10, matrix products, dot_nn(): lax.dot_general(left, right, (((1,), (0,)), ((), ())), preferred_element_...  49.4 us
    ppermute x48, starting transfers between devices, flip(): return lax.ppermute(array, 'fsdp', [(i, i ^ bit) for i in range(self.fsdp)])  43.2 us
    ppermute x10, waiting for transfers between devices, cross(): return lax.ppermute(array, 'tp', [(0, 1), (1, 0)])  35.7 us
    dot_general x11, matrix products, dot_nt(): lax.dot_general(left, right, (((1,), (1,)), ((), ())), preferred_element_...  31.9 us
    dot_general x16, matrix products, dot_tn(): lax.dot_general(left, right, (((0,), (0,)), ((), ())), preferred_element_...  23.8 us
    pallas_call x2, Pallas kernels, attend_backward(): pl.pallas_call(functools.partial(attend_backward_kernel, pairs), grid_spe...  21.4 us
    pallas_call x2, Pallas kernels, attend_forward(): pl.pallas_call(functools.partial(attend_forward_kernel, pairs), grid_spec...  18 us
  transfers between devices with their start and end apart: 58, of which 22 were waited for; matrix products, arithmetic and copies ran while one was open for 16% of the time, Pallas kernels for 4%

profile of v1, /device:TPU:0, one launch (start us, length us, event | category | flops | bytes accessed | tf_op | source)
XLA Modules:
  0.0 409.9 jit_solution(562766497610341067)
XLA Ops:
  21.9 4.0 convolution_convert_fusion.6
  42.2 16.3 %collective-permute-done.1 = bf16[96,1152]{1,0:T(8,128)(2,1)S(1)} collective-permute-done((bf16[96,1152]{1,0:T(8,128)(2,1)S(1)}, bf16[96,1152]{1,0:T(8,128)(2,1)S(1)}, u32[]{:S(2)}, u32[]{:S(2)}) %collective-permute-start.1) | collective-permute-done | bytes 221216 | tf_op jit(solution)/shard_map/ppermute | solution.py:165
  59.2 10.1 %collective-permute-done.19 = bf16[96,1536]{1,0:T(8,128)(2,1)S(1)} collective-permute-done((bf16[96,1536]{1,0:T(8,128)(2,1)S(1)}, bf16[96,1536]{1,0:T(8,128)(2,1)S(1)}, u32[]{:S(2)}, u32[]{:S(2)}) %collective-permute-start.19) | collective-permute-done | bytes 294944 | tf_op jit(solution)/shard_map/ppermute | solution.py:165
  74.0 22.8 %collective-permute-done.16 = bf16[192,1536]{1,0:T(8,128)(2,1)S(1)} collective-permute-done((bf16[192,1536]{1,0:T(8,128)(2,1)S(1)}, bf16[192,1536]{1,0:T(8,128)(2,1)S(1)}, u32[]{:S(2)}, u32[]{:S(2)}) %collective-permute-start.16) | collective-permute-done | bytes 589856 | tf_op jit(solution)/shard_map/ppermute | solution.py:165
  98.4 14.8 %collective-permute-done.25 = bf16[192,1536]{1,0:T(8,128)(2,1)S(1)} collective-permute-done((bf16[192,1536]{1,0:T(8,128)(2,1)S(1)}, bf16[192,1536]{1,0:T(8,128)(2,1)S(1)}, u32[]{:S(2)}, u32[]{:S(2)}) %collective-permute-start.25) | collective-permute-done | bytes 589856 | tf_op jit(solution)/shard_map/ppermute | solution.py:165
  117.0 9.1 %attend_forward.2 = (bf16[1024,384]{1,0:T(8,128)(2,1)S(1)}, f32[2,6,512]{2,1,0:T(8,128)S(1)}) custom-call(s32[2]{0:T(128)S(1)} %dynamic_slice.3.lengths_ref, bf16[1024,1152]{1,0:T(8,128)(2,1)S(1)} %add_convert_fusion.1.qkv_ref), custom_call_target="tpu_custom_call" | custom-call | flops 1610612736 | bytes 3145728 | tf_op jit(solution)/shard_map/attend_forward/pallas_call | solution.py:71
  129.9 8.9 %attend_forward.3 = (bf16[1024,384]{1,0:T(8,128)(2,1)S(1)}, f32[2,6,512]{2,1,0:T(8,128)S(1)}) custom-call(s32[2]{0:T(128)S(1)} %dynamic_slice.3.lengths_ref, bf16[1024,1152]{1,0:T(8,128)(2,1)S(1)} %add_convert_fusion.qkv_ref), custom_call_target="tpu_custom_call" | custom-call | flops 1610612736 | bytes 3145728 | tf_op jit(solution)/shard_map/attend_forward/pallas_call | solution.py:71
  142.2 8.7 %multiply_convert_fusion.3 = (bf16[1024,1536]{1,0:T(8,128)(2,1)S(1)}, f32[1024,1536]{1,0:T(8,128)}) fusion(f32[1536]{0:T(1024)S(1)} %copy-done.40, bf16[1024,768]{0,1:T(8,128)(2,1)S(1)} %fusion.4, bf16[768,1536]{1,0:T(8,128)(2,1)S(1)} %constant_dynamic-update-slice_fusion.15), kind=kOutput, calls=%fused_computation.15 | convolution fusion | flops 2452094976 | bytes 13375488 | tf_op jit(solution)/shard_map/dot_general | solution.py:21
  151.1 9.0 %multiply_convert_fusion.2 = (bf16[1024,1536]{1,0:T(8,128)(2,1)S(1)}, f32[1024,1536]{1,0:T(8,128)}) fusion(f32[1536]{0:T(1024)S(1)} %slice.235, bf16[1024,768]{0,1:T(8,128)(2,1)S(1)} %fusion.4, bf16[768,1536]{1,0:T(8,128)(2,1)S(1)} %constant_dynamic-update-slice_fusion.25), kind=kOutput, calls=%fused_computation.10 | convolution fusion | flops 2452094976 | bytes 13375488 | tf_op jit(solution)/shard_map/dot_general | solution.py:21
  166.1 3.7 fusion.3
  171.9 4.1 fusion.72
  183.1 8.8 %convert_reduce_fusion = (f32[1536]{0:T(1024)S(1)}, bf16[1024,1536]{1,0:T(8,128)(2,1)S(1)}) fusion(f32[1024,1536]{1,0:T(8,128)S(1)} %bitcast.83, f32[1536]{0:T(1024)S(1)} %slice.235, bf16[1024,768]{0,1:T(8,128)(2,1)S(1)} %convert_element_type.227, bf16[768,1536]{1,0:T(8,128)(2,1)S(1)} %copy-done.33), kind=kOutput, calls=%fused_computation.6 | convolution fusion | flops 2459957760 | bytes 13381632 | tf_op jit(solution)/shard_map/dot_general | solution.py:21
  191.9 8.6 %convert_reduce_fusion.1 = (f32[1536]{0:T(1024)S(1)}, bf16[1024,1536]{1,0:T(8,128)(2,1)S(1)}) fusion(f32[1024,1536]{1,0:T(8,128)S(1)} %bitcast.81, f32[1536]{0:T(1024)S(1)} %copy-done.40, bf16[1024,768]{0,1:T(8,128)(2,1)S(1)} %convert_element_type.227, bf16[768,1536]{1,0:T(8,128)(2,1)S(1)} %copy-done.39), kind=kOutput, calls=%fused_computation.7 | convolution fusion | flops 2459957760 | bytes 13381632 | tf_op jit(solution)/shard_map/dot_general | solution.py:21
  204.3 3.7 multiply_reduce_fusion
  215.9 10.5 %attend_backward.3 = bf16[1024,1152]{1,0:T(8,128)(2,1)S(1)} custom-call(s32[2]{0:T(128)S(1)} %dynamic_slice.3.lengths_ref, bf16[1024,1152]{1,0:T(8,128)(2,1)S(1)} %copy-done.9, bf16[1024,384]{1,0:T(8,128)(2,1)S(1)} %get-tuple-element.22.context_ref, bf16[1024,384]{1,0:T(8,128)(2,1)S(1)} %convolution_convert_fusion.7.d_context_ref, ...), custom_call_target="tpu_custom_call" | custom-call | flops 4026531840 | bytes 6291456 | tf_op jit(solution)/shard_map/attend_backward/pallas_call | solution.py:132
  228.9 10.9 %attend_backward.2 = bf16[1024,1152]{1,0:T(8,128)(2,1)S(1)} custom-call(s32[2]{0:T(128)S(1)} %dynamic_slice.3.lengths_ref, bf16[1024,1152]{1,0:T(8,128)(2,1)S(1)} %copy-done.7, bf16[1024,384]{1,0:T(8,128)(2,1)S(1)} %get-tuple-element.21.context_ref, bf16[1024,384]{1,0:T(8,128)(2,1)S(1)} %convolution_convert_fusion.8.d_context_ref, ...), custom_call_target="tpu_custom_call" | custom-call | flops 4026531840 | bytes 6291456 | tf_op jit(solution)/shard_map/attend_backward/pallas_call | solution.py:132
  246.4 3.9 fusion.85
  250.3 3.1 fusion.13
  257.3 6.3 %add_add_fusion = f32[1024,768]{0,1:T(8,128)S(1)} fusion(f32[1024,768]{0,1:T(8,128)} %copy-done.14, f32[1024,768]{0,1:T(8,128)} %fusion.85, bf16[1024,1152]{1,0:T(8,128)(2,1)} %copy-done.4, bf16[768,1152]{1,0:T(8,128)(2,1)} %copy-done.31), kind=kOutput, calls=%fused_computation.31 | convolution fusion | flops 1813512192 | bytes 13565952 | tf_op jit(solution)/shard_map/dot_general | solution.py:25
  265.1 3.2 fusion.12
  274.5 4.2 %collective-permute-done.56 = f32[6912]{0:T(1024)S(1)} collective-permute-done((f32[6912]{0:T(1024)S(1)}, f32[6912]{0:T(1024)S(1)}, u32[]{:S(2)}, u32[]{:S(2)}) %collective-permute-start.56) | collective-permute-done | bytes 27680 | tf_op jit(solution)/shard_map/ppermute | solution.py:165
  278.7 3.0 collective-permute-start.57
  284.5 3.5 collective-permute-done.37
  305.4 8.3 %collective-permute-done.30 = bf16[192,1152]{1,0:T(8,128)(2,1)S(1)} collective-permute-done((bf16[192,1152]{1,0:T(8,128)(2,1)S(1)}, bf16[192,1152]{1,0:T(8,128)(2,1)S(1)}, u32[]{:S(2)}, u32[]{:S(2)}) %collective-permute-start.30) | collective-permute-done | bytes 442400 | tf_op jit(solution)/shard_map/ppermute | solution.py:165
  317.4 4.9 %collective-permute-done.28 = bf16[192,1152]{1,0:T(8,128)(2,1)S(1)} collective-permute-done((bf16[192,1152]{1,0:T(8,128)(2,1)S(1)}, bf16[192,1152]{1,0:T(8,128)(2,1)S(1)}, u32[]{:S(2)}, u32[]{:S(2)}) %collective-permute-start.28) | collective-permute-done | bytes 442400 | tf_op jit(solution)/shard_map/ppermute | solution.py:165
  322.5 26.7 %collective-permute-done.31 = bf16[192,1152]{1,0:T(8,128)(2,1)S(1)} collective-permute-done((bf16[192,1152]{1,0:T(8,128)(2,1)S(1)}, bf16[192,1152]{1,0:T(8,128)(2,1)S(1)}, u32[]{:S(2)}, u32[]{:S(2)}) %collective-permute-start.31) | collective-permute-done | bytes 442400 | tf_op jit(solution)/shard_map/ppermute | solution.py:168
  354.5 5.3 %collective-permute-done.32 = bf16[96,1152]{1,0:T(8,128)(2,1)S(1)} collective-permute-done((bf16[96,1152]{1,0:T(8,128)(2,1)S(1)}, bf16[96,1152]{1,0:T(8,128)(2,1)S(1)}, u32[]{:S(2)}, u32[]{:S(2)}) %collective-permute-start.32) | collective-permute-done | bytes 221216 | tf_op jit(solution)/shard_map/ppermute | solution.py:165
  361.2 3.6 collective-permute-done.33
  366.9 8.0 %collective-permute-done.44 = bf16[192,1536]{1,0:T(8,128)(2,1)S(1)} collective-permute-done((bf16[192,1536]{1,0:T(8,128)(2,1)S(1)}, bf16[192,1536]{1,0:T(8,128)(2,1)S(1)}, u32[]{:S(2)}, u32[]{:S(2)}) %collective-permute-start.44) | collective-permute-done | bytes 589856 | tf_op jit(solution)/shard_map/ppermute | solution.py:168
  375.1 3.4 collective-permute-start.45
  381.3 15.1 %collective-permute-done.45 = bf16[96,1536]{1,0:T(8,128)(2,1)S(1)} collective-permute-done((bf16[96,1536]{1,0:T(8,128)(2,1)S(1)}, bf16[96,1536]{1,0:T(8,128)(2,1)S(1)}, u32[]{:S(2)}, u32[]{:S(2)}) %collective-permute-start.45) | collective-permute-done | bytes 294944 | tf_op jit(solution)/shard_map/ppermute | solution.py:165
  397.3 5.5 %collective-permute-done.51 = bf16[96,1536]{1,0:T(8,128)(2,1)S(1)} collective-permute-done((bf16[96,1536]{1,0:T(8,128)(2,1)S(1)}, bf16[96,1536]{1,0:T(8,128)(2,1)S(1)}, u32[]{:S(2)}, u32[]{:S(2)}) %collective-permute-start.51) | collective-permute-done | bytes 294944 | tf_op jit(solution)/shard_map/ppermute | solution.py:165
  (388 shorter events, 145.7 us)
Async XLA Ops:
  1.5 25.1 %collective-permute-start.10 = (f32[2304]{0:T(1024)S(1)}, f32[2304]{0:T(1024)S(1)}, u32[]{:S(2)}, u32[]{:S(2)}) collective-permute-start(f32[2304]{0:T(1024)S(1)} %pad_maximum_fusion.17), channel_id=1, source_target_pairs={{0,1},{1,0},{2,3},{3,2},{4,5},{5,4},{6,7},{7,6},{8,9},{9,8},{10,11... | collective-permute-start | bytes 27656 | tf_op jit(solution)/shard_map/ppermute | solution.py:168
  5.4 21.3 %collective-permute-start.4 = (bf16[48,384]{1,0:T(8,128)(2,1)S(1)}, bf16[48,384]{1,0:T(8,128)(2,1)S(1)}, u32[]{:S(2)}, u32[]{:S(2)}) collective-permute-start(bf16[48,384]{1,0:T(8,128)(2,1)S(1)} %get-tuple-element.49), channel_id=1, source_target_pairs={{0,8},{2,10},{4,12},{6,14},{8,0},{10,2},{12,4},{14,6},{16,24},{18,... | collective-permute-start | bytes 110600 | tf_op jit(solution)/shard_map/ppermute | solution.py:165
  10.3 23.9 %collective-permute-start = (bf16[48,1152]{1,0:T(8,128)(2,1)S(1)}, bf16[48,1152]{1,0:T(8,128)(2,1)S(1)}, u32[]{:S(2)}, u32[]{:S(2)}) collective-permute-start(bf16[48,1152]{1,0:T(8,128)(2,1)S(1)} %get-tuple-element.54), channel_id=1, source_target_pairs={{0,8},{2,10},{4,12},{6,14},{8,0},{10,2},{12,4},{14,6},{16,24},{18,... | collective-permute-start | bytes 331784 | tf_op jit(solution)/shard_map/ppermute | solution.py:165
  12.4 25.2 %collective-permute-start.14 = (bf16[48,1536]{1,0:T(8,128)(2,1)S(1)}, bf16[48,1536]{1,0:T(8,128)(2,1)S(1)}, u32[]{:S(2)}, u32[]{:S(2)}) collective-permute-start(bf16[48,1536]{1,0:T(8,128)(2,1)S(1)} %get-tuple-element.47), channel_id=1, source_target_pairs={{0,8},{2,10},{4,12},{6,14},{8,0},{10,2},{12,4},{14,6},{16,24},{18,... | collective-permute-start | bytes 442376 | tf_op jit(solution)/shard_map/ppermute | solution.py:165
  15.7 22.3 %collective-permute-start.18 = (bf16[48,1536]{1,0:T(8,128)(2,1)S(1)}, bf16[48,1536]{1,0:T(8,128)(2,1)S(1)}, u32[]{:S(2)}, u32[]{:S(2)}) collective-permute-start(bf16[48,1536]{1,0:T(8,128)(2,1)S(1)} %get-tuple-element.45), channel_id=1, source_target_pairs={{0,8},{2,10},{4,12},{6,14},{8,0},{10,2},{12,4},{14,6},{16,24},{18,... | collective-permute-start | bytes 442376 | tf_op jit(solution)/shard_map/ppermute | solution.py:165
  34.2 24.3 %collective-permute-start.1 = (bf16[96,1152]{1,0:T(8,128)(2,1)S(1)}, bf16[96,1152]{1,0:T(8,128)(2,1)S(1)}, u32[]{:S(2)}, u32[]{:S(2)}) collective-permute-start(bf16[96,1152]{1,0:T(8,128)(2,1)S(1)} %pad_maximum_fusion.11), channel_id=1, source_target_pairs={{0,16},{2,18},{4,20},{6,22},{8,24},{10,26},{12,28},{14,30},{16,0},... | collective-permute-start | bytes 663560 | tf_op jit(solution)/shard_map/ppermute | solution.py:165
  37.7 33.2 %collective-permute-start.15 = (bf16[96,1536]{1,0:T(8,128)(2,1)S(1)}, bf16[96,1536]{1,0:T(8,128)(2,1)S(1)}, u32[]{:S(2)}, u32[]{:S(2)}) collective-permute-start(bf16[96,1536]{1,0:T(8,128)(2,1)S(1)} %pad_maximum_fusion.9), channel_id=1, source_target_pairs={{0,16},{2,18},{4,20},{6,22},{8,24},{10,26},{12,28},{14,30},{16,0},... | collective-permute-start | bytes 884744 | tf_op jit(solution)/shard_map/ppermute | solution.py:165
  38.0 31.3 %collective-permute-start.19 = (bf16[96,1536]{1,0:T(8,128)(2,1)S(1)}, bf16[96,1536]{1,0:T(8,128)(2,1)S(1)}, u32[]{:S(2)}, u32[]{:S(2)}) collective-permute-start(bf16[96,1536]{1,0:T(8,128)(2,1)S(1)} %pad_maximum_fusion.10), channel_id=1, source_target_pairs={{0,16},{2,18},{4,20},{6,22},{8,24},{10,26},{12,28},{14,30},{16,0},... | collective-permute-start | bytes 884744 | tf_op jit(solution)/shard_map/ppermute | solution.py:165
  41.5 30.0 %collective-permute-start.7 = (bf16[384,384]{1,0:T(8,128)(2,1)S(1)}, bf16[384,384]{1,0:T(8,128)(2,1)S(1)}, u32[]{:S(2)}, u32[]{:S(2)}) collective-permute-start(bf16[384,384]{1,0:T(8,128)(2,1)S(1)} %pad_maximum_fusion.7), channel_id=1, source_target_pairs={{0,2},{2,0},{4,6},{6,4},{8,10},{10,8},{12,14},{14,12},{16,18},{18,... | collective-permute-start | bytes 884744 | tf_op jit(solution)/shard_map/ppermute | solution.py:165
  41.6 17.4 %collective-permute-start.12 = (bf16[192,384]{1,0:T(8,128)(2,1)S(1)}, bf16[192,384]{1,0:T(8,128)(2,1)S(1)}, u32[]{:S(2)}, u32[]{:S(2)}) collective-permute-start(bf16[192,384]{1,0:T(8,128)(2,1)S(1)} %collective-permute-done.11), channel_id=1, source_target_pairs={{0,4},{2,6},{4,0},{6,2},{8,12},{10,14},{12,8},{14,10},{16,20},{18,... | collective-permute-start | bytes 442376 | tf_op jit(solution)/shard_map/ppermute | solution.py:165
  69.3 28.1 %collective-permute-start.24 = (bf16[192,1536]{1,0:T(8,128)(2,1)S(1)}, bf16[192,1536]{1,0:T(8,128)(2,1)S(1)}, u32[]{:S(2)}, u32[]{:S(2)}) collective-permute-start(bf16[192,1536]{1,0:T(8,128)(2,1)S(1)} %pad_maximum_fusion.5), channel_id=1, source_target_pairs={{0,1},{1,0},{2,3},{3,2},{4,5},{5,4},{6,7},{7,6},{8,9},{9,8},{10,11... | collective-permute-start | bytes 1769480 | tf_op jit(solution)/shard_map/ppermute | solution.py:168
  70.9 26.6 %collective-permute-start.20 = (bf16[192,1536]{1,0:T(8,128)(2,1)S(1)}, bf16[192,1536]{1,0:T(8,128)(2,1)S(1)}, u32[]{:S(2)}, u32[]{:S(2)}) collective-permute-start(bf16[192,1536]{1,0:T(8,128)(2,1)S(1)} %pad_maximum_fusion.5), channel_id=1, source_target_pairs={{0,4},{2,6},{4,0},{6,2},{8,12},{10,14},{12,8},{14,10},{16,20},{18,... | collective-permute-start | bytes 1769480 | tf_op jit(solution)/shard_map/ppermute | solution.py:165
  71.5 25.2 %collective-permute-start.16 = (bf16[192,1536]{1,0:T(8,128)(2,1)S(1)}, bf16[192,1536]{1,0:T(8,128)(2,1)S(1)}, u32[]{:S(2)}, u32[]{:S(2)}) collective-permute-start(bf16[192,1536]{1,0:T(8,128)(2,1)S(1)} %pad_maximum_fusion.4), channel_id=1, source_target_pairs={{0,4},{2,6},{4,0},{6,2},{8,12},{10,14},{12,8},{14,10},{16,20},{18,... | collective-permute-start | bytes 1769480 | tf_op jit(solution)/shard_map/ppermute | solution.py:165
  73.3 40.0 %collective-permute-start.8 = (bf16[384,1152]{1,0:T(8,128)(2,1)S(1)}, bf16[384,1152]{1,0:T(8,128)(2,1)S(1)}, u32[]{:S(2)}, u32[]{:S(2)}) collective-permute-start(bf16[384,1152]{1,0:T(8,128)(2,1)S(1)} %pad_maximum_fusion.3), channel_id=1, source_target_pairs={{0,1},{1,0},{2,3},{3,2},{4,5},{5,4},{6,7},{7,6},{8,9},{9,8},{10,11... | collective-permute-start | bytes 2654216 | tf_op jit(solution)/shard_map/ppermute | solution.py:168
  73.9 40.1 %collective-permute-start.3 = (bf16[384,1152]{1,0:T(8,128)(2,1)S(1)}, bf16[384,1152]{1,0:T(8,128)(2,1)S(1)}, u32[]{:S(2)}, u32[]{:S(2)}) collective-permute-start(bf16[384,1152]{1,0:T(8,128)(2,1)S(1)} %pad_maximum_fusion.3), channel_id=1, source_target_pairs={{0,2},{2,0},{4,6},{6,4},{8,10},{10,8},{12,14},{14,12},{16,18},{18,... | collective-permute-start | bytes 2654216 | tf_op jit(solution)/shard_map/ppermute | solution.py:165
  96.8 30.3 %collective-permute-start.22 = (bf16[384,1536]{1,0:T(8,128)(2,1)S(1)}, bf16[384,1536]{1,0:T(8,128)(2,1)S(1)}, u32[]{:S(2)}, u32[]{:S(2)}) collective-permute-start(bf16[384,1536]{1,0:T(8,128)(2,1)S(1)} %pad_maximum_fusion), channel_id=1, source_target_pairs={{0,1},{1,0},{2,3},{3,2},{4,5},{5,4},{6,7},{7,6},{8,9},{9,8},{10,11... | collective-permute-start | bytes 3538952 | tf_op jit(solution)/shard_map/ppermute | solution.py:168
  97.4 29.8 %collective-permute-start.17 = (bf16[384,1536]{1,0:T(8,128)(2,1)S(1)}, bf16[384,1536]{1,0:T(8,128)(2,1)S(1)}, u32[]{:S(2)}, u32[]{:S(2)}) collective-permute-start(bf16[384,1536]{1,0:T(8,128)(2,1)S(1)} %pad_maximum_fusion), channel_id=1, source_target_pairs={{0,2},{2,0},{4,6},{6,4},{8,10},{10,8},{12,14},{14,12},{16,18},{18,... | collective-permute-start | bytes 3538952 | tf_op jit(solution)/shard_map/ppermute | solution.py:165
  97.4 15.7 %collective-permute-start.25 = (bf16[192,1536]{1,0:T(8,128)(2,1)S(1)}, bf16[192,1536]{1,0:T(8,128)(2,1)S(1)}, u32[]{:S(2)}, u32[]{:S(2)}) collective-permute-start(bf16[192,1536]{1,0:T(8,128)(2,1)S(1)} %collective-permute-done.24), channel_id=1, source_target_pairs={{0,4},{2,6},{4,0},{6,2},{8,12},{10,14},{12,8},{14,10},{16,20},{18,... | collective-permute-start | bytes 1769480 | tf_op jit(solution)/shard_map/ppermute | solution.py:165
  113.3 37.5 %collective-permute-start.26 = (bf16[384,1536]{1,0:T(8,128)(2,1)S(1)}, bf16[384,1536]{1,0:T(8,128)(2,1)S(1)}, u32[]{:S(2)}, u32[]{:S(2)}) collective-permute-start(bf16[384,1536]{1,0:T(8,128)(2,1)S(1)} %pad_maximum_fusion.2), channel_id=1, source_target_pairs={{0,2},{2,0},{4,6},{6,4},{8,10},{10,8},{12,14},{14,12},{16,18},{18,... | collective-permute-start | bytes 3538952 | tf_op jit(solution)/shard_map/ppermute | solution.py:165
  127.1 23.8 %collective-permute-start.23 = (bf16[384,1536]{1,0:T(8,128)(2,1)S(1)}, bf16[384,1536]{1,0:T(8,128)(2,1)S(1)}, u32[]{:S(2)}, u32[]{:S(2)}) collective-permute-start(bf16[384,1536]{1,0:T(8,128)(2,1)S(1)} %collective-permute-done.22), channel_id=1, source_target_pairs={{0,2},{2,0},{4,6},{6,4},{8,10},{10,8},{12,14},{14,12},{16,18},{18,... | collective-permute-start | bytes 3538952 | tf_op jit(solution)/shard_map/ppermute | solution.py:165
  254.6 110.2 %collective-permute-start.47 = (bf16[384,1536]{1,0:T(8,128)(2,1)}, bf16[384,1536]{1,0:T(8,128)(2,1)S(1)}, u32[]{:S(2)}, u32[]{:S(2)}) collective-permute-start(bf16[384,1536]{1,0:T(8,128)(2,1)} %convolution_convert_fusion.3), channel_id=1, source_target_pairs={{0,2},{2,0},{4,6},{6,4},{8,10},{10,8},{12,14},{14,12},{16,18},{18,... | collective-permute-start | bytes 3538952 | tf_op jit(solution)/shard_map/ppermute | solution.py:165
  255.1 47.0 %collective-permute-start.48 = (bf16[384,1536]{1,0:T(8,128)(2,1)}, bf16[384,1536]{1,0:T(8,128)(2,1)S(1)}, u32[]{:S(2)}, u32[]{:S(2)}) collective-permute-start(bf16[384,1536]{1,0:T(8,128)(2,1)} %convolution_convert_fusion.2), channel_id=1, source_target_pairs={{0,2},{2,0},{4,6},{6,4},{8,10},{10,8},{12,14},{14,12},{16,18},{18,... | collective-permute-start | bytes 3538952 | tf_op jit(solution)/shard_map/ppermute | solution.py:165
  256.8 21.9 %collective-permute-start.34 = (bf16[384,384]{1,0:T(8,128)(2,1)}, bf16[384,384]{1,0:T(8,128)(2,1)S(1)}, u32[]{:S(2)}, u32[]{:S(2)}) collective-permute-start(bf16[384,384]{1,0:T(8,128)(2,1)} %convolution_convert_fusion.10), channel_id=1, source_target_pairs={{0,2},{2,0},{4,6},{6,4},{8,10},{10,8},{12,14},{14,12},{16,18},{18,... | collective-permute-start | bytes 884744 | tf_op jit(solution)/shard_map/ppermute | solution.py:165
  278.7 20.1 %collective-permute-start.29 = (bf16[384,1152]{1,0:T(8,128)(2,1)S(1)}, bf16[384,1152]{1,0:T(8,128)(2,1)S(1)}, u32[]{:S(2)}, u32[]{:S(2)}) collective-permute-start(bf16[384,1152]{1,0:T(8,128)(2,1)S(1)} %copy-done.48), channel_id=1, source_target_pairs={{0,2},{2,0},{4,6},{6,4},{8,10},{10,8},{12,14},{14,12},{16,18},{18,... | collective-permute-start | bytes 2654216 | tf_op jit(solution)/shard_map/ppermute | solution.py:165
  284.4 16.2 %collective-permute-start.27 = (bf16[384,1152]{1,0:T(8,128)(2,1)S(1)}, bf16[384,1152]{1,0:T(8,128)(2,1)S(1)}, u32[]{:S(2)}, u32[]{:S(2)}) collective-permute-start(bf16[384,1152]{1,0:T(8,128)(2,1)S(1)} %copy-done.47), channel_id=1, source_target_pairs={{0,2},{2,0},{4,6},{6,4},{8,10},{10,8},{12,14},{14,12},{16,18},{18,... | collective-permute-start | bytes 2654216 | tf_op jit(solution)/shard_map/ppermute | solution.py:165
  298.2 53.9 %collective-permute-start.40 = (bf16[384,1536]{1,0:T(8,128)(2,1)S(1)}, bf16[384,1536]{1,0:T(8,128)(2,1)S(1)}, u32[]{:S(2)}, u32[]{:S(2)}) collective-permute-start(bf16[384,1536]{1,0:T(8,128)(2,1)S(1)} %convolution_convert_fusion.5), channel_id=1, source_target_pairs={{0,2},{2,0},{4,6},{6,4},{8,10},{10,8},{12,14},{14,12},{16,18},{18,... | collective-permute-start | bytes 3538952 | tf_op jit(solution)/shard_map/ppermute | solution.py:165
  302.2 20.1 %collective-permute-start.28 = (bf16[192,1152]{1,0:T(8,128)(2,1)S(1)}, bf16[192,1152]{1,0:T(8,128)(2,1)S(1)}, u32[]{:S(2)}, u32[]{:S(2)}) collective-permute-start(bf16[192,1152]{1,0:T(8,128)(2,1)S(1)} %slice.374), channel_id=1, source_target_pairs={{0,4},{2,6},{4,0},{6,2},{8,12},{10,14},{12,8},{14,10},{16,20},{18,... | collective-permute-start | bytes 1327112 | tf_op jit(solution)/shard_map/ppermute | solution.py:165
  313.7 51.1 %collective-permute-start.49 = (bf16[384,1536]{1,0:T(8,128)(2,1)S(1)}, bf16[384,1536]{1,0:T(8,128)(2,1)S(1)}, u32[]{:S(2)}, u32[]{:S(2)}) collective-permute-start(bf16[384,1536]{1,0:T(8,128)(2,1)S(1)} %add_convert_fusion.3), channel_id=1, source_target_pairs={{0,1},{1,0},{2,3},{3,2},{4,5},{5,4},{6,7},{7,6},{8,9},{9,8},{10,11... | collective-permute-start | bytes 3538952 | tf_op jit(solution)/shard_map/ppermute | solution.py:168
  314.5 34.8 %collective-permute-start.31 = (bf16[192,1152]{1,0:T(8,128)(2,1)S(1)}, bf16[192,1152]{1,0:T(8,128)(2,1)S(1)}, u32[]{:S(2)}, u32[]{:S(2)}) collective-permute-start(bf16[192,1152]{1,0:T(8,128)(2,1)S(1)} %fusion.31), channel_id=1, source_target_pairs={{0,1},{1,0},{2,3},{3,2},{4,5},{5,4},{6,7},{7,6},{8,9},{9,8},{10,11... | collective-permute-start | bytes 1327112 | tf_op jit(solution)/shard_map/ppermute | solution.py:168
  322.2 38.4 %collective-permute-start.43 = (bf16[192,1536]{1,0:T(8,128)(2,1)S(1)}, bf16[192,1536]{1,0:T(8,128)(2,1)S(1)}, u32[]{:S(2)}, u32[]{:S(2)}) collective-permute-start(bf16[192,1536]{1,0:T(8,128)(2,1)S(1)} %slice.371), channel_id=1, source_target_pairs={{0,4},{2,6},{4,0},{6,2},{8,12},{10,14},{12,8},{14,10},{16,20},{18,... | collective-permute-start | bytes 1769480 | tf_op jit(solution)/shard_map/ppermute | solution.py:165
  375.1 21.3 %collective-permute-start.45 = (bf16[96,1536]{1,0:T(8,128)(2,1)S(1)}, bf16[96,1536]{1,0:T(8,128)(2,1)S(1)}, u32[]{:S(2)}, u32[]{:S(2)}) collective-permute-start(bf16[96,1536]{1,0:T(8,128)(2,1)S(1)} %slice.376), channel_id=1, source_target_pairs={{0,16},{2,18},{4,20},{6,22},{8,24},{10,26},{12,28},{14,30},{16,0},... | collective-permute-start | bytes 884744 | tf_op jit(solution)/shard_map/ppermute | solution.py:165
  378.8 23.9 %collective-permute-start.51 = (bf16[96,1536]{1,0:T(8,128)(2,1)S(1)}, bf16[96,1536]{1,0:T(8,128)(2,1)S(1)}, u32[]{:S(2)}, u32[]{:S(2)}) collective-permute-start(bf16[96,1536]{1,0:T(8,128)(2,1)S(1)} %slice.375), channel_id=1, source_target_pairs={{0,16},{2,18},{4,20},{6,22},{8,24},{10,26},{12,28},{14,30},{16,0},... | collective-permute-start | bytes 884744 | tf_op jit(solution)/shard_map/ppermute | solution.py:165
  (90 other events, 970.5 us)

commit v2 on v1

v2 whole, which is shorter than its diff:
```python
import functools

import jax
import jax.numpy as jnp
import numpy as np
from jax import lax
from jax.experimental import pallas as pl
from jax.experimental.pallas import tpu as pltpu
from jax.sharding import PartitionSpec as P

DH = 64
SEQ = 512
PAIR = 2 * DH
norm_eps = 1e-12
masked_score = -1000000000.0
bf16 = jnp.bfloat16
f32 = jnp.float32
TILE = 256
COST = dict.fromkeys(
    (
        "attend_forward",
        "attend_backward",
        "attention_out",
        "hidden",
        "turn",
        "d_hidden",
        "d_attention",
        "d_inputs",
        "send_grads",
        "keep_grads",
    ),
    0.02,
)


def cost(micros):
    return pl.CostEstimate(flops=int(micros * 9e8), bytes_accessed=1024, transcendentals=0)


def dot_nn(left, right):
    return lax.dot_general(left, right, (((1,), (0,)), ((), ())), preferred_element_type=f32)


def dot_nt(left, right):
    return lax.dot_general(left, right, (((1,), (1,)), ((), ())), preferred_element_type=f32)


def dot_tn(left, right):
    return lax.dot_general(left, right, (((0,), (0,)), ((), ())), preferred_element_type=f32)


ERF_P = 0.3275911
ERF_A = (0.254829592, -0.284496736, 1.421413741, -1.453152027, 1.061405429)


def gelu_parts(values):
    size = jnp.abs(values)
    t = 1.0 / (1.0 + (ERF_P * 2**-0.5) * size)
    expo = jnp.exp(-0.5 * values * values)
    poly = ERF_A[4]
    for coefficient in ERF_A[3::-1]:
        poly = poly * t + coefficient
    tail = (0.5 * poly) * (t * expo)
    phi = jnp.where(values < 0, tail, 1.0 - tail)
    return values * phi, phi + values * (expo * (2 * np.pi) ** -0.5)


def norm_parts(values):
    centred = values - jnp.mean(values, axis=-1, keepdims=True)
    scale = lax.rsqrt(jnp.mean(centred * centred, axis=-1, keepdims=True) + norm_eps)
    return centred * scale, scale


def norm_pull(grads, gain, normal, scale):
    inner = grads * gain
    return scale * (
        inner
        - jnp.mean(inner, axis=-1, keepdims=True)
        - normal * jnp.mean(inner * normal, axis=-1, keepdims=True)
    )


def head_slice(block, head):
    return block[:, head * DH : (head + 1) * DH]


def live_rows(lengths_ref):
    rows = lax.broadcasted_iota(jnp.int32, (SEQ, 1), 0)
    return rows < lengths_ref[pl.program_id(0)]


def attend_forward_kernel(
    pairs, lengths_ref, inputs_ref, first_ref, second_ref, shift_ref, qkv_ref, context_ref, lse_ref
):
    live = live_rows(lengths_ref)
    width = pairs * PAIR
    half = first_ref.shape[0]
    qkv_ref[...] = (
        dot_nn(inputs_ref[:, :half], first_ref[...])
        + dot_nn(inputs_ref[:, half:], second_ref[...])
        + shift_ref[...]
    ).astype(bf16)

    def one_pair(index, carry):
        at = pl.multiple_of(index * PAIR, PAIR)
        query = qkv_ref[:, pl.ds(at, PAIR)] * jnp.asarray(DH ** (-0.5), bf16)
        keys = qkv_ref[:, pl.ds(width + at, PAIR)]
        values = qkv_ref[:, pl.ds(2 * width + at, PAIR)]
        turned = []
        for head in range(2):
            scores = dot_nt(head_slice(keys, head), head_slice(query, head))
            scores = jnp.where(live, scores, masked_score)
            top = jnp.max(scores, axis=0, keepdims=True)
            expo = jnp.exp(scores - top)
            total = jnp.sum(expo, axis=0, keepdims=True)
            probs = (expo * (1.0 / total)).astype(bf16)
            turned.append(dot_tn(head_slice(values, head), probs))
            lse_ref[0, pl.ds(index * 2 + head, 1), :] = top + jnp.log(total)
        context_ref[:, pl.ds(at, PAIR)] = jnp.concatenate(turned, axis=0).T.astype(bf16)
        return carry

    lax.fori_loop(0, pairs, one_pair, 0)


def attend_forward(inputs, weight, shift, lengths):
    rows, model = inputs.shape
    half, triple = weight[0].shape
    width = triple // 3
    seqs, pairs = rows // SEQ, width // PAIR
    heads = 2 * pairs
    return pl.pallas_call(
        functools.partial(attend_forward_kernel, pairs),
        grid_spec=pltpu.PrefetchScalarGridSpec(
            num_scalar_prefetch=1,
            grid=(seqs,),
            in_specs=[
                pl.BlockSpec((SEQ, model), lambda s, n: (s, 0)),
                pl.BlockSpec((half, triple), lambda s, n: (0, 0), pipeline_mode=pl.Buffered(1)),
                pl.BlockSpec((half, triple), lambda s, n: (0, 0), pipeline_mode=pl.Buffered(1)),
                pl.BlockSpec((1, triple), lambda s, n: (0, 0)),
            ],
            out_specs=[
                pl.BlockSpec((SEQ, triple), lambda s, n: (s, 0)),
                pl.BlockSpec((SEQ, width), lambda s, n: (s, 0)),
                pl.BlockSpec((1, heads, SEQ), lambda s, n: (s, 0, 0)),
            ],
        ),
        out_shape=[
            jax.ShapeDtypeStruct((rows, triple), bf16),
            jax.ShapeDtypeStruct((rows, width), bf16),
            jax.ShapeDtypeStruct((seqs, heads, SEQ), f32),
        ],
        compiler_params=pltpu.CompilerParams(vmem_limit_bytes=24 << 20),
        cost_estimate=cost(COST["attend_forward"]),
        name="attend_forward",
    )(lengths, inputs, *weight, shift[None, :])


def attend_backward_kernel(pairs, lengths_ref, qkv_ref, context_ref, d_context_ref, lse_ref, out_ref, sums_ref):
    live = live_rows(lengths_ref)

    @pl.when(pl.program_id(0) == 0)
    def _():
        sums_ref[...] = jnp.zeros_like(sums_ref)

    width = pairs * PAIR
    scale = DH ** (-0.5)

    def one_pair(index, carry):
        at = pl.multiple_of(index * PAIR, PAIR)
        query = qkv_ref[:, pl.ds(at, PAIR)] * jnp.asarray(scale, bf16)
        keys = qkv_ref[:, pl.ds(width + at, PAIR)]
        values = qkv_ref[:, pl.ds(2 * width + at, PAIR)]
        d_context = d_context_ref[:, pl.ds(at, PAIR)]
        weighed = (context_ref[:, pl.ds(at, PAIR)].astype(f32) * d_context.astype(f32)).T
        d_query, d_key, d_value = [], [], []
        for head in range(2):
            q_h, k_h, v_h = head_slice(query, head), head_slice(keys, head), head_slice(values, head)
            g_h = head_slice(d_context, head)
            row_dot = jnp.sum(weighed[head * DH : (head + 1) * DH], axis=0, keepdims=True)
            scores = jnp.where(live, dot_nt(k_h, q_h), masked_score)
            probs = jnp.exp(scores - lse_ref[0, pl.ds(index * 2 + head, 1), :])
            d_probs = dot_nt(v_h, g_h)
            d_scores = (probs * (d_probs - row_dot)).astype(bf16)
            d_value.append(dot_nn(probs.astype(bf16), g_h))
            d_key.append(dot_nn(d_scores, q_h))
            d_query.append(dot_tn(k_h, d_scores))
        turned = (jnp.concatenate(d_query, axis=0).T * scale).astype(bf16)
        d_value = jnp.concatenate(d_value, axis=1).astype(bf16)
        out_ref[:, pl.ds(at, PAIR)] = turned
        out_ref[:, pl.ds(width + at, PAIR)] = jnp.concatenate(d_key, axis=1).astype(bf16)
        out_ref[:, pl.ds(2 * width + at, PAIR)] = d_value
        sums_ref[0:1, pl.ds(at, PAIR)] += jnp.sum(turned.astype(f32), axis=0, keepdims=True)
        sums_ref[1:2, pl.ds(at, PAIR)] += jnp.sum(d_value.astype(f32), axis=0, keepdims=True)
        return carry

    lax.fori_loop(0, pairs, one_pair, 0)


def attend_backward(qkv, context, d_context, lse, lengths):
    rows, triple = qkv.shape
    width = triple // 3
    seqs, pairs = rows // SEQ, width // PAIR
    heads = 2 * pairs
    return pl.pallas_call(
        functools.partial(attend_backward_kernel, pairs),
        grid_spec=pltpu.PrefetchScalarGridSpec(
            num_scalar_prefetch=1,
            grid=(seqs,),
            in_specs=[
                pl.BlockSpec((SEQ, triple), lambda s, n: (s, 0)),
                pl.BlockSpec((SEQ, width), lambda s, n: (s, 0)),
                pl.BlockSpec((SEQ, width), lambda s, n: (s, 0)),
                pl.BlockSpec((1, heads, SEQ), lambda s, n: (s, 0, 0)),
            ],
            out_specs=[
                pl.BlockSpec((SEQ, triple), lambda s, n: (s, 0)),
                pl.BlockSpec((8, width), lambda s, n: (0, 0)),
            ],
        ),
        out_shape=[jax.ShapeDtypeStruct((rows, triple), bf16), jax.ShapeDtypeStruct((8, width), f32)],
        compiler_params=pltpu.CompilerParams(vmem_limit_bytes=24 << 20),
        cost_estimate=cost(COST["attend_backward"]),
        name="attend_backward",
    )(lengths, qkv, context, d_context, lse)


def in_vmem(kernel, name, limit, outs, *args):
    return pl.pallas_call(
        kernel,
        in_specs=[pl.BlockSpec(memory_space=pltpu.VMEM)] * len(args),
        out_specs=[pl.BlockSpec(memory_space=pltpu.VMEM)] * len(outs),
        out_shape=[jax.ShapeDtypeStruct(*out) for out in outs],
        compiler_params=pltpu.CompilerParams(vmem_limit_bytes=limit << 20),
        cost_estimate=cost(COST[name]),
        name=name,
    )(*args)


def tiles_of(ref, body):
    def one(index, carry):
        body(pl.ds(pl.multiple_of(index * TILE, TILE), TILE))
        return carry

    lax.fori_loop(0, ref.shape[0] // TILE, one, 0)


def add_sums(ref, row, values):
    ref[row : row + 1, :] += jnp.sum(values, axis=0, keepdims=True)


def nn_rows(left, pieces):
    total, start = None, 0
    for piece in pieces:
        part = dot_nn(left[:, start : start + piece.shape[0]], piece[...])
        total = part if total is None else total + part
        start += piece.shape[0]
    return total


def nt_rows(lefts, pieces):
    parts = []
    for index in range(len(pieces[0])):
        parts.append(sum(dot_nt(left, piece[index][...]) for left, piece in zip(lefts, pieces)))
    return jnp.concatenate(parts, axis=1)


def attention_out_kernel(
    own_ref, other_ref, own_a, own_b, other_a, other_b, inputs_ref, vectors_ref, normal_ref, scale_ref, normed_ref
):
    def body(at):
        mixed = nt_rows((own_ref[at], other_ref[at]), ((own_a, own_b), (other_a, other_b)))
        normal, scale = norm_parts(mixed + vectors_ref[0:1] + inputs_ref[at].astype(f32))
        normal_ref[at] = normal
        scale_ref[at] = scale
        normed_ref[at] = (normal * vectors_ref[1:2] + vectors_ref[2:3]).astype(bf16)

    tiles_of(own_ref, body)


def attention_out(own, other, w_own, w_other, inputs, vectors):
    shape = inputs.shape
    outs = [(shape, f32), ((shape[0], 1), f32), (shape, bf16)]
    return in_vmem(attention_out_kernel, "attention_out", 16, outs, own, other, *w_own, *w_other, inputs, vectors)


def hidden_kernel(normed_ref, w_a, w_b, shift_ref, hidden_ref, slope_ref):
    def body(at):
        hidden, slope = gelu_parts(nn_rows(normed_ref[at], (w_a, w_b)) + shift_ref[...])
        hidden_ref[at] = hidden.astype(bf16)
        slope_ref[at] = slope.astype(bf16)

    tiles_of(normed_ref, body)


def hidden_parts(normed, w, shift):
    shape = (normed.shape[0], w[0].shape[1])
    return in_vmem(hidden_kernel, "hidden", 24, [(shape, bf16), (shape, bf16)], normed, *w, shift[None, :])


def turn_kernel(
    own_ref,
    other_ref,
    own_a,
    own_b,
    other_a,
    other_b,
    normal_one_ref,
    cotan_ref,
    vectors_ref,
    place_ref,
    mixed_ref,
    d_before_ref,
    d_ffn_ref,
    sums_ref,
):
    sums_ref[...] = jnp.zeros_like(sums_ref)

    def body(at):
        ffn = nt_rows((own_ref[at], other_ref[at]), ((own_a, own_b), (other_a, other_b)))
        normed = normal_one_ref[at] * vectors_ref[1:2] + vectors_ref[2:3]
        normal, scale = norm_parts(ffn + vectors_ref[3:4] + normed)
        result = (normal * vectors_ref[4:5] + vectors_ref[5:6]).astype(bf16)
        mixed_ref[at] = dot_nt(result, place_ref[...]).astype(bf16)
        cotan = cotan_ref[at].astype(f32)
        d_before = norm_pull(cotan, vectors_ref[4:5], normal, scale)
        d_before_ref[at] = d_before
        d_ffn_ref[at] = d_before.astype(bf16)
        add_sums(sums_ref, 0, d_before)
        add_sums(sums_ref, 1, cotan * normal)
        add_sums(sums_ref, 2, cotan)

    tiles_of(own_ref, body)


def turn(own, other, w_own, w_other, normal_one, cotan, vectors, place):
    shape = normal_one.shape
    outs = [(shape, bf16), (shape, f32), (shape, bf16), ((8, shape[1]), f32)]
    args = (own, other, *w_own, *w_other, normal_one, cotan, vectors, place)
    return in_vmem(turn_kernel, "turn", 20, outs, *args)


def d_hidden_kernel(d_ffn_ref, w_a, w_b, slope_ref, d_inner_ref, sums_ref):
    sums_ref[...] = jnp.zeros_like(sums_ref)

    def body(at):
        d_inner = (nn_rows(d_ffn_ref[at], (w_a, w_b)) * slope_ref[at].astype(f32)).astype(bf16)
        d_inner_ref[at] = d_inner
        add_sums(sums_ref, 0, d_inner.astype(f32))

    tiles_of(d_ffn_ref, body)


def d_hidden(d_ffn, w, slope):
    outs = [(slope.shape, bf16), ((8, slope.shape[1]), f32)]
    return in_vmem(d_hidden_kernel, "d_hidden", 20, outs, d_ffn, *w, slope)


def d_attention_kernel(
    own_ref,
    other_ref,
    own_a,
    own_b,
    other_a,
    other_b,
    d_before_ref,
    normal_ref,
    scale_ref,
    vectors_ref,
    out_own_a,
    out_own_b,
    out_other_a,
    out_other_b,
    d_summed_ref,
    d_attn_ref,
    d_own_ref,
    d_other_ref,
    sums_ref,
):
    sums_ref[...] = jnp.zeros_like(sums_ref)

    def body(at):
        d_normed = d_before_ref[at] + nt_rows(
            (own_ref[at], other_ref[at]), ((own_a, own_b), (other_a, other_b))
        )
        normal = normal_ref[at]
        d_summed = norm_pull(d_normed, vectors_ref[1:2], normal, scale_ref[at])
        d_summed_ref[at] = d_summed
        d_attn = d_summed.astype(bf16)
        d_attn_ref[at] = d_attn
        d_own_ref[at] = nn_rows(d_attn, (out_own_a, out_own_b)).astype(bf16)
        d_other_ref[at] = nn_rows(d_attn, (out_other_a, out_other_b)).astype(bf16)
        add_sums(sums_ref, 0, d_summed)
        add_sums(sums_ref, 1, d_normed * normal)
        add_sums(sums_ref, 2, d_normed)

    tiles_of(own_ref, body)


def d_attention(own, other, w_own, w_other, d_before, normal, scale, vectors, out_own, out_other):
    shape = d_before.shape
    part = (shape[0], out_own[0].shape[1])
    outs = [(shape, f32), (shape, bf16), (part, bf16), (part, bf16), ((8, shape[1]), f32)]
    args = (own, other, *w_own, *w_other, d_before, normal, scale, vectors, *out_own, *out_other)
    return in_vmem(d_attention_kernel, "d_attention", 20, outs, *args)


def d_inputs_kernel(d_summed_ref, own_ref, other_ref, own_a, own_b, other_a, other_b, place_ref, out_ref):
    def body(at):
        grads = d_summed_ref[at] + nt_rows((own_ref[at], other_ref[at]), ((own_a, own_b), (other_a, other_b)))
        high = grads.astype(bf16)
        low = (grads - high.astype(f32)).astype(bf16)
        out_ref[at] = dot_nt(high, place_ref[...]) + dot_nt(low, place_ref[...])

    tiles_of(d_summed_ref, body)


def d_inputs(d_summed, own, other, w_own, w_other, place):
    outs = [(d_summed.shape, f32)]
    args = (d_summed, own, other, *w_own, *w_other, place)
    return in_vmem(d_inputs_kernel, "d_inputs", 16, outs, *args)[0]


def column_chunks(width):
    step = next(step for step in (512, 384, 256, 128) if width % step == 0)
    return [(start, step) for start in range(0, width, step)]


def send_kernel(count, left_ref, *refs):
    half = left_ref.shape[1] // 2
    left = left_ref[:, half:]
    for right_ref, out_ref in zip(refs[:count], refs[count:]):
        for start, step in column_chunks(right_ref.shape[1]):
            out_ref[:, start : start + step] = dot_tn(left, right_ref[:, start : start + step]).astype(bf16)


def send_grads(left, *rights):
    outs = [((left.shape[1] // 2, right.shape[1]), bf16) for right in rights]
    return in_vmem(functools.partial(send_kernel, len(rights)), "send_grads", 16, outs, left, *rights)


def keep_kernel(count, left_ref, *refs):
    half = left_ref.shape[1] // 2
    left = left_ref[:, :half]
    rights, others, outs = refs[:count], refs[count : 2 * count], refs[2 * count :]
    for index, (right_ref, other_ref) in enumerate(zip(rights, others)):
        upper_ref, lower_ref = outs[2 * index : 2 * index + 2]
        for start, step in column_chunks(right_ref.shape[1]):
            at = slice(start, start + step)
            total = dot_tn(left, right_ref[:, at]) + other_ref[:, at].astype(f32)
            upper_ref[:, at] = total[: half // 2].astype(upper_ref.dtype)
            lower_ref[:, at] = total[half // 2 :].astype(bf16)


def keep_grads(left, rights, others, kinds):
    quarter = left.shape[1] // 4
    outs = []
    for right, kind in zip(rights, kinds):
        outs += [((quarter, right.shape[1]), kind), ((quarter, right.shape[1]), bf16)]
    return in_vmem(functools.partial(keep_kernel, len(rights)), "keep_grads", 16, outs, left, *rights, *others)


class Exchange:
    def __init__(self, fsdp):
        self.fsdp = fsdp
        bits = [1 << i for i in range(2, fsdp.bit_length() - 1)]
        self.far = []
        for i in range(0, len(bits), 2):
            steps = [0]
            for bit in bits[i : i + 2]:
                steps = steps + [step ^ bit for step in steps]
            self.far.append(steps)
        self.masks = [0]
        for steps in self.far + [[0, 2], [0, 1]]:
            self.masks = [step ^ mask for step in steps for mask in self.masks]

    def flip(self, array, bit):
        return lax.ppermute(array, "fsdp", [(i, i ^ bit) for i in range(self.fsdp)])

    def cross(self, array):
        return lax.ppermute(array, "tp", [(0, 1), (1, 0)])

    def flip_cross(self, array, bit):
        pairs = [(2 * i + j, 2 * (i ^ bit) + 1 - j) for i in range(self.fsdp) for j in range(2)]
        return lax.ppermute(array, ("fsdp", "tp"), pairs)

    def gather_far(self, array):
        for steps in self.far[:-1]:
            array = join([array] + [self.flip(array, step) for step in steps[1:]])
        return [array] + [self.flip(array, step) for step in self.far[-1][1:]]

    def scatter_far(self, array):
        for steps in reversed(self.far):
            size = array.shape[0] // len(steps)
            parts = [array[i * size : (i + 1) * size] for i in range(len(steps))]
            array = parts[0]
            for part, step in zip(parts[1:], steps[1:]):
                array = array + self.flip(part.astype(bf16), step).astype(f32)
        return array

    def total_far(self, array):
        for steps in reversed(self.far):
            parts = [array] + [self.flip(array, step) for step in steps[1:]]
            while len(parts) > 1:
                parts = [parts[i] + parts[i + 1] for i in range(0, len(parts), 2)]
            array = parts[0]
        return array


def join(arrays):
    return jnp.concatenate(arrays, axis=0)


def top(array):
    return array[: array.shape[0] // 2]


def bottom(array):
    return array[array.shape[0] // 2 :]


def gate(values, *others):
    return lax.optimization_barrier((values, others))[0]


def shards(
    tokens,
    lengths,
    cotangent,
    w_query,
    w_key,
    w_value,
    w_output,
    w_inner,
    w_outer,
    bias_query,
    bias_value,
    bias_output,
    norm1_gain,
    norm1_bias,
    bias_inner,
    bias_outer,
    norm2_gain,
    norm2_bias,
):
    fsdp = lax.axis_size("fsdp")
    exchange = Exchange(fsdp)
    rows, model = tokens.shape
    seqs = rows // SEQ
    block = w_query.shape[0]
    width = w_query.shape[1]
    half = model // 2

    here = lax.axis_index("fsdp")
    masks = jnp.repeat(jnp.asarray(exchange.masks, jnp.int32), block)
    inside = jnp.tile(jnp.arange(block, dtype=jnp.int32), fsdp)
    source = (here ^ masks) * block + inside
    place = jnp.arange(model, dtype=jnp.int32)[:, None] == source[None, :]
    place16 = place.astype(bf16)
    place32 = place.astype(f32)
    lengths_here = lax.dynamic_slice_in_dim(lengths, lax.axis_index("tp") * seqs, seqs, 0)

    def permuted(vectors, dims):
        return lax.dot_general(
            vectors, place32, ((dims), ((), ())), precision=lax.Precision.HIGHEST, preferred_element_type=f32
        )

    zero = jnp.zeros((width,), f32)

    def qkv_bias(biases):
        return jnp.concatenate([biases[:width], zero, biases[width : 2 * width]])

    def inner_bias(biases):
        return biases[2 * width :]

    def merge(keep, received):
        return keep + received.astype(f32)

    flip, cross, flip_cross = exchange.flip, exchange.cross, exchange.flip_cross

    def ring(array):
        return flip(array, 2), cross(array), flip_cross(array, 2)

    shard_qkv = jnp.concatenate([w_query, w_key, w_value], axis=1).astype(bf16)
    biases_own = jnp.concatenate([bias_query, bias_value, bias_inner])
    biases_other = cross(biases_own)
    far_qkv = exchange.gather_far(shard_qkv)
    inputs = dot_nn(tokens, place16).astype(bf16)
    vectors = jnp.stack([bias_output, norm1_gain, norm1_bias, bias_outer, norm2_gain, norm2_bias])

    far_qkv, shard_mid, shard_outer, cotangent, vectors = gate(
        (
            far_qkv,
            jnp.concatenate([w_output.T.astype(bf16), w_inner.astype(bf16)], axis=1),
            w_outer.T.astype(bf16),
            cotangent,
            vectors,
        ),
        inputs,
        biases_other,
    )
    far_qkv = join(far_qkv)
    near_qkv, across_qkv, corner_qkv = ring(far_qkv)
    far_mid = exchange.gather_far(shard_mid)
    cotan = dot_nn(cotangent, place16).astype(bf16)
    vectors = permuted(vectors, ((1,), (0,)))

    half_qkv_own, half_qkv_other, far_mid, shard_outer = gate(
        ((far_qkv, near_qkv), (across_qkv, corner_qkv), far_mid, shard_outer), cotan, vectors
    )
    half_qkv_own, half_qkv_other, far_mid = join(half_qkv_own), join(half_qkv_other), join(far_mid)
    pair_qkv_own, pair_qkv_other = flip(half_qkv_own, 1), flip(half_qkv_other, 1)
    near_mid, across_mid, corner_mid = ring(far_mid)
    far_outer = exchange.gather_far(shard_outer)
    qkv_own = (half_qkv_own, pair_qkv_own)
    proj_own, context_own, lse_own = attend_forward(inputs, qkv_own, qkv_bias(biases_own), lengths_here)
    qkv_other = gate((half_qkv_other, pair_qkv_other), context_own)
    proj_other, context_other, lse_other = attend_forward(inputs, qkv_other, qkv_bias(biases_other), lengths_here)

    half_mid_own, half_mid_other, far_outer, context_other = gate(
        ((far_mid, near_mid), (across_mid, corner_mid), far_outer, context_other)
    )
    half_mid_own, half_mid_other, far_outer = join(half_mid_own), join(half_mid_other), join(far_outer)
    pair_mid_own, pair_mid_other = flip(half_mid_own, 1), flip(half_mid_other, 1)
    near_outer, across_outer, corner_outer = ring(far_outer)
    mid_own, mid_other = (half_mid_own, pair_mid_own), (half_mid_other, pair_mid_other)
    out_own, out_other = [[piece[:, :width] for piece in mid] for mid in (mid_own, mid_other)]
    inner_own, inner_other = [[piece[:, width:] for piece in mid] for mid in (mid_own, mid_other)]
    normal_one, scale_one, normed16 = attention_out(context_own, context_other, out_own, out_other, inputs, vectors)
    hidden_own, slope_own = hidden_parts(normed16, inner_own, inner_bias(biases_own))
    left = gate(normed16, hidden_own)
    hidden_other, slope_other = hidden_parts(left, inner_other, inner_bias(biases_other))

    half_outer_own, half_outer_other, hidden_other = gate(
        ((far_outer, near_outer), (across_outer, corner_outer), hidden_other)
    )
    half_outer_own, half_outer_other = join(half_outer_own), join(half_outer_other)
    outer_own = (half_outer_own, flip(half_outer_own, 1))
    outer_other = (half_outer_other, flip(half_outer_other, 1))

    mixed, d_before, d_ffn, sums_two = turn(
        hidden_own, hidden_other, outer_own, outer_other, normal_one, cotan, vectors, place16
    )

    def swap(arrays):
        return [flip(array, 1) for array in arrays]

    def spread(own_lower, other_upper, other_lower):
        return flip(own_lower, 2), cross(other_upper), flip_cross(other_lower, 2)

    def add_all(keep, parts):
        for part in parts:
            keep = merge(keep, part)
        return keep

    send_outer = send_grads(d_ffn, hidden_own, hidden_other)

    send_outer, d_ffn = gate((send_outer, d_ffn))
    pair_outer = swap(send_outer)
    d_inner_own, inner_sums_own = d_hidden(d_ffn, outer_own, slope_own)

    pair_outer, d_ffn, d_inner_own = gate((pair_outer, d_ffn, d_inner_own))
    keep_outer, *away_outer = keep_grads(d_ffn, (hidden_own, hidden_other), pair_outer, (f32, bf16))

    keep_outer, away_outer, d_ffn = gate((keep_outer, away_outer, d_ffn))
    ring_outer = spread(*away_outer)
    d_inner_other, inner_sums_other = d_hidden(d_ffn, outer_other, slope_other)
    send_inner = send_grads(normed16, d_inner_own, d_inner_other)

    send_inner, d_inner_other, normed16 = gate((send_inner, d_inner_other, normed16))
    pair_inner = swap(send_inner)
    d_summed, d_attn, d_context_own, d_context_other, sums_one = d_attention(
        d_inner_own, d_inner_other, inner_own, inner_other, d_before, normal_one, scale_one, vectors, out_own, out_other
    )

    pair_inner, d_attn, normed16 = gate((pair_inner, d_attn, normed16))
    keep_inner, *away_inner = keep_grads(normed16, (d_inner_own, d_inner_other), pair_inner, (f32, bf16))

    keep_inner, away_inner, d_attn = gate((keep_inner, away_inner, d_attn))
    ring_inner = spread(*away_inner)
    send_output = send_grads(d_attn, context_own, context_other)

    send_output, keep_outer, ring_outer, d_context_other = gate((send_output, keep_outer, ring_outer, d_context_other))
    pair_output = swap(send_output)
    sum_outer = exchange.scatter_far(add_all(keep_outer, ring_outer))
    d_proj_other, qkv_sums_other = attend_backward(
        proj_other, context_other, d_context_other, lse_other, lengths_here
    )
    send_qkv_other = send_grads(inputs, d_proj_other)

    send_qkv_other, pair_output, d_attn = gate((send_qkv_other, pair_output, d_attn))
    pair_qkv_other = swap(send_qkv_other)
    keep_output, *away_output = keep_grads(d_attn, (context_own, context_other), pair_output, (f32, bf16))

    pair_qkv_other, keep_output, d_proj_other = gate((pair_qkv_other, keep_output, d_proj_other))
    upper_qkv_other, lower_qkv_other = keep_grads(inputs, (d_proj_other,), pair_qkv_other, (bf16,))

    upper_qkv_other, lower_qkv_other, away_output, d_context_own = gate(
        (upper_qkv_other, lower_qkv_other, away_output, d_context_own)
    )
    ring_output = spread(*away_output)
    ring_qkv = (cross(upper_qkv_other), flip_cross(lower_qkv_other, 2))
    d_proj_own, qkv_sums_own = attend_backward(proj_own, context_own, d_context_own, lse_own, lengths_here)
    send_qkv_own = send_grads(inputs, d_proj_own)

    send_qkv_own, keep_inner, ring_inner, keep_output, ring_output, d_proj_own, qkv_sums_own = gate(
        (send_qkv_own, keep_inner, ring_inner, keep_output, ring_output, d_proj_own, qkv_sums_own), sum_outer
    )
    pair_qkv_own = swap(send_qkv_own)
    whole = permuted(jnp.concatenate([sums_one[:3], sums_two[:3]]), ((1,), (1,))).reshape(-1)
    small_own = jnp.concatenate([qkv_sums_own[0], qkv_sums_own[1], inner_sums_own[0], whole])
    small_other = jnp.concatenate([qkv_sums_other[0], qkv_sums_other[1], inner_sums_other[0], whole])
    across_small = cross(small_other)
    sum_inner = exchange.scatter_far(add_all(keep_inner, ring_inner))
    sum_output = exchange.scatter_far(add_all(keep_output, ring_output))

    pair_qkv_own, d_proj_own, across_small, small_own = gate((pair_qkv_own, d_proj_own, across_small, small_own))
    keep_qkv, away_qkv = keep_grads(inputs, (d_proj_own,), pair_qkv_own, (f32,))

    keep_qkv, away_qkv, d_proj_own = gate((keep_qkv, away_qkv, d_proj_own))
    near_qkv = flip(away_qkv, 2)
    small = small_own + across_small
    near_small = flip(small, 2)
    grad_tokens = d_inputs(d_summed, d_proj_own, d_proj_other, qkv_own, qkv_other, place16)

    keep_qkv, near_qkv, ring_qkv, small, near_small, grad_tokens = gate(
        (keep_qkv, near_qkv, ring_qkv, small, near_small, grad_tokens), sum_output, sum_inner
    )
    sum_qkv = exchange.scatter_far(add_all(keep_qkv, (near_qkv,) + tuple(ring_qkv)))
    small = small + near_small
    small = small + flip(small, 1)
    small = exchange.total_far(small)

    inner_width = bias_inner.shape[0]
    cuts = np.cumsum([width, width, inner_width] + [model] * 6)
    query_bias, value_bias, inner_bias_sum, *rest = jnp.split(small, cuts[:-1])

    return (
        mixed,
        grad_tokens,
        sum_qkv[:, :width],
        sum_qkv[:, width : 2 * width],
        sum_qkv[:, 2 * width :],
        sum_output.T,
        sum_inner,
        sum_outer.T,
        query_bias,
        value_bias,
        rest[0],
        rest[1],
        rest[2],
        inner_bias_sum,
        rest[3],
        rest[4],
        rest[5],
    )


def solution(mesh):
    both = P(("fsdp", "tp"), None)
    cols, rows = P("fsdp", "tp"), P("tp", "fsdp")
    return jax.shard_map(
        shards,
        mesh=mesh,
        in_specs=(both, P("fsdp"), both, cols, cols, cols, rows, cols, rows)
        + (P("tp"), P("tp"), P(), P(), P(), P("tp"), P(), P(), P()),
        out_specs=(both, both, cols, cols, cols, rows, cols, rows)
        + (P("tp"), P("tp"), P(), P(), P(), P("tp"), P(), P(), P()),
        check_vma=False,
    )
```

time: 417 us -> 310 us (0.74)
  waiting for transfers between devices: 164 us -> 52 us
  matrix products: 107 us -> 7.39 us
  Pallas kernels: 39.4 us -> 135 us
  starting transfers between devices: 53.9 us -> 68.1 us
  other arithmetic: 23.2 us -> 14.1 us
  local copies, waits for them, and re-layouts: 20.2 us -> 24.9 us
    ppermute x48 -> x47, waiting for transfers between devices: 128 us -> 27.7 us  [flip(): return lax.ppermute(array, 'fsdp', [(i, i ^ bit) for i in range(self.fsdp)])]
    pallas_call x0 -> x18, Pallas kernels: none -> 87.6 us  [in_vmem(): pl.pallas_call(kernel, in_specs=[pl.BlockSpec(memory_space=pltpu.VMEM)] *...]
    dot_general x29 -> x2, matrix products: 57.7 us -> 1.95 us  [permuted(): lax.dot_general(vectors, place32, (dims, ((), ())), precision=lax.Precisi...]
    dot_general x10 -> x2, matrix products: 49.4 us -> 5.44 us  [dot_nn(): lax.dot_general(left, right, (((1,), (0,)), ((), ())), preferred_element_...]
    ppermute x10 -> x9, waiting for transfers between devices: 35.7 us -> 12.5 us  [cross(): return lax.ppermute(array, 'tp', [(0, 1), (1, 0)])]
    ppermute x0 -> x7, waiting for transfers between devices: none -> 11.8 us  [flip_cross(): return lax.ppermute(array, ('fsdp', 'tp'), pairs)]
    ppermute x0 -> x7, starting transfers between devices: none -> 11 us  [flip_cross(): return lax.ppermute(array, ('fsdp', 'tp'), pairs)]
    reduce_sum x7 -> x0, other arithmetic: 8.87 us -> none  [the longest x1 4.08 us: shards(): grad_outer_bias = jnp.sum(d_before, axis=0)]
  transfers between devices with their start and end apart: 58 -> 63, of which waited for: 22 -> 20; matrix products, arithmetic and copies ran while one was open for 16% -> 10% of each run, Pallas kernels for 4% -> 36%
where the time goes in v2:
time: 310 us; the launch traced here: 304 us
  Pallas kernels  135 us (44%)
  starting transfers between devices  68.1 us (22%)
  waiting for transfers between devices  52 us (17%)
  local copies, waits for them, and re-layouts  24.9 us (8%)
  other arithmetic  14.1 us (5%)
  matrix products  7.39 us (2%)
    pallas_call x18, Pallas kernels, in_vmem(): pl.pallas_call(kernel, in_specs=[pl.BlockSpec(memory_space=pltpu.VMEM)] *...  87.6 us
    ppermute x47, starting transfers between devices, flip(): return lax.ppermute(array, 'fsdp', [(i, i ^ bit) for i in range(self.fsdp)])  47.1 us
    ppermute x47, waiting for transfers between devices, flip(): return lax.ppermute(array, 'fsdp', [(i, i ^ bit) for i in range(self.fsdp)])  27.7 us
    pallas_call x2, Pallas kernels, attend_forward(): pl.pallas_call(functools.partial(attend_forward_kernel, pairs), grid_spec...  26.4 us
    pallas_call x2, Pallas kernels, attend_backward(): pl.pallas_call(functools.partial(attend_backward_kernel, pairs), grid_spe...  21.4 us
    unnamed x119, local copies, waits for them, and re-layouts  16.7 us
    ppermute x9, waiting for transfers between devices, cross(): return lax.ppermute(array, 'tp', [(0, 1), (1, 0)])  12.5 us
    ppermute x7, waiting for transfers between devices, flip_cross(): return lax.ppermute(array, ('fsdp', 'tp'), pairs)  11.8 us
  transfers between devices with their start and end apart: 63, of which 20 were waited for; matrix products, arithmetic and copies ran while one was open for 10% of the time, Pallas kernels for 36%

profile of v2, /device:TPU:0, one launch (start us, length us, event | category | flops | bytes accessed | tf_op | source)
XLA Modules:
  0.0 304.0 jit_solution(4191078002910789285)
XLA Ops:
  3.5 5.1 %collective-permute-start.2 = (bf16[48,1152]{1,0:T(8,128)(2,1)S(1)}, bf16[48,1152]{1,0:T(8,128)(2,1)S(1)}, u32[]{:S(2)}, u32[]{:S(2)}) collective-permute-start(bf16[48,1152]{1,0:T(8,128)(2,1)S(1)} %pad_maximum_fusion.1), channel_id=1, source_target_pairs={{0,24},{2,26},{4,28},{6,30},{8,16},{10,18},{12,20},{14,22},{16,8},... | collective-permute-start | bytes 331784 | tf_op jit(solution)/shard_map/ppermute | solution.py:478
  18.0 2.7 collective-permute-start.9
  26.2 4.0 %fusion.6.cotan_ref = bf16[1024,768]{1,0:T(8,128)(2,1)} fusion(bf16[1024,768]{1,0:T(8,128)(2,1)} %param.21, s32[768]{0:T(1024)S(1)} %add.105), kind=kOutput, calls=%fused_computation.7 | convolution fusion | flops 1209335808 | bytes 3148800 | tf_op jit(solution)/shard_map/dot_general | solution.py:41
  30.2 3.3 %collective-permute-start.7 = (bf16[48,1920]{1,0:T(8,128)(2,1)S(1)}, bf16[48,1920]{1,0:T(8,128)(2,1)S(1)}, u32[]{:S(2)}, u32[]{:S(2)}) collective-permute-start(bf16[48,1920]{1,0:T(8,128)(2,1)S(1)} %pad_maximum_fusion), channel_id=1, source_target_pairs={{0,8},{2,10},{4,12},{6,14},{8,0},{10,2},{12,4},{14,6},{16,24},{18,... | collective-permute-start | bytes 552968 | tf_op jit(solution)/shard_map/ppermute | solution.py:478
  35.3 2.6 collective-permute-done.7
  37.9 5.8 %collective-permute-done.5 = bf16[192,1152]{1,0:T(8,128)(2,1)S(1)} collective-permute-done((bf16[192,1152]{1,0:T(8,128)(2,1)S(1)}, bf16[192,1152]{1,0:T(8,128)(2,1)S(1)}, u32[]{:S(2)}, u32[]{:S(2)}) %collective-permute-start.5) | collective-permute-done | bytes 442400 | tf_op jit(solution)/shard_map/ppermute | solution.py:481
  54.5 2.7 collective-permute-start.15
  58.6 13.2 %attend_forward.2 = (bf16[1024,1152]{1,0:T(8,128)(2,1)S(1)}, bf16[1024,384]{1,0:T(8,128)(2,1)S(1)}, f32[2,6,512]{2,1,0:T(8,128)S(1)}) custom-call(s32[2]{0:T(128)S(1)} %dynamic_slice.3.lengths_ref, bf16[1024,768]{1,0:T(8,128)(2,1)S(1)} %fusion.7.inputs_ref.left_ref, bf16[384,1152]{1,0:T(8,128)(2,1)S(1)} %copy-done.9, ...), custom_call_target="tpu_custom_call" | custom-call | flops 18000000 | bytes 1024 | tf_op jit(solution)/shard_map/attend_forward/pallas_call | solution.py:131
  73.2 13.2 %attend_forward.3 = (bf16[1024,1152]{1,0:T(8,128)(2,1)S(1)}, bf16[1024,384]{1,0:T(8,128)(2,1)S(1)}, f32[2,6,512]{2,1,0:T(8,128)S(1)}) custom-call(s32[2]{0:T(128)S(1)} %dynamic_slice.3.lengths_ref, bf16[1024,768]{1,0:T(8,128)(2,1)S(1)} %fusion.7.inputs_ref.left_ref, bf16[384,1152]{1,0:T(8,128)(2,1)} %constant_dynamic-update-slice_fusion.10.first_ref.other_a, ...), custom_call_target="tpu_custom_call" | custom-call | flops 18000000 | bytes 1024 | tf_op jit(solution)/shard_map/attend_forward/pallas_call | solution.py:131
  92.6 2.4 collective-permute-start.22
  96.6 3.8 %attention_out.1 = (f32[1024,768]{1,0:T(8,128)S(1)}, f32[1024,1]{1,0:T(8,128)S(1)}, bf16[1024,768]{1,0:T(8,128)(2,1)S(1)}) custom-call(bf16[1024,384]{1,0:T(8,128)(2,1)S(1)} %get-tuple-element.183.own_ref.refs_0_.context_ref, bf16[1024,384]{1,0:T(8,128)(2,1)S(1)} %get-tuple-element.194.other_ref.refs_1_.context_ref, ...), custom_call_target="tpu_custom_call" | custom-call | flops 18000000 | bytes 1024 | tf_op jit(solution)/shard_map/attention_out/pallas_call | solution.py:229
  100.5 8.6 %hidden.2 = (bf16[1024,1536]{1,0:T(8,128)(2,1)S(1)}, bf16[1024,1536]{1,0:T(8,128)(2,1)S(1)}) custom-call(bf16[1024,768]{1,0:T(8,128)(2,1)S(1)} %get-tuple-element.244.normed_ref.left_ref, bf16[384,1536]{1,0:T(8,128)(2,1)S(1)} %slice.170.w_a.own_a, bf16[384,1536]{1,0:T(8,128)(2,1)S(1)} %slice.171.w_b.own_b, f32[1,1536]{1,0:T(1,128)S(1)} %broadcast_in_dim.24.shift_ref), custom_call_target="tpu_custom_call" | custom-call | flops 18000000 | bytes 1024 | tf_op jit(solution)/shard_map/hidden/pallas_call | solution.py:229
  109.1 8.6 %hidden.3 = (bf16[1024,1536]{1,0:T(8,128)(2,1)S(1)}, bf16[1024,1536]{1,0:T(8,128)(2,1)S(1)}) custom-call(bf16[1024,768]{1,0:T(8,128)(2,1)S(1)} %get-tuple-element.244.normed_ref.left_ref, bf16[384,1536]{1,0:T(8,128)(2,1)S(1)} %slice.172.w_a.other_a, bf16[384,1536]{1,0:T(8,128)(2,1)S(1)} %slice.173.w_b.other_b, f32[1,1536]{1,0:T(1,128)S(1)} %broadcast_in_dim.25.shift_ref), custom_call_target="tpu_custom_call" | custom-call | flops 18000000 | bytes 1024 | tf_op jit(solution)/shard_map/hidden/pallas_call | solution.py:229
  117.7 3.7 %collective-permute-done.21 = bf16[192,1536]{1,0:T(8,128)(2,1)S(1)} collective-permute-done((bf16[192,1536]{1,0:T(8,128)(2,1)S(1)}, bf16[192,1536]{1,0:T(8,128)(2,1)S(1)}, u32[]{:S(2)}, u32[]{:S(2)}) %collective-permute-start.21) | collective-permute-done | bytes 589856 | tf_op jit(solution)/shard_map/ppermute | solution.py:481
  126.2 13.2 %turn.1 = (bf16[1024,768]{1,0:T(8,128)(2,1)}, f32[1024,768]{1,0:T(8,128)S(1)}, bf16[1024,768]{1,0:T(8,128)(2,1)S(1)}, f32[8,768]{1,0:T(8,128)S(1)}) custom-call(bf16[1024,1536]{1,0:T(8,128)(2,1)S(1)} %get-tuple-element.200.own_ref.refs_0_, bf16[1024,1536]{1,0:T(8,128)(2,1)S(1)} %get-tuple-element.207.other_ref.refs_1_, ...), custom_call_target="tpu_custom_call" | custom-call | flops 18000000 | bytes 1024 | tf_op jit(solution)/shard_map/turn/pallas_call | solution.py:229
  139.4 2.6 send_grads.5
  142.7 4.1 %d_hidden.2 = (bf16[1024,1536]{1,0:T(8,128)(2,1)S(1)}, f32[8,1536]{1,0:T(8,128)S(1)}) custom-call(bf16[1024,768]{1,0:T(8,128)(2,1)S(1)} %get-tuple-element.232.left_ref.d_ffn_ref, bf16[384,1536]{1,0:T(8,128)(2,1)S(1)} %constant_dynamic-update-slice_fusion.20.own_a.w_a, bf16[384,1536]{1,0:T(8,128)(2,1)S(1)} %collective-permute-done.23.own_b.w_b, ...), custom_call_target="tpu_custom_call" | custom-call | flops 18000000 | bytes 1024 | tf_op jit(solution)/shard_map/d_hidden/pallas_call | solution.py:229
  146.8 3.4 %keep_grads.5 = (f32[192,1536]{1,0:T(8,128)S(1)}, bf16[192,1536]{1,0:T(8,128)(2,1)}, bf16[192,1536]{1,0:T(8,128)(2,1)}, bf16[192,1536]{1,0:T(8,128)(2,1)S(1)}) custom-call(bf16[1024,768]{1,0:T(8,128)(2,1)S(1)} %get-tuple-element.232.left_ref.d_ffn_ref, bf16[1024,1536]{1,0:T(8,128)(2,1)S(1)} %get-tuple-element.200.own_ref.refs_0_, ...), custom_call_target="tpu_custom_call" | custom-call | flops 18000000 | bytes 1024 | tf_op jit(solution)/shard_map/keep_grads/pallas_call | solution.py:229
  150.2 4.1 %d_hidden.3 = (bf16[1024,1536]{1,0:T(8,128)(2,1)S(1)}, f32[8,1536]{1,0:T(8,128)S(1)}) custom-call(bf16[1024,768]{1,0:T(8,128)(2,1)S(1)} %get-tuple-element.232.left_ref.d_ffn_ref, bf16[384,1536]{1,0:T(8,128)(2,1)S(1)} %constant_dynamic-update-slice_fusion.22.other_a.w_a, bf16[384,1536]{1,0:T(8,128)(2,1)S(1)} %copy-done.12, bf16[1024,1536]{1,0:T(8,128)(2,1)S(1)} %copy-done.16), custom_call_target="tpu_custom_call" | custom-call | flops 18000000 | bytes 1024 | tf_op jit(solution)/shard_map/d_hidden/pallas_call | solution.py:229
  154.4 2.6 send_grads.6
  161.1 10.9 %d_attention.1 = (f32[1024,768]{1,0:T(8,128)S(1)}, bf16[1024,768]{1,0:T(8,128)(2,1)S(1)}, bf16[1024,384]{1,0:T(8,128)(2,1)S(1)}, bf16[1024,384]{1,0:T(8,128)(2,1)S(1)}, f32[8,768]{1,0:T(8,128)S(1)}) custom-call(bf16[1024,1536]{1,0:T(8,128)(2,1)S(1)} %get-tuple-element.224.refs_0_.own_ref, bf16[1024,1536]{1,0:T(8,128)(2,1)S(1)} %get-tuple-element.239.refs_1_.other_ref, ...), custom_call_target="tpu_custom_call" | custom-call | flops 18000000 | bytes 1024 | tf_op jit(solution)/shard_map/d_attention/pallas_call | solution.py:229
  174.5 2.6 keep_grads.6
  178.3 8.7 %collective-permute-done.31 = bf16[192,1536]{1,0:T(8,128)(2,1)S(1)} collective-permute-done((bf16[192,1536]{1,0:T(8,128)(2,1)S(1)}, bf16[192,1536]{1,0:T(8,128)(2,1)S(1)}, u32[]{:S(2)}, u32[]{:S(2)}) %collective-permute-start.31) | collective-permute-done | bytes 589856 | tf_op jit(solution)/shard_map/ppermute | solution.py:485
  188.9 10.6 %attend_backward.2 = (bf16[1024,1152]{1,0:T(8,128)(2,1)S(1)}, f32[8,384]{1,0:T(8,128)S(1)}) custom-call(s32[2]{0:T(128)S(1)} %dynamic_slice.3.lengths_ref, bf16[1024,1152]{1,0:T(8,128)(2,1)S(1)} %copy-done.24, bf16[1024,384]{1,0:T(8,128)(2,1)S(1)} %get-tuple-element.194.other_ref.refs_1_.context_ref, bf16[1024,384]{1,0:T(8,128)(2,1)S(1)} %get-tuple-element.260.d_context_ref, ...), custom_call_target="tpu_custom_call" | custom-call | flops 18000000 | bytes 1024 | tf_op jit(solution)/shard_map/attend_backward/pallas_call | solution.py:205
  217.0 2.7 keep_grads.8
  226.7 10.8 %attend_backward.3 = (bf16[1024,1152]{1,0:T(8,128)(2,1)S(1)}, f32[8,384]{1,0:T(8,128)S(1)}) custom-call(s32[2]{0:T(128)S(1)} %dynamic_slice.3.lengths_ref, bf16[1024,1152]{1,0:T(8,128)(2,1)S(1)} %copy-done.22, bf16[1024,384]{1,0:T(8,128)(2,1)S(1)} %get-tuple-element.183.own_ref.refs_0_.context_ref, bf16[1024,384]{1,0:T(8,128)(2,1)S(1)} %copy-done.31, ...), custom_call_target="tpu_custom_call" | custom-call | flops 18000000 | bytes 1024 | tf_op jit(solution)/shard_map/attend_backward/pallas_call | solution.py:205
  240.0 3.0 collective-permute-done.39
  251.8 2.6 collective-permute-start.53
  265.1 4.6 %collective-permute-done.54 = bf16[48,1536]{1,0:T(8,128)(2,1)S(1)} collective-permute-done((bf16[48,1536]{1,0:T(8,128)(2,1)S(1)}, bf16[48,1536]{1,0:T(8,128)(2,1)S(1)}, u32[]{:S(2)}, u32[]{:S(2)}) %collective-permute-start.54) | collective-permute-done | bytes 147488 | tf_op jit(solution)/shard_map/ppermute | solution.py:478
  270.4 13.2 %d_inputs.1 = f32[1024,768]{1,0:T(8,128)} custom-call(f32[1024,768]{1,0:T(8,128)S(1)} %copy-done.20, bf16[1024,1152]{1,0:T(8,128)(2,1)S(1)} %get-tuple-element.313.refs_0_.own_ref, bf16[1024,1152]{1,0:T(8,128)(2,1)S(1)} %copy-done.3, bf16[384,1152]{1,0:T(8,128)(2,1)S(1)} %copy-done.10, bf16[384,1152]{1,0:T(8,128)(2,1)} %collective-permute-done.10.second_ref.own_b, ...), custom_call_target="tpu_custom_call" | custom-call | flops 18000000 | bytes 1024 | tf_op jit(solution)/shard_map/d_inputs/pallas_call | solution.py:229
  296.9 2.4 collective-permute-done.58
  299.3 3.8 %collective-permute-done.57 = bf16[48,1152]{1,0:T(8,128)(2,1)S(1)} collective-permute-done((bf16[48,1152]{1,0:T(8,128)(2,1)S(1)}, bf16[48,1152]{1,0:T(8,128)(2,1)S(1)}, u32[]{:S(2)}, u32[]{:S(2)}) %collective-permute-start.57) | collective-permute-done | bytes 110624 | tf_op jit(solution)/shard_map/ppermute | solution.py:478
  (312 shorter events, 116.4 us)
Async XLA Ops:
  3.5 13.6 %collective-permute-start.2 = (bf16[48,1152]{1,0:T(8,128)(2,1)S(1)}, bf16[48,1152]{1,0:T(8,128)(2,1)S(1)}, u32[]{:S(2)}, u32[]{:S(2)}) collective-permute-start(bf16[48,1152]{1,0:T(8,128)(2,1)S(1)} %pad_maximum_fusion.1), channel_id=1, source_target_pairs={{0,24},{2,26},{4,28},{6,30},{8,16},{10,18},{12,20},{14,22},{16,8},... | collective-permute-start | bytes 331784 | tf_op jit(solution)/shard_map/ppermute | solution.py:478
  20.7 14.6 %collective-permute-start.8 = (bf16[48,1920]{1,0:T(8,128)(2,1)S(1)}, bf16[48,1920]{1,0:T(8,128)(2,1)S(1)}, u32[]{:S(2)}, u32[]{:S(2)}) collective-permute-start(bf16[48,1920]{1,0:T(8,128)(2,1)S(1)} %pad_maximum_fusion), channel_id=1, source_target_pairs={{0,16},{2,18},{4,20},{6,22},{8,24},{10,26},{12,28},{14,30},{16,0},... | collective-permute-start | bytes 552968 | tf_op jit(solution)/shard_map/ppermute | solution.py:478
  22.6 15.3 %collective-permute-start.6 = (bf16[192,1152]{1,0:T(8,128)(2,1)S(1)}, bf16[192,1152]{1,0:T(8,128)(2,1)S(1)}, u32[]{:S(2)}, u32[]{:S(2)}) collective-permute-start(bf16[192,1152]{1,0:T(8,128)(2,1)S(1)} %constant_dynamic-update-slice_fusion), channel_id=1, source_target_pairs={{0,5},{1,4},{2,7},{3,6},{4,1},{5,0},{6,3},{7,2},{8,13},{9,12},{10,... | collective-permute-start | bytes 1327112 | tf_op jit(solution)/shard_map/ppermute | solution.py:485
  24.9 18.8 %collective-permute-start.5 = (bf16[192,1152]{1,0:T(8,128)(2,1)S(1)}, bf16[192,1152]{1,0:T(8,128)(2,1)S(1)}, u32[]{:S(2)}, u32[]{:S(2)}) collective-permute-start(bf16[192,1152]{1,0:T(8,128)(2,1)S(1)} %constant_dynamic-update-slice_fusion), channel_id=1, source_target_pairs={{0,1},{1,0},{2,3},{3,2},{4,5},{5,4},{6,7},{7,6},{8,9},{9,8},{10,11... | collective-permute-start | bytes 1327112 | tf_op jit(solution)/shard_map/ppermute | solution.py:481
  25.7 18.1 %collective-permute-start.4 = (bf16[192,1152]{1,0:T(8,128)(2,1)S(1)}, bf16[192,1152]{1,0:T(8,128)(2,1)S(1)}, u32[]{:S(2)}, u32[]{:S(2)}) collective-permute-start(bf16[192,1152]{1,0:T(8,128)(2,1)S(1)} %constant_dynamic-update-slice_fusion), channel_id=1, source_target_pairs={{0,4},{2,6},{4,0},{6,2},{8,12},{10,14},{12,8},{14,10},{16,20},{18,... | collective-permute-start | bytes 1327112 | tf_op jit(solution)/shard_map/ppermute | solution.py:478
  50.3 36.2 %collective-permute-start.13 = (bf16[192,1920]{1,0:T(8,128)(2,1)}, bf16[192,1920]{1,0:T(8,128)(2,1)}, u32[]{:S(2)}, u32[]{:S(2)}) collective-permute-start(bf16[192,1920]{1,0:T(8,128)(2,1)} %constant_dynamic-update-slice_fusion.6), channel_id=1, source_target_pairs={{0,5},{1,4},{2,7},{3,6},{4,1},{5,0},{6,3},{7,2},{8,13},{9,12},{10,... | collective-permute-start | bytes 2211848 | tf_op jit(solution)/shard_map/ppermute | solution.py:485
  52.6 33.9 %collective-permute-start.12 = (bf16[192,1920]{1,0:T(8,128)(2,1)}, bf16[192,1920]{1,0:T(8,128)(2,1)}, u32[]{:S(2)}, u32[]{:S(2)}) collective-permute-start(bf16[192,1920]{1,0:T(8,128)(2,1)} %constant_dynamic-update-slice_fusion.6), channel_id=1, source_target_pairs={{0,1},{1,0},{2,3},{3,2},{4,5},{5,4},{6,7},{7,6},{8,9},{9,8},{10,11... | collective-permute-start | bytes 2211848 | tf_op jit(solution)/shard_map/ppermute | solution.py:481
  53.8 32.7 %collective-permute-start.11 = (bf16[192,1920]{1,0:T(8,128)(2,1)}, bf16[192,1920]{1,0:T(8,128)(2,1)}, u32[]{:S(2)}, u32[]{:S(2)}) collective-permute-start(bf16[192,1920]{1,0:T(8,128)(2,1)} %constant_dynamic-update-slice_fusion.6), channel_id=1, source_target_pairs={{0,4},{2,6},{4,0},{6,2},{8,12},{10,14},{12,8},{14,10},{16,20},{18,... | collective-permute-start | bytes 2211848 | tf_op jit(solution)/shard_map/ppermute | solution.py:478
  54.5 32.0 %collective-permute-start.15 = (bf16[48,1536]{1,0:T(8,128)(2,1)S(1)}, bf16[48,1536]{1,0:T(8,128)(2,1)S(1)}, u32[]{:S(2)}, u32[]{:S(2)}) collective-permute-start(bf16[48,1536]{1,0:T(8,128)(2,1)S(1)} %convert_bitcast_fusion), channel_id=1, source_target_pairs={{0,16},{2,18},{4,20},{6,22},{8,24},{10,26},{12,28},{14,30},{16,0},... | collective-permute-start | bytes 442376 | tf_op jit(solution)/shard_map/ppermute | solution.py:478
  57.2 29.3 %collective-permute-start.14 = (bf16[48,1536]{1,0:T(8,128)(2,1)S(1)}, bf16[48,1536]{1,0:T(8,128)(2,1)S(1)}, u32[]{:S(2)}, u32[]{:S(2)}) collective-permute-start(bf16[48,1536]{1,0:T(8,128)(2,1)S(1)} %convert_bitcast_fusion), channel_id=1, source_target_pairs={{0,8},{2,10},{4,12},{6,14},{8,0},{10,2},{12,4},{14,6},{16,24},{18,... | collective-permute-start | bytes 442376 | tf_op jit(solution)/shard_map/ppermute | solution.py:478
  92.6 25.1 %collective-permute-start.22 = (bf16[192,1536]{1,0:T(8,128)(2,1)S(1)}, bf16[192,1536]{1,0:T(8,128)(2,1)S(1)}, u32[]{:S(2)}, u32[]{:S(2)}) collective-permute-start(bf16[192,1536]{1,0:T(8,128)(2,1)S(1)} %constant_dynamic-update-slice_fusion.16), channel_id=1, source_target_pairs={{0,5},{1,4},{2,7},{3,6},{4,1},{5,0},{6,3},{7,2},{8,13},{9,12},{10,... | collective-permute-start | bytes 1769480 | tf_op jit(solution)/shard_map/ppermute | solution.py:485
  95.0 26.4 %collective-permute-start.21 = (bf16[192,1536]{1,0:T(8,128)(2,1)S(1)}, bf16[192,1536]{1,0:T(8,128)(2,1)S(1)}, u32[]{:S(2)}, u32[]{:S(2)}) collective-permute-start(bf16[192,1536]{1,0:T(8,128)(2,1)S(1)} %constant_dynamic-update-slice_fusion.16), channel_id=1, source_target_pairs={{0,1},{1,0},{2,3},{3,2},{4,5},{5,4},{6,7},{7,6},{8,9},{9,8},{10,11... | collective-permute-start | bytes 1769480 | tf_op jit(solution)/shard_map/ppermute | solution.py:481
  95.5 25.9 %collective-permute-start.20 = (bf16[192,1536]{1,0:T(8,128)(2,1)S(1)}, bf16[192,1536]{1,0:T(8,128)(2,1)S(1)}, u32[]{:S(2)}, u32[]{:S(2)}) collective-permute-start(bf16[192,1536]{1,0:T(8,128)(2,1)S(1)} %constant_dynamic-update-slice_fusion.16), channel_id=1, source_target_pairs={{0,4},{2,6},{4,0},{6,2},{8,12},{10,14},{12,8},{14,10},{16,20},{18,... | collective-permute-start | bytes 1769480 | tf_op jit(solution)/shard_map/ppermute | solution.py:478
  157.0 17.6 %collective-permute-start.27 = (bf16[384,1536]{1,0:T(8,128)(2,1)S(1)}, bf16[384,1536]{1,0:T(8,128)(2,1)S(1)}, u32[]{:S(2)}, u32[]{:S(2)}) collective-permute-start(bf16[384,1536]{1,0:T(8,128)(2,1)S(1)} %get-tuple-element.237), channel_id=1, source_target_pairs={{0,2},{2,0},{4,6},{6,4},{8,10},{10,8},{12,14},{14,12},{16,18},{18,... | collective-permute-start | bytes 3538952 | tf_op jit(solution)/shard_map/ppermute | solution.py:478
  157.2 17.4 %collective-permute-start.28 = (bf16[384,1536]{1,0:T(8,128)(2,1)S(1)}, bf16[384,1536]{1,0:T(8,128)(2,1)S(1)}, u32[]{:S(2)}, u32[]{:S(2)}) collective-permute-start(bf16[384,1536]{1,0:T(8,128)(2,1)S(1)} %get-tuple-element.238), channel_id=1, source_target_pairs={{0,2},{2,0},{4,6},{6,4},{8,10},{10,8},{12,14},{14,12},{16,18},{18,... | collective-permute-start | bytes 3538952 | tf_op jit(solution)/shard_map/ppermute | solution.py:478
  157.6 20.7 %collective-permute-start.29 = (bf16[192,1536]{1,0:T(8,128)(2,1)}, bf16[192,1536]{1,0:T(8,128)(2,1)S(1)}, u32[]{:S(2)}, u32[]{:S(2)}) collective-permute-start(bf16[192,1536]{1,0:T(8,128)(2,1)} %get-tuple-element.256), channel_id=1, source_target_pairs={{0,4},{2,6},{4,0},{6,2},{8,12},{10,14},{12,8},{14,10},{16,20},{18,... | collective-permute-start | bytes 1769480 | tf_op jit(solution)/shard_map/ppermute | solution.py:478
  159.0 19.3 %collective-permute-start.30 = (bf16[192,1536]{1,0:T(8,128)(2,1)}, bf16[192,1536]{1,0:T(8,128)(2,1)S(1)}, u32[]{:S(2)}, u32[]{:S(2)}) collective-permute-start(bf16[192,1536]{1,0:T(8,128)(2,1)} %get-tuple-element.257), channel_id=1, source_target_pairs={{0,1},{1,0},{2,3},{3,2},{4,5},{5,4},{6,7},{7,6},{8,9},{9,8},{10,11... | collective-permute-start | bytes 1769480 | tf_op jit(solution)/shard_map/ppermute | solution.py:481
  160.5 26.5 %collective-permute-start.31 = (bf16[192,1536]{1,0:T(8,128)(2,1)S(1)}, bf16[192,1536]{1,0:T(8,128)(2,1)S(1)}, u32[]{:S(2)}, u32[]{:S(2)}) collective-permute-start(bf16[192,1536]{1,0:T(8,128)(2,1)S(1)} %get-tuple-element.258), channel_id=1, source_target_pairs={{0,5},{1,4},{2,7},{3,6},{4,1},{5,0},{6,3},{7,2},{8,13},{9,12},{10,... | collective-permute-start | bytes 1769480 | tf_op jit(solution)/shard_map/ppermute | solution.py:485
  187.0 14.9 %collective-permute-start.32 = (bf16[384,384]{1,0:T(8,128)(2,1)S(1)}, bf16[384,384]{1,0:T(8,128)(2,1)S(1)}, u32[]{:S(2)}, u32[]{:S(2)}) collective-permute-start(bf16[384,384]{1,0:T(8,128)(2,1)S(1)} %get-tuple-element.263), channel_id=1, source_target_pairs={{0,2},{2,0},{4,6},{6,4},{8,10},{10,8},{12,14},{14,12},{16,18},{18,... | collective-permute-start | bytes 884744 | tf_op jit(solution)/shard_map/ppermute | solution.py:478
  187.0 14.9 %collective-permute-start.33 = (bf16[384,384]{1,0:T(8,128)(2,1)S(1)}, bf16[384,384]{1,0:T(8,128)(2,1)S(1)}, u32[]{:S(2)}, u32[]{:S(2)}) collective-permute-start(bf16[384,384]{1,0:T(8,128)(2,1)S(1)} %get-tuple-element.264), channel_id=1, source_target_pairs={{0,2},{2,0},{4,6},{6,4},{8,10},{10,8},{12,14},{14,12},{16,18},{18,... | collective-permute-start | bytes 884744 | tf_op jit(solution)/shard_map/ppermute | solution.py:478
  187.5 36.6 %collective-permute-start.35 = (bf16[192,1536]{1,0:T(8,128)(2,1)}, bf16[192,1536]{1,0:T(8,128)(2,1)}, u32[]{:S(2)}, u32[]{:S(2)}) collective-permute-start(bf16[192,1536]{1,0:T(8,128)(2,1)} %get-tuple-element.282), channel_id=1, source_target_pairs={{0,4},{2,6},{4,0},{6,2},{8,12},{10,14},{12,8},{14,10},{16,20},{18,... | collective-permute-start | bytes 1769480 | tf_op jit(solution)/shard_map/ppermute | solution.py:478
  208.5 14.0 %collective-permute-start.42 = (bf16[48,1536]{1,0:T(8,128)(2,1)}, bf16[48,1536]{1,0:T(8,128)(2,1)}, u32[]{:S(2)}, u32[]{:S(2)}) collective-permute-start(bf16[48,1536]{1,0:T(8,128)(2,1)} %get-tuple-element.346), channel_id=1, source_target_pairs={{0,16},{2,18},{4,20},{6,22},{8,24},{10,26},{12,28},{14,30},{16,0},... | collective-permute-start | bytes 442376 | tf_op jit(solution)/shard_map/ppermute | solution.py:478
  210.7 28.2 %collective-permute-start.36 = (bf16[192,1536]{1,0:T(8,128)(2,1)}, bf16[192,1536]{1,0:T(8,128)(2,1)S(1)}, u32[]{:S(2)}, u32[]{:S(2)}) collective-permute-start(bf16[192,1536]{1,0:T(8,128)(2,1)} %copy-done.37), channel_id=1, source_target_pairs={{0,1},{1,0},{2,3},{3,2},{4,5},{5,4},{6,7},{7,6},{8,9},{9,8},{10,11... | collective-permute-start | bytes 1769480 | tf_op jit(solution)/shard_map/ppermute | solution.py:481
  212.2 27.7 %collective-permute-start.37 = (bf16[192,1536]{1,0:T(8,128)(2,1)}, bf16[192,1536]{1,0:T(8,128)(2,1)S(1)}, u32[]{:S(2)}, u32[]{:S(2)}) collective-permute-start(bf16[192,1536]{1,0:T(8,128)(2,1)} %copy-done.36), channel_id=1, source_target_pairs={{0,5},{1,4},{2,7},{3,6},{4,1},{5,0},{6,3},{7,2},{8,13},{9,12},{10,... | collective-permute-start | bytes 1769480 | tf_op jit(solution)/shard_map/ppermute | solution.py:485
  219.8 20.2 %collective-permute-start.38 = (bf16[192,384]{1,0:T(8,128)(2,1)S(1)}, bf16[192,384]{1,0:T(8,128)(2,1)S(1)}, u32[]{:S(2)}, u32[]{:S(2)}) collective-permute-start(bf16[192,384]{1,0:T(8,128)(2,1)S(1)} %get-tuple-element.286), channel_id=1, source_target_pairs={{0,4},{2,6},{4,0},{6,2},{8,12},{10,14},{12,8},{14,10},{16,20},{18,... | collective-permute-start | bytes 442376 | tf_op jit(solution)/shard_map/ppermute | solution.py:478
  222.5 20.4 %collective-permute-start.39 = (bf16[192,384]{1,0:T(8,128)(2,1)S(1)}, bf16[192,384]{1,0:T(8,128)(2,1)S(1)}, u32[]{:S(2)}, u32[]{:S(2)}) collective-permute-start(bf16[192,384]{1,0:T(8,128)(2,1)S(1)} %get-tuple-element.287), channel_id=1, source_target_pairs={{0,1},{1,0},{2,3},{3,2},{4,5},{5,4},{6,7},{7,6},{8,9},{9,8},{10,11... | collective-permute-start | bytes 442376 | tf_op jit(solution)/shard_map/ppermute | solution.py:481
  224.0 21.0 %collective-permute-start.40 = (bf16[192,384]{1,0:T(8,128)(2,1)S(1)}, bf16[192,384]{1,0:T(8,128)(2,1)S(1)}, u32[]{:S(2)}, u32[]{:S(2)}) collective-permute-start(bf16[192,384]{1,0:T(8,128)(2,1)S(1)} %get-tuple-element.288), channel_id=1, source_target_pairs={{0,5},{1,4},{2,7},{3,6},{4,1},{5,0},{6,3},{7,2},{8,13},{9,12},{10,... | collective-permute-start | bytes 442376 | tf_op jit(solution)/shard_map/ppermute | solution.py:485
  256.1 13.5 %collective-permute-start.54 = (bf16[48,1536]{1,0:T(8,128)(2,1)S(1)}, bf16[48,1536]{1,0:T(8,128)(2,1)S(1)}, u32[]{:S(2)}, u32[]{:S(2)}) collective-permute-start(bf16[48,1536]{1,0:T(8,128)(2,1)S(1)} %get-tuple-element.343), channel_id=1, source_target_pairs={{0,16},{2,18},{4,20},{6,22},{8,24},{10,26},{12,28},{14,30},{16,0},... | collective-permute-start | bytes 442376 | tf_op jit(solution)/shard_map/ppermute | solution.py:478
  256.8 26.8 %collective-permute-start.47 = (bf16[192,1152]{1,0:T(8,128)(2,1)S(1)}, bf16[192,1152]{1,0:T(8,128)(2,1)S(1)}, u32[]{:S(2)}, u32[]{:S(2)}) collective-permute-start(bf16[192,1152]{1,0:T(8,128)(2,1)S(1)} %get-tuple-element.308), channel_id=1, source_target_pairs={{0,1},{1,0},{2,3},{3,2},{4,5},{5,4},{6,7},{7,6},{8,9},{9,8},{10,11... | collective-permute-start | bytes 1327112 | tf_op jit(solution)/shard_map/ppermute | solution.py:481
  257.3 26.3 %collective-permute-start.48 = (bf16[192,1152]{1,0:T(8,128)(2,1)S(1)}, bf16[192,1152]{1,0:T(8,128)(2,1)S(1)}, u32[]{:S(2)}, u32[]{:S(2)}) collective-permute-start(bf16[192,1152]{1,0:T(8,128)(2,1)S(1)} %get-tuple-element.309), channel_id=1, source_target_pairs={{0,5},{1,4},{2,7},{3,6},{4,1},{5,0},{6,3},{7,2},{8,13},{9,12},{10,... | collective-permute-start | bytes 1327112 | tf_op jit(solution)/shard_map/ppermute | solution.py:485
  260.7 22.9 %collective-permute-start.49 = (f32[6912]{0:T(1024)S(1)}, f32[6912]{0:T(1024)S(1)}, u32[]{:S(2)}, u32[]{:S(2)}) collective-permute-start(f32[6912]{0:T(1024)S(1)} %add.112), channel_id=1, source_target_pairs={{0,4},{2,6},{4,0},{6,2},{8,12},{10,14},{12,8},{14,10},{16,20},{18,... | collective-permute-start | bytes 82952 | tf_op jit(solution)/shard_map/ppermute | solution.py:478
  264.1 20.7 %collective-permute-start.46 = (bf16[192,1152]{1,0:T(8,128)(2,1)S(1)}, bf16[192,1152]{1,0:T(8,128)(2,1)S(1)}, u32[]{:S(2)}, u32[]{:S(2)}) collective-permute-start(bf16[192,1152]{1,0:T(8,128)(2,1)S(1)} %get-tuple-element.307), channel_id=1, source_target_pairs={{0,4},{2,6},{4,0},{6,2},{8,12},{10,14},{12,8},{14,10},{16,20},{18,... | collective-permute-start | bytes 1327112 | tf_op jit(solution)/shard_map/ppermute | solution.py:478
  (83 other events, 547.2 us)

commit v3 on v2

v3 whole, which is shorter than its diff:
```python
import functools

import jax
import jax.numpy as jnp
import numpy as np
from jax import lax
from jax.experimental import pallas as pl
from jax.experimental.pallas import tpu as pltpu
from jax.sharding import PartitionSpec as P

DH = 64
SEQ = 512
PAIR = 2 * DH
norm_eps = 1e-12
masked_score = -1000000000.0
bf16 = jnp.bfloat16
f32 = jnp.float32
TILE = 256
COST = dict(
    attend_forward=39,
    attend_backward=0.02,
    attention_out=12,
    hidden=25.5,
    turn=39,
    d_hidden=10.8,
    d_attention=30,
    d_context=6,
    d_inputs=0.02,
    join=3,
    send_grads=0.02,
    keep_grads=10.5,
)


def cost(micros):
    return pl.CostEstimate(flops=int(micros * 9e8), bytes_accessed=1024, transcendentals=0)


def dot_nn(left, right):
    return lax.dot_general(left, right, (((1,), (0,)), ((), ())), preferred_element_type=f32)


def dot_nt(left, right):
    return lax.dot_general(left, right, (((1,), (1,)), ((), ())), preferred_element_type=f32)


def dot_tn(left, right):
    return lax.dot_general(left, right, (((0,), (0,)), ((), ())), preferred_element_type=f32)


ERF_P = 0.3275911
ERF_A = (0.254829592, -0.284496736, 1.421413741, -1.453152027, 1.061405429)


def gelu_parts(values):
    size = jnp.abs(values)
    t = 1.0 / (1.0 + (ERF_P * 2**-0.5) * size)
    expo = jnp.exp(-0.5 * values * values)
    poly = ERF_A[4]
    for coefficient in ERF_A[3::-1]:
        poly = poly * t + coefficient
    tail = (0.5 * poly) * (t * expo)
    phi = jnp.where(values < 0, tail, 1.0 - tail)
    return values * phi, phi + values * (expo * (2 * np.pi) ** -0.5)


def norm_parts(values):
    centred = values - jnp.mean(values, axis=-1, keepdims=True)
    scale = lax.rsqrt(jnp.mean(centred * centred, axis=-1, keepdims=True) + norm_eps)
    return centred * scale, scale


def norm_pull(grads, gain, normal, scale):
    inner = grads * gain
    return scale * (
        inner
        - jnp.mean(inner, axis=-1, keepdims=True)
        - normal * jnp.mean(inner * normal, axis=-1, keepdims=True)
    )


def fill(ref, column, pieces, start, width):
    part = pieces[0].shape[0]
    step = 32 if part % 32 == 0 else part
    for index, piece in enumerate(pieces):

        def one(at, carry, piece=piece, base=index * part):
            rows = pl.ds(pl.multiple_of(at * step, step), step)
            to = pl.ds(pl.multiple_of(base + at * step, step), step)
            ref[to, column : column + width] = piece[rows, start : start + width]
            return carry

        lax.fori_loop(0, part // step, one, 0)


def head_slice(block, head):
    return block[:, head * DH : (head + 1) * DH]


def live_rows(lengths_ref):
    rows = lax.broadcasted_iota(jnp.int32, (SEQ, 1), 0)
    return rows < lengths_ref[pl.program_id(0)]


def attend_forward_kernel(
    pairs, lengths_ref, inputs_ref, a_ref, b_ref, c_ref, d_ref, shift_ref, qkv_ref, context_ref, lse_ref, weight_ref
):
    live = live_rows(lengths_ref)
    width = pairs * PAIR

    @pl.when(pl.program_id(0) == 0)
    def _():
        fill(weight_ref, 0, (a_ref, b_ref, c_ref, d_ref), 0, 3 * width)

    qkv_ref[...] = (dot_nn(inputs_ref[...], weight_ref[...]) + shift_ref[...]).astype(bf16)

    def one_pair(index, carry):
        at = pl.multiple_of(index * PAIR, PAIR)
        query = qkv_ref[:, pl.ds(at, PAIR)] * jnp.asarray(DH ** (-0.5), bf16)
        keys = qkv_ref[:, pl.ds(width + at, PAIR)]
        values = qkv_ref[:, pl.ds(2 * width + at, PAIR)]
        turned = []
        for head in range(2):
            scores = dot_nt(head_slice(keys, head), head_slice(query, head))
            scores = jnp.where(live, scores, masked_score)
            top = jnp.max(scores, axis=0, keepdims=True)
            expo = jnp.exp(scores - top)
            total = jnp.sum(expo, axis=0, keepdims=True)
            probs = (expo * (1.0 / total)).astype(bf16)
            turned.append(dot_tn(head_slice(values, head), probs))
            lse_ref[0, pl.ds(index * 2 + head, 1), :] = top + jnp.log(total)
        context_ref[:, pl.ds(at, PAIR)] = jnp.concatenate(turned, axis=0).T.astype(bf16)
        return carry

    lax.fori_loop(0, pairs, one_pair, 0)


def attend_forward(inputs, pieces, shift, lengths):
    rows, model = inputs.shape
    part, _ = pieces[0].shape
    triple = shift.shape[0]
    width = triple // 3
    seqs, pairs = rows // SEQ, width // PAIR
    heads = 2 * pairs
    piece_spec = pl.BlockSpec((part, triple), lambda s, n: (0, 0), pipeline_mode=pl.Buffered(1))
    return pl.pallas_call(
        functools.partial(attend_forward_kernel, pairs),
        grid_spec=pltpu.PrefetchScalarGridSpec(
            num_scalar_prefetch=1,
            grid=(seqs,),
            in_specs=[pl.BlockSpec((SEQ, model), lambda s, n: (s, 0))]
            + [piece_spec] * 4
            + [pl.BlockSpec((1, triple), lambda s, n: (0, 0))],
            out_specs=[
                pl.BlockSpec((SEQ, triple), lambda s, n: (s, 0)),
                pl.BlockSpec((SEQ, width), lambda s, n: (s, 0)),
                pl.BlockSpec((1, heads, SEQ), lambda s, n: (s, 0, 0)),
            ],
            scratch_shapes=[pltpu.VMEM((model, triple), bf16)],
        ),
        out_shape=[
            jax.ShapeDtypeStruct((rows, triple), bf16),
            jax.ShapeDtypeStruct((rows, width), bf16),
            jax.ShapeDtypeStruct((seqs, heads, SEQ), f32),
        ],
        compiler_params=pltpu.CompilerParams(vmem_limit_bytes=18 << 20),
        cost_estimate=cost(COST["attend_forward"]),
        name="attend_forward",
    )(lengths, inputs, *pieces, shift[None, :])


def attend_backward_kernel(pairs, lengths_ref, qkv_ref, context_ref, d_context_ref, lse_ref, out_ref, sums_ref):
    live = live_rows(lengths_ref)

    @pl.when(pl.program_id(0) == 0)
    def _():
        sums_ref[...] = jnp.zeros_like(sums_ref)

    width = pairs * PAIR
    scale = DH ** (-0.5)

    def one_pair(index, carry):
        at = pl.multiple_of(index * PAIR, PAIR)
        query = qkv_ref[:, pl.ds(at, PAIR)] * jnp.asarray(scale, bf16)
        keys = qkv_ref[:, pl.ds(width + at, PAIR)]
        values = qkv_ref[:, pl.ds(2 * width + at, PAIR)]
        d_context = d_context_ref[:, pl.ds(at, PAIR)]
        weighed = (context_ref[:, pl.ds(at, PAIR)].astype(f32) * d_context.astype(f32)).T
        d_query, d_key, d_value = [], [], []
        for head in range(2):
            q_h, k_h, v_h = head_slice(query, head), head_slice(keys, head), head_slice(values, head)
            g_h = head_slice(d_context, head)
            row_dot = jnp.sum(weighed[head * DH : (head + 1) * DH], axis=0, keepdims=True)
            scores = jnp.where(live, dot_nt(k_h, q_h), masked_score)
            probs = jnp.exp(scores - lse_ref[0, pl.ds(index * 2 + head, 1), :])
            d_probs = dot_nt(v_h, g_h)
            d_scores = (probs * (d_probs - row_dot)).astype(bf16)
            d_value.append(dot_nn(probs.astype(bf16), g_h))
            d_key.append(dot_nn(d_scores, q_h))
            d_query.append(dot_tn(k_h, d_scores))
        turned = (jnp.concatenate(d_query, axis=0).T * scale).astype(bf16)
        d_value = jnp.concatenate(d_value, axis=1).astype(bf16)
        out_ref[:, pl.ds(at, PAIR)] = turned
        out_ref[:, pl.ds(width + at, PAIR)] = jnp.concatenate(d_key, axis=1).astype(bf16)
        out_ref[:, pl.ds(2 * width + at, PAIR)] = d_value
        sums_ref[0:1, pl.ds(at, PAIR)] += jnp.sum(turned.astype(f32), axis=0, keepdims=True)
        sums_ref[1:2, pl.ds(at, PAIR)] += jnp.sum(d_value.astype(f32), axis=0, keepdims=True)
        return carry

    lax.fori_loop(0, pairs, one_pair, 0)


def attend_backward(qkv, context, d_context, lse, lengths):
    rows, triple = qkv.shape
    width = triple // 3
    seqs, pairs = rows // SEQ, width // PAIR
    heads = 2 * pairs
    return pl.pallas_call(
        functools.partial(attend_backward_kernel, pairs),
        grid_spec=pltpu.PrefetchScalarGridSpec(
            num_scalar_prefetch=1,
            grid=(seqs,),
            in_specs=[
                pl.BlockSpec((SEQ, triple), lambda s, n: (s, 0)),
                pl.BlockSpec((SEQ, width), lambda s, n: (s, 0)),
                pl.BlockSpec((SEQ, width), lambda s, n: (s, 0)),
                pl.BlockSpec((1, heads, SEQ), lambda s, n: (s, 0, 0)),
            ],
            out_specs=[
                pl.BlockSpec((SEQ, triple), lambda s, n: (s, 0)),
                pl.BlockSpec((8, width), lambda s, n: (0, 0)),
            ],
        ),
        out_shape=[jax.ShapeDtypeStruct((rows, triple), bf16), jax.ShapeDtypeStruct((8, width), f32)],
        compiler_params=pltpu.CompilerParams(vmem_limit_bytes=14 << 20),
        cost_estimate=cost(COST["attend_backward"]),
        name="attend_backward",
    )(lengths, qkv, context, d_context, lse)


def in_vmem(kernel, name, limit, outs, *args, scratch=()):
    return pl.pallas_call(
        kernel,
        in_specs=[pl.BlockSpec(memory_space=pltpu.VMEM)] * len(args),
        out_specs=[pl.BlockSpec(memory_space=pltpu.VMEM)] * len(outs),
        out_shape=[jax.ShapeDtypeStruct(*out) for out in outs],
        scratch_shapes=[pltpu.VMEM(shape, bf16) for shape in scratch],
        compiler_params=pltpu.CompilerParams(vmem_limit_bytes=limit << 20),
        cost_estimate=cost(COST[name]),
        name=name,
    )(*args)


def tiles_of(ref, body):
    def one(index, carry):
        body(pl.ds(pl.multiple_of(index * TILE, TILE), TILE))
        return carry

    lax.fori_loop(0, ref.shape[0] // TILE, one, 0)


def add_sums(ref, row, values):
    ref[row : row + 1, :] += jnp.sum(values, axis=0, keepdims=True)


def side(one, other):
    return jnp.concatenate([one, other], axis=1)


def join_kernel(*refs):
    *pieces, out_ref = refs
    fill(out_ref, 0, pieces, 0, out_ref.shape[1])


def join(arrays):
    if len(arrays) == 1:
        return arrays[0]
    rows, width = arrays[0].shape
    if rows % 16:
        return jnp.concatenate(arrays, axis=0)
    return in_vmem(join_kernel, "join", 8, [((len(arrays) * rows, width), arrays[0].dtype)], *arrays)[0]


def attention_out_kernel(own_ref, other_ref, *refs):
    pieces, (inputs_ref, vectors_ref, normal_ref, scale_ref, normed_ref, weight_ref) = refs[:8], refs[8:]
    width = own_ref.shape[1]
    fill(weight_ref, 0, pieces[:4], 3 * width, width)
    fill(weight_ref, width, pieces[4:], 3 * width, width)

    def body(at):
        mixed = dot_nt(side(own_ref[at], other_ref[at]), weight_ref[...])
        normal, scale = norm_parts(mixed + vectors_ref[0:1] + inputs_ref[at].astype(f32))
        normal_ref[at] = normal
        scale_ref[at] = scale
        normed_ref[at] = (normal * vectors_ref[1:2] + vectors_ref[2:3]).astype(bf16)

    tiles_of(own_ref, body)


def attention_out(own, other, w_own, w_other, inputs, vectors):
    shape = inputs.shape
    outs = [(shape, f32), ((shape[0], 1), f32), (shape, bf16)]
    args = (own, other, *w_own, *w_other, inputs, vectors)
    return in_vmem(attention_out_kernel, "attention_out", 6, outs, *args, scratch=[(shape[1], shape[1])])


def hidden_kernel(normed_ref, *refs):
    pieces, (shift_ref, hidden_ref, slope_ref, weight_ref) = refs[:4], refs[4:]
    fill(weight_ref, 0, pieces, 0, weight_ref.shape[1])

    def body(at):
        hidden, slope = gelu_parts(dot_nn(normed_ref[at], weight_ref[...]) + shift_ref[...])
        hidden_ref[at] = hidden.astype(bf16)
        slope_ref[at] = slope.astype(bf16)

    tiles_of(normed_ref, body)


def hidden_parts(normed, w, shift):
    rows, model = normed.shape
    shape = (rows, w[0].shape[1])
    outs = [(shape, bf16), (shape, bf16)]
    args = (normed, *w, shift[None, :])
    return in_vmem(hidden_kernel, "hidden", 8, outs, *args, scratch=[(model, shape[1])])


def turn_kernel(own_ref, other_ref, *refs):
    pieces, (normal_one_ref, cotan_ref, vectors_ref, place_ref) = refs[:8], refs[8:12]
    mixed_ref, d_before_ref, d_ffn_ref, sums_ref, w_own_ref, w_other_ref = refs[12:]
    sums_ref[...] = jnp.zeros_like(sums_ref)
    fill(w_own_ref, 0, pieces[:4], 0, w_own_ref.shape[1])
    fill(w_other_ref, 0, pieces[4:], 0, w_other_ref.shape[1])

    def body(at):
        ffn = dot_nt(own_ref[at], w_own_ref[...]) + dot_nt(other_ref[at], w_other_ref[...])
        normed = normal_one_ref[at] * vectors_ref[1:2] + vectors_ref[2:3]
        normal, scale = norm_parts(ffn + vectors_ref[3:4] + normed)
        result = (normal * vectors_ref[4:5] + vectors_ref[5:6]).astype(bf16)
        mixed_ref[at] = dot_nt(result, place_ref[...]).astype(bf16)
        cotan = cotan_ref[at].astype(f32)
        d_before = norm_pull(cotan, vectors_ref[4:5], normal, scale)
        d_before_ref[at] = d_before
        d_ffn_ref[at] = d_before.astype(bf16)
        add_sums(sums_ref, 0, d_before)
        add_sums(sums_ref, 1, cotan * normal)
        add_sums(sums_ref, 2, cotan)

    tiles_of(own_ref, body)


def turn(own, other, w_own, w_other, normal_one, cotan, vectors, place):
    shape = normal_one.shape
    outs = [(shape, bf16), (shape, f32), (shape, bf16), ((8, shape[1]), f32)]
    args = (own, other, *w_own, *w_other, normal_one, cotan, vectors, place)
    return in_vmem(turn_kernel, "turn", 10, outs, *args, scratch=[(shape[1], own.shape[1])] * 2)


def d_hidden_kernel(d_ffn_ref, *refs):
    pieces, (slope_ref, d_inner_ref, sums_ref, weight_ref) = refs[:4], refs[4:]
    sums_ref[...] = jnp.zeros_like(sums_ref)
    fill(weight_ref, 0, pieces, 0, weight_ref.shape[1])

    def body(at):
        d_inner = (dot_nn(d_ffn_ref[at], weight_ref[...]) * slope_ref[at].astype(f32)).astype(bf16)
        d_inner_ref[at] = d_inner
        add_sums(sums_ref, 0, d_inner.astype(f32))

    tiles_of(d_ffn_ref, body)


def d_hidden(d_ffn, w, slope):
    outs = [(slope.shape, bf16), ((8, slope.shape[1]), f32)]
    return in_vmem(d_hidden_kernel, "d_hidden", 8, outs, d_ffn, *w, slope, scratch=[(d_ffn.shape[1], slope.shape[1])])


def d_attention_kernel(own_ref, other_ref, *refs):
    pieces, (d_before_ref, normal_ref, scale_ref, vectors_ref) = refs[:8], refs[8:12]
    d_summed_ref, d_attn_ref, sums_ref, w_own_ref, w_other_ref = refs[12:]
    sums_ref[...] = jnp.zeros_like(sums_ref)
    fill(w_own_ref, 0, pieces[:4], 0, w_own_ref.shape[1])
    fill(w_other_ref, 0, pieces[4:], 0, w_other_ref.shape[1])

    def body(at):
        d_normed = d_before_ref[at] + dot_nt(own_ref[at], w_own_ref[...]) + dot_nt(other_ref[at], w_other_ref[...])
        normal = normal_ref[at]
        d_summed = norm_pull(d_normed, vectors_ref[1:2], normal, scale_ref[at])
        d_summed_ref[at] = d_summed
        d_attn_ref[at] = d_summed.astype(bf16)
        add_sums(sums_ref, 0, d_summed)
        add_sums(sums_ref, 1, d_normed * normal)
        add_sums(sums_ref, 2, d_normed)

    tiles_of(own_ref, body)


def d_attention(own, other, w_own, w_other, d_before, normal, scale, vectors):
    shape = d_before.shape
    outs = [(shape, f32), (shape, bf16), ((8, shape[1]), f32)]
    args = (own, other, *w_own, *w_other, d_before, normal, scale, vectors)
    return in_vmem(d_attention_kernel, "d_attention", 10, outs, *args, scratch=[(shape[1], own.shape[1])] * 2)


def d_context_kernel(d_attn_ref, *refs):
    pieces, (own_ref, other_ref, weight_ref) = refs[:8], refs[8:]
    width = own_ref.shape[1]
    fill(weight_ref, 0, pieces[:4], 3 * width, width)
    fill(weight_ref, width, pieces[4:], 3 * width, width)

    def body(at):
        result = dot_nn(d_attn_ref[at], weight_ref[...]).astype(bf16)
        own_ref[at] = result[:, :width]
        other_ref[at] = result[:, width:]

    tiles_of(d_attn_ref, body)


def d_context(d_attn, w_own, w_other):
    rows, model = d_attn.shape
    outs = [((rows, model // 2), bf16)] * 2
    return in_vmem(d_context_kernel, "d_context", 5, outs, d_attn, *w_own, *w_other, scratch=[(model, model)])


def d_inputs_kernel(d_summed_ref, own_ref, other_ref, *refs):
    pieces, place_ref, (out_ref, weight_ref) = refs[:8], refs[8], refs[-2:]
    triple = own_ref.shape[1]

    @pl.when(pl.program_id(0) == 0)
    def _():
        fill(weight_ref, 0, pieces[:4], 0, triple)
        fill(weight_ref, triple, pieces[4:], 0, triple)

    grads = d_summed_ref[...] + dot_nt(side(own_ref[...], other_ref[...]), weight_ref[...])
    high = grads.astype(bf16)
    low = (grads - high.astype(f32)).astype(bf16)
    out_ref[...] = dot_nt(high, place_ref[...]) + dot_nt(low, place_ref[...])


def d_inputs(d_summed, own, other, w_own, w_other, place, half, earlier=()):
    rows, model = d_summed.shape
    part, triple = w_own[0].shape[0], own.shape[1]
    steps = rows // 2 // TILE

    def tile(width):
        return pl.BlockSpec((TILE, width), lambda i: (i + half * steps, 0))

    def fixed(shape):
        return pl.BlockSpec(shape, lambda i: (0, 0), pipeline_mode=pl.Buffered(1))

    args = (d_summed, own, other, *w_own, *w_other, place)
    return pl.pallas_call(
        d_inputs_kernel,
        grid=(steps,),
        in_specs=[tile(model), tile(triple), tile(triple)]
        + [fixed((part, triple))] * 8
        + [fixed(place.shape)]
        + [pl.BlockSpec(memory_space=pl.ANY)] * len(earlier),
        out_specs=tile(model),
        out_shape=jax.ShapeDtypeStruct((rows, model), f32),
        scratch_shapes=[pltpu.VMEM((model, 2 * triple), bf16)],
        input_output_aliases={len(args): 0} if earlier else {},
        compiler_params=pltpu.CompilerParams(vmem_limit_bytes=18 << 20),
        cost_estimate=cost(COST["d_inputs"]),
        name="d_inputs",
    )(*args, *earlier)


def chunks(width):
    step = next(step for step in (512, 384, 256, 128) if width % step == 0)
    return [(start, step) for start in range(0, width, step)]


def send_kernel(left_ref, *refs):
    *rights, out_ref = refs
    half = left_ref.shape[1] // 2
    left = left_ref[:, half:]
    base = 0
    for right_ref in rights:
        for start, step in chunks(right_ref.shape[1]):
            part = dot_tn(left, right_ref[:, start : start + step])
            out_ref[:, base + start : base + start + step] = part.astype(bf16)
        base += right_ref.shape[1]


def send_grads(left, *rights):
    outs = [((left.shape[1] // 2, sum(right.shape[1] for right in rights)), bf16)]
    return in_vmem(send_kernel, "send_grads", 5, outs, left, *rights)[0]


def keep_kernel(terms, *refs):
    for left_at, right_at, adds, upper, lower in terms:
        left_ref, right_ref = refs[left_at], refs[right_at]
        half = left_ref.shape[1] // 2
        left = left_ref[:, :half]
        for start, step in chunks(right_ref.shape[1]):
            total = dot_tn(left, right_ref[:, start : start + step])
            for add_at, column in adds:
                total = total + refs[add_at][:, column + start : column + start + step].astype(f32)
            for part, places in ((total[: half // 2], upper), (total[half // 2 :], lower)):
                for first, last, out_at, row, column in places:
                    if first <= start < last:
                        out_ref = refs[out_at]
                        to = column + start - first
                        out_ref[row : row + half // 2, to : to + step] = part.astype(out_ref.dtype)


def keep_grads(args, terms, outs):
    return in_vmem(functools.partial(keep_kernel, terms), "keep_grads", 8, outs, *args)


class Exchange:
    def __init__(self, fsdp):
        self.fsdp = fsdp
        bits = [1 << i for i in range(2, fsdp.bit_length() - 1)]
        self.bits, self.far = bits, []
        for i in range(0, len(bits), 2):
            steps = [0]
            for bit in bits[i : i + 2]:
                steps = steps + [step ^ bit for step in steps]
            self.far.append(steps)
        self.masks = [0]
        for steps in self.far + [[0, 2], [0, 1]]:
            self.masks = [step ^ mask for step in steps for mask in self.masks]

    def flip(self, array, bit):
        return lax.ppermute(array, "fsdp", [(i, i ^ bit) for i in range(self.fsdp)])

    def cross(self, array):
        return lax.ppermute(array, "tp", [(0, 1), (1, 0)])

    def flip_cross(self, array, bit):
        pairs = [(2 * i + j, 2 * (i ^ bit) + 1 - j) for i in range(self.fsdp) for j in range(2)]
        return lax.ppermute(array, ("fsdp", "tp"), pairs)

    def gather_far(self, array):
        for steps in self.far[:-1]:
            array = join([array] + [self.flip(array, step) for step in steps[1:]])
        return [array] + [self.flip(array, step) for step in self.far[-1][1:]]

    def scatter_far(self, array):
        for steps in reversed(self.far):
            size = array.shape[0] // len(steps)
            parts = [array[i * size : (i + 1) * size] for i in range(len(steps))]
            array = parts[0]
            for part, step in zip(parts[1:], steps[1:]):
                array = array + self.flip(part.astype(bf16), step).astype(f32)
        return array

    def halve(self, parts, bit):
        away = self.flip(jnp.concatenate(parts[1::2], axis=0).astype(bf16), bit)
        size = parts[0].shape[0]
        return parts[::2], [away[at : at + size] for at in range(0, away.shape[0], size)]

    def halve_first(self, array):
        size = array.shape[0] >> len(self.bits)
        return self.halve([array[at : at + size] for at in range(0, array.shape[0], size)], self.bits[0])

    def halve_rest(self, keep, away):
        for bit in self.bits[1:]:
            keep, away = self.halve([mine + theirs.astype(f32) for mine, theirs in zip(keep, away)], bit)
        return keep[0] + away[0].astype(f32)

    def total_far(self, array):
        for steps in reversed(self.far):
            parts = [array] + [self.flip(array, step) for step in steps[1:]]
            while len(parts) > 1:
                parts = [parts[i] + parts[i + 1] for i in range(0, len(parts), 2)]
            array = parts[0]
        return array


def gate(values, *others):
    return lax.optimization_barrier((values, others))[0]


def shards(
    tokens,
    lengths,
    cotangent,
    w_query,
    w_key,
    w_value,
    w_output,
    w_inner,
    w_outer,
    bias_query,
    bias_value,
    bias_output,
    norm1_gain,
    norm1_bias,
    bias_inner,
    bias_outer,
    norm2_gain,
    norm2_bias,
):
    fsdp = lax.axis_size("fsdp")
    exchange = Exchange(fsdp)
    rows, model = tokens.shape
    seqs = rows // SEQ
    block = w_query.shape[0]
    width = w_query.shape[1]
    half = model // 2

    here = lax.axis_index("fsdp")
    masks = jnp.repeat(jnp.asarray(exchange.masks, jnp.int32), block)
    inside = jnp.tile(jnp.arange(block, dtype=jnp.int32), fsdp)
    source = (here ^ masks) * block + inside
    place = jnp.arange(model, dtype=jnp.int32)[:, None] == source[None, :]
    place16 = place.astype(bf16)
    place32 = place.astype(f32)
    lengths_here = lax.dynamic_slice_in_dim(lengths, lax.axis_index("tp") * seqs, seqs, 0)

    def permuted(vectors, dims):
        return lax.dot_general(
            vectors, place32, ((dims), ((), ())), precision=lax.Precision.HIGHEST, preferred_element_type=f32
        )

    zero = jnp.zeros((width,), f32)

    def qkv_bias(biases):
        return jnp.concatenate([biases[:width], zero, biases[width : 2 * width]])

    def inner_bias(biases):
        return biases[2 * width :]

    flip, cross, flip_cross = exchange.flip, exchange.cross, exchange.flip_cross

    shard_attn = jnp.concatenate([w_query, w_key, w_value, w_output.T], axis=1).astype(bf16)
    biases_own = jnp.concatenate([bias_query, bias_value, bias_inner])
    far_attn = exchange.gather_far(shard_attn)
    biases_other = cross(biases_own)
    inputs = dot_nn(tokens, place16).astype(bf16)
    shard_inner, shard_outer = w_inner.astype(bf16), w_outer.T.astype(bf16)
    vectors = jnp.stack([bias_output, norm1_gain, norm1_bias, bias_outer, norm2_gain, norm2_bias])

    far_attn, shard_inner, shard_outer, biases_other, cotangent, vectors, inputs = gate(
        (far_attn, shard_inner, shard_outer, biases_other, cotangent, vectors, inputs)
    )
    far_attn = join(far_attn)
    near_attn, across_attn = flip(far_attn, 2), cross(far_attn)
    far_inner = exchange.gather_far(shard_inner)
    cotan = dot_nn(cotangent, place16).astype(bf16)
    vectors = permuted(vectors, ((1,), (0,)))

    far_attn, near_attn, across_attn, far_inner, shard_outer, inputs = gate(
        (far_attn, near_attn, across_attn, far_inner, shard_outer, inputs), cotan, vectors
    )
    pair_far_attn, pair_near_attn, corner_attn = flip(far_attn, 1), flip(near_attn, 1), cross(near_attn)
    far_inner = join(far_inner)
    near_inner = flip(far_inner, 2)
    far_outer = exchange.gather_far(shard_outer)
    attn_own = (far_attn, near_attn, pair_far_attn, pair_near_attn)
    proj_own, context_own, lse_own = attend_forward(inputs, attn_own, qkv_bias(biases_own), lengths_here)

    across_attn, corner_attn, far_inner, near_inner, far_outer, context_own = gate(
        (across_attn, corner_attn, far_inner, near_inner, far_outer, context_own)
    )
    pair_across_attn, pair_corner_attn = flip(across_attn, 1), flip(corner_attn, 1)
    across_inner = cross(far_inner)
    far_outer = join(far_outer)
    near_outer = flip(far_outer, 2)
    attn_other = (across_attn, corner_attn, pair_across_attn, pair_corner_attn)
    proj_other, context_other, lse_other = attend_forward(inputs, attn_other, qkv_bias(biases_other), lengths_here)

    far_inner, near_inner, across_inner, far_outer, near_outer, context_other = gate(
        (far_inner, near_inner, across_inner, far_outer, near_outer, context_other)
    )
    pair_far_inner, pair_near_inner = flip(far_inner, 1), flip(near_inner, 1)
    corner_inner = flip(across_inner, 2)
    across_outer = cross(far_outer)
    normal_one, scale_one, normed16 = attention_out(context_own, context_other, attn_own, attn_other, inputs, vectors)
    inner_own = (far_inner, near_inner, pair_far_inner, pair_near_inner)
    hidden_own, slope_own = hidden_parts(normed16, inner_own, inner_bias(biases_own))

    across_inner, corner_inner, far_outer, near_outer, across_outer, normed16, hidden_own = gate(
        (across_inner, corner_inner, far_outer, near_outer, across_outer, normed16, hidden_own)
    )
    corner_outer = cross(near_outer)
    pair_across_inner, pair_corner_inner = flip(across_inner, 1), flip(corner_inner, 1)
    pair_far_outer, pair_near_outer = flip(far_outer, 1), flip(near_outer, 1)
    inner_other = (across_inner, corner_inner, pair_across_inner, pair_corner_inner)
    hidden_other, slope_other = hidden_parts(normed16, inner_other, inner_bias(biases_other))

    across_outer, corner_outer, hidden_other = gate((across_outer, corner_outer, hidden_other))
    pair_across_outer, pair_corner_outer = flip(across_outer, 1), flip(corner_outer, 1)
    outer_own = (far_outer, near_outer, pair_far_outer, pair_near_outer)
    outer_other = (across_outer, corner_outer, pair_across_outer, pair_corner_outer)

    mixed, d_before, d_ffn, sums_two = turn(
        hidden_own, hidden_other, outer_own, outer_other, normal_one, cotan, vectors, place16
    )
    upper = model // 4
    inner_width = bias_inner.shape[0]

    def received(array):
        return array.astype(f32)

    send_outer = send_grads(d_ffn, hidden_own, hidden_other)

    send_outer, d_ffn = gate((send_outer, d_ffn))
    pair_outer = flip(send_outer, 1)
    d_inner_own, inner_sums_own = d_hidden(d_ffn, outer_own, slope_own)

    pair_outer, d_ffn, d_inner_own = gate((pair_outer, d_ffn, d_inner_own))
    part = (upper, inner_width)
    keep_outer, *away_outer = keep_grads(
        (d_ffn, hidden_own, hidden_other, pair_outer),
        (
            (0, 1, ((3, 0),), ((0, inner_width, 4, 0, 0),), ((0, inner_width, 5, 0, 0),)),
            (0, 2, ((3, inner_width),), ((0, inner_width, 6, 0, 0),), ((0, inner_width, 7, 0, 0),)),
        ),
        [(part, f32), (part, bf16), (part, bf16), (part, bf16)],
    )

    keep_outer, away_outer, d_ffn = gate((keep_outer, away_outer, d_ffn))
    ring_outer = (flip(away_outer[0], 2), cross(away_outer[1]), flip_cross(away_outer[2], 2))
    d_inner_other, inner_sums_other = d_hidden(d_ffn, outer_other, slope_other)
    send_inner = send_grads(normed16, d_inner_own, d_inner_other)

    send_inner, d_inner_other, normed16 = gate((send_inner, d_inner_other, normed16))
    pair_inner = flip(send_inner, 1)
    d_summed, d_attn, sums_one = d_attention(
        d_inner_own, d_inner_other, inner_own, inner_other, d_before, normal_one, scale_one, vectors
    )
    send_output = send_grads(d_attn, context_own, context_other)

    send_output, d_attn = gate((send_output, d_attn))
    pair_output = flip(send_output, 1)
    d_context_own, d_context_other = d_context(d_attn, attn_own, attn_other)

    pair_output, pair_inner, d_attn, normed16, d_context_other = gate(
        (pair_output, pair_inner, d_attn, normed16, d_context_other)
    )
    cut = 2 * inner_width // 3
    late = inner_width - cut
    rest = late + width
    args = (normed16, d_attn, d_inner_own, d_inner_other, context_own, context_other, pair_inner, pair_output)
    own_cut, own_low, other_cut, own_rest, other_rest, near_rest = range(8, 14)
    first_keep, first_low, first_away, last_keep, last_cross, last_away = keep_grads(
        args,
        (
            (
                0,
                2,
                ((6, 0),),
                ((0, cut, own_cut, 0, 0), (cut, inner_width, own_rest, 0, 0)),
                ((0, cut, own_low, 0, 0), (cut, inner_width, near_rest, 0, 0)),
            ),
            (
                0,
                3,
                ((6, inner_width),),
                ((0, cut, other_cut, 0, 0), (cut, inner_width, other_rest, 0, 0)),
                ((0, cut, other_cut, upper, 0), (cut, inner_width, near_rest, 0, rest)),
            ),
            (1, 4, ((7, 0),), ((0, width, own_rest, 0, late),), ((0, width, near_rest, 0, late),)),
            (1, 5, ((7, width),), ((0, width, other_rest, 0, late),), ((0, width, near_rest, 0, rest + late),)),
        ),
        [
            ((upper, cut), f32),
            ((upper, cut), f32),
            ((2 * upper, cut), bf16),
            ((upper, rest), f32),
            ((upper, rest), f32),
            ((upper, 2 * rest), bf16),
        ],
    )

    first_keep, first_low, first_away, last_keep, last_cross, last_away, d_context_other, keep_outer, ring_outer = gate(
        (first_keep, first_low, first_away, last_keep, last_cross, last_away, d_context_other, keep_outer, ring_outer)
    )
    first_across, last_near = cross(first_away), flip(last_away, 2)
    for piece in ring_outer:
        keep_outer = keep_outer + received(piece)
    keep_outer, lower_outer = exchange.halve_first(keep_outer)
    d_proj_other, qkv_sums_other = attend_backward(
        proj_other, context_other, d_context_other, lse_other, lengths_here
    )
    send_other = send_grads(inputs, d_proj_other)

    send_other, d_proj_other, first_across, last_near, keep_outer, lower_outer = gate(
        (send_other, d_proj_other, first_across, last_near, keep_outer, lower_outer)
    )
    pair_other = flip(send_other, 1)
    first_near = flip((first_low + received(first_across[upper:])).astype(bf16), 2)
    last_across = cross((last_cross + received(last_near[:, rest:])).astype(bf16))
    sum_outer = exchange.halve_rest(keep_outer, lower_outer)

    pair_other, d_proj_other = gate((pair_other, d_proj_other))
    triple = 3 * width
    (away_other,) = keep_grads(
        (inputs, d_proj_other, pair_other),
        ((0, 1, ((2, 0),), ((0, triple, 3, 0, 0),), ((0, triple, 3, upper, 0),)),),
        [((2 * upper, triple), bf16)],
    )

    away_other, d_context_own, qkv_sums_other, first_near, last_across, sum_outer = gate(
        (away_other, d_context_own, qkv_sums_other, first_near, last_across, sum_outer)
    )
    across_qkv = cross(away_other)
    whole = permuted(jnp.concatenate([sums_one[:3], sums_two[:3]]), ((1,), (1,))).reshape(-1)
    across_small = cross(jnp.concatenate([qkv_sums_other[0], qkv_sums_other[1], inner_sums_other[0], whole]))
    first_keep = first_keep + received(first_across[:upper]) + received(first_near)
    last_keep = last_keep + received(last_near[:, :rest]) + received(last_across)
    keep_mid, lower_mid = exchange.halve_first(jnp.concatenate([first_keep, last_keep], axis=1))
    d_proj_own, qkv_sums_own = attend_backward(proj_own, context_own, d_context_own, lse_own, lengths_here)
    send_own = send_grads(inputs, d_proj_own)
    early = d_inputs(d_summed, d_proj_own, d_proj_other, attn_own, attn_other, place16, 0)

    send_own, d_proj_own, qkv_sums_own, across_small, across_qkv, early, keep_mid, lower_mid = gate(
        (send_own, d_proj_own, qkv_sums_own, across_small, across_qkv, early, keep_mid, lower_mid)
    )
    pair_own = flip(send_own, 1)
    small = jnp.concatenate([qkv_sums_own[0], qkv_sums_own[1], inner_sums_own[0], whole]) + across_small
    pair_small = flip(small, 1)
    sum_mid = exchange.halve_rest(keep_mid, lower_mid)

    pair_own, d_proj_own, small, pair_small = gate((pair_own, d_proj_own, small, pair_small))
    small = small + pair_small
    near_small = flip(small, 2)
    keep_qkv, away_qkv = keep_grads(
        (inputs, d_proj_own, pair_own, across_qkv),
        ((0, 1, ((2, 0), (3, 0)), ((0, triple, 4, 0, 0),), ((0, triple, 5, 0, 0),)),),
        [((upper, triple), f32), ((upper, triple), bf16)],
    )

    keep_qkv, away_qkv, small, near_small, early = gate((keep_qkv, away_qkv, small, near_small, early))
    near_qkv = flip(away_qkv, 2)
    small = exchange.total_far(small + near_small)
    grad_tokens = d_inputs(d_summed, d_proj_own, d_proj_other, attn_own, attn_other, place16, 1, (early,))

    keep_qkv, near_qkv, small, grad_tokens, sum_mid = gate((keep_qkv, near_qkv, small, grad_tokens, sum_mid))
    sum_qkv = exchange.scatter_far(keep_qkv + received(near_qkv))

    inner_width = bias_inner.shape[0]
    cuts = np.cumsum([width, width, inner_width] + [model] * 6)
    query_bias, value_bias, inner_bias_sum, *rest = jnp.split(small, cuts[:-1])

    return (
        mixed,
        grad_tokens,
        sum_qkv[:, :width],
        sum_qkv[:, width : 2 * width],
        sum_qkv[:, 2 * width :],
        sum_mid[:, inner_width:].T,
        sum_mid[:, :inner_width],
        sum_outer.T,
        query_bias,
        value_bias,
        rest[0],
        rest[1],
        rest[2],
        inner_bias_sum,
        rest[3],
        rest[4],
        rest[5],
    )


def solution(mesh):
    both = P(("fsdp", "tp"), None)
    cols, rows = P("fsdp", "tp"), P("tp", "fsdp")
    return jax.shard_map(
        shards,
        mesh=mesh,
        in_specs=(both, P("fsdp"), both, cols, cols, cols, rows, cols, rows)
        + (P("tp"), P("tp"), P(), P(), P(), P("tp"), P(), P(), P()),
        out_specs=(both, both, cols, cols, cols, rows, cols, rows)
        + (P("tp"), P("tp"), P(), P(), P(), P("tp"), P(), P(), P()),
        check_vma=False,
    )
```

time: 310 us -> 276 us (0.89)
  starting transfers between devices: 68.1 us -> 52.7 us
  local copies, waits for them, and re-layouts: 24.9 us -> 14.6 us
  waiting for transfers between devices: 52 us -> 47.3 us
  other arithmetic: 14.1 us -> 9.95 us
    pallas_call x0 -> x2, Pallas kernels: none -> 16.3 us  [d_inputs(): pl.pallas_call(d_inputs_kernel, grid=(steps,), in_specs=[tile(model), til...]
    ppermute x7 -> x1, waiting for transfers between devices: 11.8 us -> 0.01 us  [flip_cross(): return lax.ppermute(array, ('fsdp', 'tp'), pairs)]
    pallas_call x18 -> x20, Pallas kernels: 87.6 us -> 76 us  [in_vmem(): pl.pallas_call(kernel, in_specs=[pl.BlockSpec(memory_space=pltpu.VMEM)] *...]
    ppermute x47 -> x46, waiting for transfers between devices: 27.7 us -> 38.2 us  [flip(): return lax.ppermute(array, 'fsdp', [(i, i ^ bit) for i in range(self.fsdp)])]
    ppermute x7 -> x1, starting transfers between devices: 11 us -> 2.2 us  [flip_cross(): return lax.ppermute(array, ('fsdp', 'tp'), pairs)]
    ppermute x47 -> x46, starting transfers between devices: 47.1 us -> 39.3 us  [flip(): return lax.ppermute(array, 'fsdp', [(i, i ^ bit) for i in range(self.fsdp)])]
    unnamed x119 -> x110, local copies, waits for them, and re-layouts: 16.7 us -> 10.2 us
    concatenate x9 -> x0, local copies, waits for them, and re-layouts: 4.05 us -> none  [join(): return jnp.concatenate(arrays, axis=0)]
  transfers between devices with their start and end apart: 63 -> 58, of which waited for: 20 -> 22; matrix products, arithmetic and copies ran while one was open for 10% -> 5% of each run, Pallas kernels for 36% -> 43%
where the time goes in v3:
time: 276 us; the launch traced here: 271 us
  Pallas kernels  138 us (50%)
  starting transfers between devices  52.7 us (19%)
  waiting for transfers between devices  47.3 us (17%)
  local copies, waits for them, and re-layouts  14.6 us (5%)
  other arithmetic  9.95 us (4%)
  matrix products  6.25 us (2%)
    pallas_call x20, Pallas kernels, in_vmem(): pl.pallas_call(kernel, in_specs=[pl.BlockSpec(memory_space=pltpu.VMEM)] *...  76 us
    ppermute x46, starting transfers between devices, flip(): return lax.ppermute(array, 'fsdp', [(i, i ^ bit) for i in range(self.fsdp)])  39.3 us
    ppermute x46, waiting for transfers between devices, flip(): return lax.ppermute(array, 'fsdp', [(i, i ^ bit) for i in range(self.fsdp)])  38.2 us
    pallas_call x2, Pallas kernels, attend_forward(): pl.pallas_call(functools.partial(attend_forward_kernel, pairs), grid_spec...  24.4 us
    pallas_call x2, Pallas kernels, attend_backward(): pl.pallas_call(functools.partial(attend_backward_kernel, pairs), grid_spe...  21.2 us
    pallas_call x2, Pallas kernels, d_inputs(): pl.pallas_call(d_inputs_kernel, grid=(steps,), in_specs=[tile(model), til...  16.3 us
    ppermute x11, starting transfers between devices, cross(): return lax.ppermute(array, 'tp', [(0, 1), (1, 0)])  11.2 us
    unnamed x110, local copies, waits for them, and re-layouts  10.2 us
  transfers between devices with their start and end apart: 58, of which 22 were waited for; matrix products, arithmetic and copies ran while one was open for 5% of the time, Pallas kernels for 43%

profile of v3, /device:TPU:0, one launch (start us, length us, event | category | flops | bytes accessed | tf_op | source)
XLA Modules:
  0.0 270.7 jit_solution(5611588892708041400)
XLA Ops:
  4.4 5.1 %collective-permute-start.2 = (bf16[48,1536]{1,0:T(8,128)(2,1)S(1)}, bf16[48,1536]{1,0:T(8,128)(2,1)}, u32[]{:S(2)}, u32[]{:S(2)}) collective-permute-start(bf16[48,1536]{1,0:T(8,128)(2,1)S(1)} %pad_maximum_fusion.3.refs_0_), channel_id=1, source_target_pairs={{0,24},{2,26},{4,28},{6,30},{8,16},{10,18},{12,20},{14,22},{16,8},... | collective-permute-start | bytes 442376 | tf_op jit(solution)/shard_map/ppermute | solution.py:525
  16.1 6.0 %collective-permute-done.1.refs_2_ = bf16[48,1536]{1,0:T(8,128)(2,1)} collective-permute-done((bf16[48,1536]{1,0:T(8,128)(2,1)S(1)}, bf16[48,1536]{1,0:T(8,128)(2,1)}, u32[]{:S(2)}, u32[]{:S(2)}) %collective-permute-start.1) | collective-permute-done | bytes 147488 | tf_op jit(solution)/shard_map/ppermute | solution.py:525
  26.4 2.5 collective-permute-start.8
  30.8 2.9 %fusion.6.refs_9_ = bf16[1024,768]{1,0:T(8,128)(2,1)S(1)} fusion(bf16[1024,768]{1,0:T(8,128)(2,1)} %param.21, s32[768]{0:T(1024)S(1)} %add.89), kind=kOutput, calls=%fused_computation.12 | convolution fusion | flops 1209335808 | bytes 3148800 | tf_op jit(solution)/shard_map/dot_general | solution.py:40
  34.9 5.1 %collective-permute-done.7.refs_2_ = bf16[48,1536]{1,0:T(8,128)(2,1)S(1)} collective-permute-done((bf16[48,1536]{1,0:T(8,128)(2,1)S(1)}, bf16[48,1536]{1,0:T(8,128)(2,1)S(1)}, u32[]{:S(2)}, u32[]{:S(2)}) %collective-permute-start.7) | collective-permute-done | bytes 147488 | tf_op jit(solution)/shard_map/ppermute | solution.py:525
  42.2 2.9 %collective-permute-start.11 = (bf16[48,1536]{1,0:T(8,128)(2,1)S(1)}, bf16[48,1536]{1,0:T(8,128)(2,1)S(1)}, u32[]{:S(2)}, u32[]{:S(2)}) collective-permute-start(bf16[48,1536]{1,0:T(8,128)(2,1)S(1)} %convert_bitcast_fusion.refs_0_), channel_id=1, source_target_pairs={{0,8},{2,10},{4,12},{6,14},{8,0},{10,2},{12,4},{14,6},{16,24},{18,... | collective-permute-start | bytes 442376 | tf_op jit(solution)/shard_map/ppermute | solution.py:525
  46.3 12.8 %attend_forward.2 = (bf16[1024,1152]{1,0:T(8,128)(2,1)S(1)}, bf16[1024,384]{1,0:T(8,128)(2,1)S(1)}, f32[2,6,512]{2,1,0:T(8,128)S(1)}) custom-call(s32[2]{0:T(128)S(1)} %dynamic_slice.3.lengths_ref, bf16[1024,768]{1,0:T(8,128)(2,1)S(1)} %fusion.7.inputs_ref.refs_8_.left_ref.refs_0_, bf16[192,1536]{1,0:T(8,128)(2,1)S(1)} %join.3.a_ref.refs_0_, ...), custom_call_target="tpu_custom_call" | custom-call | flops 35100000256 | bytes 1024 | tf_op jit(solution)/shard_map/attend_forward/pallas_call | solution.py:146
  63.6 11.7 %attend_forward.3 = (bf16[1024,1152]{1,0:T(8,128)(2,1)S(1)}, bf16[1024,384]{1,0:T(8,128)(2,1)S(1)}, f32[2,6,512]{2,1,0:T(8,128)S(1)}) custom-call(s32[2]{0:T(128)S(1)} %dynamic_slice.3.lengths_ref, bf16[1024,768]{1,0:T(8,128)(2,1)S(1)} %fusion.7.inputs_ref.refs_8_.left_ref.refs_0_, bf16[192,1536]{1,0:T(8,128)(2,1)S(1)} %collective-permute-done.5.a_ref.refs_4_, ...), custom_call_target="tpu_custom_call" | custom-call | flops 35100000256 | bytes 1024 | tf_op jit(solution)/shard_map/attend_forward/pallas_call | solution.py:146
  79.8 4.6 %attention_out.1 = (f32[1024,768]{1,0:T(8,128)S(1)}, f32[1024,1]{1,0:T(8,128)S(1)}, bf16[1024,768]{1,0:T(8,128)(2,1)S(1)}) custom-call(bf16[1024,384]{1,0:T(8,128)(2,1)S(1)} %get-tuple-element.206.own_ref.refs_0_.refs_4_.context_ref, bf16[1024,384]{1,0:T(8,128)(2,1)S(1)} %get-tuple-element.207.other_ref.refs_1_.refs_5_.context_ref, ...), custom_call_target="tpu_custom_call" | custom-call | flops 10800000000 | bytes 1024 | tf_op jit(solution)/shard_map/attention_out/pallas_call | solution.py:242
  84.4 8.0 %hidden.2 = (bf16[1024,1536]{1,0:T(8,128)(2,1)S(1)}, bf16[1024,1536]{1,0:T(8,128)(2,1)S(1)}) custom-call(bf16[1024,768]{1,0:T(8,128)(2,1)S(1)} %get-tuple-element.251.normed_ref.left_ref.refs_0_, bf16[192,1536]{1,0:T(8,128)(2,1)S(1)} %join.4.refs_0_, bf16[192,1536]{1,0:T(8,128)(2,1)S(1)} %collective-permute-done.10.refs_1_, ...), custom_call_target="tpu_custom_call" | custom-call | flops 22950000640 | bytes 1024 | tf_op jit(solution)/shard_map/hidden/pallas_call | solution.py:242
  95.4 8.0 %hidden.3 = (bf16[1024,1536]{1,0:T(8,128)(2,1)S(1)}, bf16[1024,1536]{1,0:T(8,128)(2,1)S(1)}) custom-call(bf16[1024,768]{1,0:T(8,128)(2,1)S(1)} %get-tuple-element.251.normed_ref.left_ref.refs_0_, bf16[192,1536]{1,0:T(8,128)(2,1)S(1)} %collective-permute-done.16.refs_0_.refs_4_, bf16[192,1536]{1,0:T(8,128)(2,1)S(1)} %collective-permute-done.20.refs_1_.refs_5_, ...), custom_call_target="tpu_custom_call" | custom-call | flops 22950000640 | bytes 1024 | tf_op jit(solution)/shard_map/hidden/pallas_call | solution.py:242
  103.3 5.5 %collective-permute-done.24.refs_5_.refs_1_ = bf16[192,1536]{1,0:T(8,128)(2,1)S(1)} collective-permute-done((bf16[192,1536]{1,0:T(8,128)(2,1)S(1)}, bf16[192,1536]{1,0:T(8,128)(2,1)S(1)}, u32[]{:S(2)}, u32[]{:S(2)}) %collective-permute-start.24) | collective-permute-done | bytes 589856 | tf_op jit(solution)/shard_map/ppermute | solution.py:528
  111.7 13.7 %turn.1 = (bf16[1024,768]{1,0:T(8,128)(2,1)}, f32[1024,768]{1,0:T(8,128)S(1)}, bf16[1024,768]{1,0:T(8,128)(2,1)S(1)}, f32[8,768]{1,0:T(8,128)S(1)}) custom-call(bf16[1024,1536]{1,0:T(8,128)(2,1)S(1)} %get-tuple-element.212.own_ref.refs_0_.refs_1_, bf16[1024,1536]{1,0:T(8,128)(2,1)S(1)} %get-tuple-element.219.other_ref.refs_1_.refs_2_, ...), custom_call_target="tpu_custom_call" | custom-call | flops 35100000256 | bytes 1024 | tf_op jit(solution)/shard_map/turn/pallas_call | solution.py:242
  125.3 2.6 send_grads.5
  128.2 3.6 %d_hidden.2 = (bf16[1024,1536]{1,0:T(8,128)(2,1)S(1)}, f32[8,1536]{1,0:T(8,128)S(1)}) custom-call(bf16[1024,768]{1,0:T(8,128)(2,1)S(1)} %get-tuple-element.239.left_ref.d_ffn_ref.refs_0_, bf16[192,1536]{1,0:T(8,128)(2,1)S(1)} %join.5.refs_0_, bf16[192,1536]{1,0:T(8,128)(2,1)S(1)} %collective-permute-done.17.refs_1_, ...), custom_call_target="tpu_custom_call" | custom-call | flops 9720000512 | bytes 1024 | tf_op jit(solution)/shard_map/d_hidden/pallas_call | solution.py:242
  132.6 3.6 %keep_grads.4 = (f32[192,1536]{1,0:T(8,128)S(1)}, bf16[192,1536]{1,0:T(8,128)(2,1)}, bf16[192,1536]{1,0:T(8,128)(2,1)}, bf16[192,1536]{1,0:T(8,128)(2,1)}) custom-call(bf16[1024,768]{1,0:T(8,128)(2,1)S(1)} %get-tuple-element.239.left_ref.d_ffn_ref.refs_0_, bf16[1024,1536]{1,0:T(8,128)(2,1)S(1)} %get-tuple-element.212.own_ref.refs_0_.refs_1_, ...), custom_call_target="tpu_custom_call" | custom-call | flops 9450000384 | bytes 1024 | tf_op jit(solution)/shard_map/keep_grads/pallas_call | solution.py:242
  138.5 2.2 collective-permute-start.36
  140.7 3.6 %d_hidden.3 = (bf16[1024,1536]{1,0:T(8,128)(2,1)S(1)}, f32[8,1536]{1,0:T(8,128)S(1)}) custom-call(bf16[1024,768]{1,0:T(8,128)(2,1)S(1)} %get-tuple-element.239.left_ref.d_ffn_ref.refs_0_, bf16[192,1536]{1,0:T(8,128)(2,1)S(1)} %collective-permute-done.21.refs_4_.refs_0_, bf16[192,1536]{1,0:T(8,128)(2,1)S(1)} %collective-permute-done.24.refs_5_.refs_1_, ...), custom_call_target="tpu_custom_call" | custom-call | flops 9720000512 | bytes 1024 | tf_op jit(solution)/shard_map/d_hidden/pallas_call | solution.py:242
  144.3 4.1 %send_grads.6 = bf16[384,3072]{1,0:T(8,128)(2,1)} custom-call(bf16[1024,768]{1,0:T(8,128)(2,1)S(1)} %get-tuple-element.251.normed_ref.left_ref.refs_0_, bf16[1024,1536]{1,0:T(8,128)(2,1)S(1)} %get-tuple-element.232.refs_0_.own_ref.refs_2_, bf16[1024,1536]{1,0:T(8,128)(2,1)S(1)} %get-tuple-element.242.refs_1_.other_ref.refs_3_), custom_call_target="tpu_custom_call" | custom-call | flops 18000000 | bytes 1024 | tf_op jit(solution)/shard_map/send_grads/pallas_call | solution.py:242
  148.4 7.4 %d_attention.1 = (f32[1024,768]{1,0:T(8,128)S(1)}, bf16[1024,768]{1,0:T(8,128)(2,1)S(1)}, f32[8,768]{1,0:T(8,128)S(1)}) custom-call(bf16[1024,1536]{1,0:T(8,128)(2,1)S(1)} %get-tuple-element.232.refs_0_.own_ref.refs_2_, bf16[1024,1536]{1,0:T(8,128)(2,1)S(1)} %get-tuple-element.242.refs_1_.other_ref.refs_3_, bf16[192,1536]{1,0:T(8,128)(2,1)S(1)} %join.4.refs_0_, ...), custom_call_target="tpu_custom_call" | custom-call | flops 27000000512 | bytes 1024 | tf_op jit(solution)/shard_map/d_attention/pallas_call | solution.py:242
  166.3 3.8 %d_context.1 = (bf16[1024,384]{1,0:T(8,128)(2,1)S(1)}, bf16[1024,384]{1,0:T(8,128)(2,1)S(1)}) custom-call(bf16[1024,768]{1,0:T(8,128)(2,1)S(1)} %copy-done.39, bf16[192,1536]{1,0:T(8,128)(2,1)S(1)} %copy-done.17, bf16[192,1536]{1,0:T(8,128)(2,1)} %collective-permute-done.4.b_ref.refs_1_, bf16[192,1536]{1,0:T(8,128)(2,1)S(1)} %copy-done.21, ...), custom_call_target="tpu_custom_call" | custom-call | flops 5400000000 | bytes 1024 | tf_op jit(solution)/shard_map/d_context/pallas_call | solution.py:242
  170.2 5.2 %keep_grads.5 = (f32[192,1024]{1,0:T(8,128)S(1)}, f32[192,1024]{1,0:T(8,128)S(1)}, bf16[384,1024]{1,0:T(8,128)(2,1)S(1)}, f32[192,896]{1,0:T(8,128)S(1)}, f32[19...) custom-call(bf16[1024,768]{1,0:T(8,128)(2,1)S(1)} %copy-done.36, bf16[1024,768]{1,0:T(8,128)(2,1)S(1)} %copy-done.39, ...), custom_call_target="tpu_custom_call" | custom-call | flops 9450000384 | bytes 1024 | tf_op jit(solution)/shard_map/keep_grads/pallas_call | solution.py:242
  180.2 10.6 %attend_backward.2 = (bf16[1024,1152]{1,0:T(8,128)(2,1)S(1)}, f32[8,384]{1,0:T(8,128)S(1)}) custom-call(s32[2]{0:T(128)S(1)} %copy-done.43, bf16[1024,1152]{1,0:T(8,128)(2,1)S(1)} %copy-done.34, bf16[1024,384]{1,0:T(8,128)(2,1)S(1)} %copy-done.11, bf16[1024,384]{1,0:T(8,128)(2,1)S(1)} %get-tuple-element.266.d_context_ref, ...), custom_call_target="tpu_custom_call" | custom-call | flops 18000000 | bytes 1024 | tf_op jit(solution)/shard_map/attend_backward/pallas_call | solution.py:218
  193.4 2.6 collective-permute-done.37
  198.5 6.3 %collective-permute-done.43 = bf16[48,1536]{1,0:T(8,128)(2,1)S(1)} collective-permute-done((bf16[48,1536]{1,0:T(8,128)(2,1)S(1)}, bf16[48,1536]{1,0:T(8,128)(2,1)S(1)}, u32[]{:S(2)}, u32[]{:S(2)}) %collective-permute-start.43) | collective-permute-done | bytes 147488 | tf_op jit(solution)/shard_map/ppermute | solution.py:525
  213.2 10.6 %attend_backward.3 = (bf16[1024,1152]{1,0:T(8,128)(2,1)S(1)}, f32[8,384]{1,0:T(8,128)S(1)}) custom-call(s32[2]{0:T(128)S(1)} %copy-done.43, bf16[1024,1152]{1,0:T(8,128)(2,1)S(1)} %copy-done.32, bf16[1024,384]{1,0:T(8,128)(2,1)S(1)} %copy-done.8, bf16[1024,384]{1,0:T(8,128)(2,1)S(1)} %get-tuple-element.289.d_context_ref, ...), custom_call_target="tpu_custom_call" | custom-call | flops 18000000 | bytes 1024 | tf_op jit(solution)/shard_map/attend_backward/pallas_call | solution.py:218
  225.3 8.2 %d_inputs.2.refs_9_ = f32[1024,768]{1,0:T(8,128)} custom-call(f32[1024,768]{1,0:T(8,128)S(1)} %get-tuple-element.298.d_summed_ref, bf16[1024,1152]{1,0:T(8,128)(2,1)S(1)} %get-tuple-element.308.refs_0_.own_ref.refs_1_, bf16[1024,1152]{1,0:T(8,128)(2,1)S(1)} %get-tuple-element.277.refs_0_.refs_1_.other_ref, bf16[192,1536]{1,0:T(8,128)(2,1)S(1)} %copy-done.17, ...), custom_call_target="tpu_custom_call" | custom-call | flops 18000000 | bytes 1024 | tf_op jit(solution)/shard_map/d_inputs/pallas_call | solution.py:450
  240.1 1.9 collective-permute-start.53
  242.4 2.1 collective-permute-start.51
  247.0 8.1 %d_inputs.3 = f32[1024,768]{1,0:T(8,128)} custom-call(f32[1024,768]{1,0:T(8,128)S(1)} %get-tuple-element.298.d_summed_ref, bf16[1024,1152]{1,0:T(8,128)(2,1)S(1)} %get-tuple-element.308.refs_0_.own_ref.refs_1_, bf16[1024,1152]{1,0:T(8,128)(2,1)S(1)} %get-tuple-element.277.refs_0_.refs_1_.other_ref, ...), custom_call_target="tpu_custom_call", output_to_operand_aliasing={{}: (12, {})} | custom-call | flops 18000000 | bytes 1024 | tf_op jit(solution)/shard_map/d_inputs/pallas_call | solution.py:450
  262.0 2.6 collective-permute-done.57
  264.6 5.2 %collective-permute-done.56 = bf16[48,1152]{1,0:T(8,128)(2,1)S(1)} collective-permute-done((bf16[48,1152]{1,0:T(8,128)(2,1)S(1)}, bf16[48,1152]{1,0:T(8,128)(2,1)S(1)}, u32[]{:S(2)}, u32[]{:S(2)}) %collective-permute-start.56) | collective-permute-done | bytes 110624 | tf_op jit(solution)/shard_map/ppermute | solution.py:525
  (291 shorter events, 85.6 us)
Async XLA Ops:
  4.4 11.7 %collective-permute-start.2 = (bf16[48,1536]{1,0:T(8,128)(2,1)S(1)}, bf16[48,1536]{1,0:T(8,128)(2,1)}, u32[]{:S(2)}, u32[]{:S(2)}) collective-permute-start(bf16[48,1536]{1,0:T(8,128)(2,1)S(1)} %pad_maximum_fusion.3.refs_0_), channel_id=1, source_target_pairs={{0,24},{2,26},{4,28},{6,30},{8,16},{10,18},{12,20},{14,22},{16,8},... | collective-permute-start | bytes 442376 | tf_op jit(solution)/shard_map/ppermute | solution.py:525
  9.5 12.6 %collective-permute-start.1 = (bf16[48,1536]{1,0:T(8,128)(2,1)S(1)}, bf16[48,1536]{1,0:T(8,128)(2,1)}, u32[]{:S(2)}, u32[]{:S(2)}) collective-permute-start(bf16[48,1536]{1,0:T(8,128)(2,1)S(1)} %pad_maximum_fusion.3.refs_0_), channel_id=1, source_target_pairs={{0,16},{2,18},{4,20},{6,22},{8,24},{10,26},{12,28},{14,30},{16,0},... | collective-permute-start | bytes 442376 | tf_op jit(solution)/shard_map/ppermute | solution.py:525
  9.5 12.6 %collective-permute-start = (bf16[48,1536]{1,0:T(8,128)(2,1)S(1)}, bf16[48,1536]{1,0:T(8,128)(2,1)}, u32[]{:S(2)}, u32[]{:S(2)}) collective-permute-start(bf16[48,1536]{1,0:T(8,128)(2,1)S(1)} %pad_maximum_fusion.3.refs_0_), channel_id=1, source_target_pairs={{0,8},{2,10},{4,12},{6,14},{8,0},{10,2},{12,4},{14,6},{16,24},{18,... | collective-permute-start | bytes 442376 | tf_op jit(solution)/shard_map/ppermute | solution.py:525
  23.2 16.8 %collective-permute-start.5 = (bf16[192,1536]{1,0:T(8,128)(2,1)S(1)}, bf16[192,1536]{1,0:T(8,128)(2,1)S(1)}, u32[]{:S(2)}, u32[]{:S(2)}) collective-permute-start(bf16[192,1536]{1,0:T(8,128)(2,1)S(1)} %join.3.a_ref.refs_0_), channel_id=1, source_target_pairs={{0,1},{1,0},{2,3},{3,2},{4,5},{5,4},{6,7},{7,6},{8,9},{9,8},{10,11... | collective-permute-start | bytes 1769480 | tf_op jit(solution)/shard_map/ppermute | solution.py:528
  24.8 15.3 %collective-permute-start.4 = (bf16[192,1536]{1,0:T(8,128)(2,1)S(1)}, bf16[192,1536]{1,0:T(8,128)(2,1)}, u32[]{:S(2)}, u32[]{:S(2)}) collective-permute-start(bf16[192,1536]{1,0:T(8,128)(2,1)S(1)} %join.3.a_ref.refs_0_), channel_id=1, source_target_pairs={{0,4},{2,6},{4,0},{6,2},{8,12},{10,14},{12,8},{14,10},{16,20},{18,... | collective-permute-start | bytes 1769480 | tf_op jit(solution)/shard_map/ppermute | solution.py:525
  40.7 18.4 %collective-permute-start.13 = (bf16[48,1536]{1,0:T(8,128)(2,1)S(1)}, bf16[48,1536]{1,0:T(8,128)(2,1)S(1)}, u32[]{:S(2)}, u32[]{:S(2)}) collective-permute-start(bf16[48,1536]{1,0:T(8,128)(2,1)S(1)} %convert_bitcast_fusion.refs_0_), channel_id=1, source_target_pairs={{0,24},{2,26},{4,28},{6,30},{8,16},{10,18},{12,20},{14,22},{16,8},... | collective-permute-start | bytes 442376 | tf_op jit(solution)/shard_map/ppermute | solution.py:525
  42.2 16.9 %collective-permute-start.12 = (bf16[48,1536]{1,0:T(8,128)(2,1)S(1)}, bf16[48,1536]{1,0:T(8,128)(2,1)S(1)}, u32[]{:S(2)}, u32[]{:S(2)}) collective-permute-start(bf16[48,1536]{1,0:T(8,128)(2,1)S(1)} %convert_bitcast_fusion.refs_0_), channel_id=1, source_target_pairs={{0,16},{2,18},{4,20},{6,22},{8,24},{10,26},{12,28},{14,30},{16,0},... | collective-permute-start | bytes 442376 | tf_op jit(solution)/shard_map/ppermute | solution.py:525
  42.2 16.9 %collective-permute-start.11 = (bf16[48,1536]{1,0:T(8,128)(2,1)S(1)}, bf16[48,1536]{1,0:T(8,128)(2,1)S(1)}, u32[]{:S(2)}, u32[]{:S(2)}) collective-permute-start(bf16[48,1536]{1,0:T(8,128)(2,1)S(1)} %convert_bitcast_fusion.refs_0_), channel_id=1, source_target_pairs={{0,8},{2,10},{4,12},{6,14},{8,0},{10,2},{12,4},{14,6},{16,24},{18,... | collective-permute-start | bytes 442376 | tf_op jit(solution)/shard_map/ppermute | solution.py:525
  45.2 14.8 %collective-permute-start.9 = (bf16[192,1536]{1,0:T(8,128)(2,1)}, bf16[192,1536]{1,0:T(8,128)(2,1)S(1)}, u32[]{:S(2)}, u32[]{:S(2)}) collective-permute-start(bf16[192,1536]{1,0:T(8,128)(2,1)} %collective-permute-done.4.b_ref.refs_1_), channel_id=1, source_target_pairs={{0,1},{1,0},{2,3},{3,2},{4,5},{5,4},{6,7},{7,6},{8,9},{9,8},{10,11... | collective-permute-start | bytes 1769480 | tf_op jit(solution)/shard_map/ppermute | solution.py:528
  45.8 14.2 %collective-permute-start.10 = (bf16[192,1536]{1,0:T(8,128)(2,1)S(1)}, bf16[192,1536]{1,0:T(8,128)(2,1)S(1)}, u32[]{:S(2)}, u32[]{:S(2)}) collective-permute-start(bf16[192,1536]{1,0:T(8,128)(2,1)S(1)} %join.4.refs_0_), channel_id=1, source_target_pairs={{0,4},{2,6},{4,0},{6,2},{8,12},{10,14},{12,8},{14,10},{16,20},{18,... | collective-permute-start | bytes 1769480 | tf_op jit(solution)/shard_map/ppermute | solution.py:525
  60.6 15.4 %collective-permute-start.17 = (bf16[192,1536]{1,0:T(8,128)(2,1)S(1)}, bf16[192,1536]{1,0:T(8,128)(2,1)S(1)}, u32[]{:S(2)}, u32[]{:S(2)}) collective-permute-start(bf16[192,1536]{1,0:T(8,128)(2,1)S(1)} %join.5.refs_0_), channel_id=1, source_target_pairs={{0,4},{2,6},{4,0},{6,2},{8,12},{10,14},{12,8},{14,10},{16,20},{18,... | collective-permute-start | bytes 1769480 | tf_op jit(solution)/shard_map/ppermute | solution.py:525
  62.1 14.4 %collective-permute-start.16 = (bf16[192,1536]{1,0:T(8,128)(2,1)S(1)}, bf16[192,1536]{1,0:T(8,128)(2,1)S(1)}, u32[]{:S(2)}, u32[]{:S(2)}) collective-permute-start(bf16[192,1536]{1,0:T(8,128)(2,1)S(1)} %join.4.refs_0_), channel_id=1, source_target_pairs={{0,1},{1,0},{2,3},{3,2},{4,5},{5,4},{6,7},{7,6},{8,9},{9,8},{10,11... | collective-permute-start | bytes 1769480 | tf_op jit(solution)/shard_map/ppermute | solution.py:528
  76.5 16.0 %collective-permute-start.20 = (bf16[192,1536]{1,0:T(8,128)(2,1)S(1)}, bf16[192,1536]{1,0:T(8,128)(2,1)S(1)}, u32[]{:S(2)}, u32[]{:S(2)}) collective-permute-start(bf16[192,1536]{1,0:T(8,128)(2,1)S(1)} %collective-permute-done.16.refs_0_.refs_4_), channel_id=1, source_target_pairs={{0,4},{2,6},{4,0},{6,2},{8,12},{10,14},{12,8},{14,10},{16,20},{18,... | collective-permute-start | bytes 1769480 | tf_op jit(solution)/shard_map/ppermute | solution.py:525
  77.7 14.7 %collective-permute-start.21 = (bf16[192,1536]{1,0:T(8,128)(2,1)S(1)}, bf16[192,1536]{1,0:T(8,128)(2,1)S(1)}, u32[]{:S(2)}, u32[]{:S(2)}) collective-permute-start(bf16[192,1536]{1,0:T(8,128)(2,1)S(1)} %join.5.refs_0_), channel_id=1, source_target_pairs={{0,1},{1,0},{2,3},{3,2},{4,5},{5,4},{6,7},{7,6},{8,9},{9,8},{10,11... | collective-permute-start | bytes 1769480 | tf_op jit(solution)/shard_map/ppermute | solution.py:528
  93.0 16.8 %collective-permute-start.28 = (bf16[192,1536]{1,0:T(8,128)(2,1)S(1)}, bf16[192,1536]{1,0:T(8,128)(2,1)S(1)}, u32[]{:S(2)}, u32[]{:S(2)}) collective-permute-start(bf16[192,1536]{1,0:T(8,128)(2,1)S(1)} %collective-permute-done.17.refs_1_), channel_id=1, source_target_pairs={{0,2},{2,0},{4,6},{6,4},{8,10},{10,8},{12,14},{14,12},{16,18},{18,... | collective-permute-start | bytes 1769480 | tf_op jit(solution)/shard_map/ppermute | solution.py:525
  93.2 15.7 %collective-permute-start.24 = (bf16[192,1536]{1,0:T(8,128)(2,1)S(1)}, bf16[192,1536]{1,0:T(8,128)(2,1)S(1)}, u32[]{:S(2)}, u32[]{:S(2)}) collective-permute-start(bf16[192,1536]{1,0:T(8,128)(2,1)S(1)} %collective-permute-done.17.refs_1_), channel_id=1, source_target_pairs={{0,1},{1,0},{2,3},{3,2},{4,5},{5,4},{6,7},{7,6},{8,9},{9,8},{10,11... | collective-permute-start | bytes 1769480 | tf_op jit(solution)/shard_map/ppermute | solution.py:528
  93.8 16.0 %collective-permute-start.27 = (bf16[192,1536]{1,0:T(8,128)(2,1)S(1)}, bf16[192,1536]{1,0:T(8,128)(2,1)S(1)}, u32[]{:S(2)}, u32[]{:S(2)}) collective-permute-start(bf16[192,1536]{1,0:T(8,128)(2,1)S(1)} %join.5.refs_0_), channel_id=1, source_target_pairs={{0,2},{2,0},{4,6},{6,4},{8,10},{10,8},{12,14},{14,12},{16,18},{18,... | collective-permute-start | bytes 1769480 | tf_op jit(solution)/shard_map/ppermute | solution.py:525
  137.2 38.2 %collective-permute-start.34 = (bf16[192,1536]{1,0:T(8,128)(2,1)}, bf16[192,1536]{1,0:T(8,128)(2,1)}, u32[]{:S(2)}, u32[]{:S(2)}) collective-permute-start(bf16[192,1536]{1,0:T(8,128)(2,1)} %get-tuple-element.263), channel_id=1, source_target_pairs={{0,4},{2,6},{4,0},{6,2},{8,12},{10,14},{12,8},{14,10},{16,20},{18,... | collective-permute-start | bytes 1769480 | tf_op jit(solution)/shard_map/ppermute | solution.py:525
  138.0 37.5 %collective-permute-start.35 = (bf16[192,1536]{1,0:T(8,128)(2,1)}, bf16[192,1536]{1,0:T(8,128)(2,1)}, u32[]{:S(2)}, u32[]{:S(2)}) collective-permute-start(bf16[192,1536]{1,0:T(8,128)(2,1)} %get-tuple-element.264), channel_id=1, source_target_pairs={{0,1},{1,0},{2,3},{3,2},{4,5},{5,4},{6,7},{7,6},{8,9},{9,8},{10,11... | collective-permute-start | bytes 1769480 | tf_op jit(solution)/shard_map/ppermute | solution.py:528
  138.5 37.0 %collective-permute-start.36 = (bf16[192,1536]{1,0:T(8,128)(2,1)}, bf16[192,1536]{1,0:T(8,128)(2,1)}, u32[]{:S(2)}, u32[]{:S(2)}) collective-permute-start(bf16[192,1536]{1,0:T(8,128)(2,1)} %get-tuple-element.265), channel_id=1, source_target_pairs={{0,5},{1,4},{2,7},{3,6},{4,1},{5,0},{6,3},{7,2},{8,13},{9,12},{10,... | collective-permute-start | bytes 1769480 | tf_op jit(solution)/shard_map/ppermute | solution.py:532
  148.4 21.8 %collective-permute-start.33 = (bf16[384,3072]{1,0:T(8,128)(2,1)}, bf16[384,3072]{1,0:T(8,128)(2,1)}, u32[]{:S(2)}, u32[]{:S(2)}) collective-permute-start(bf16[384,3072]{1,0:T(8,128)(2,1)} %send_grads.6), channel_id=1, source_target_pairs={{0,2},{2,0},{4,6},{6,4},{8,10},{10,8},{12,14},{14,12},{16,18},{18,... | collective-permute-start | bytes 7077896 | tf_op jit(solution)/shard_map/ppermute | solution.py:525
  175.5 17.9 %collective-permute-start.38 = (bf16[192,1792]{1,0:T(8,128)(2,1)S(1)}, bf16[192,1792]{1,0:T(8,128)(2,1)S(1)}, u32[]{:S(2)}, u32[]{:S(2)}) collective-permute-start(bf16[192,1792]{1,0:T(8,128)(2,1)S(1)} %get-tuple-element.270), channel_id=1, source_target_pairs={{0,4},{2,6},{4,0},{6,2},{8,12},{10,14},{12,8},{14,10},{16,20},{18,... | collective-permute-start | bytes 2064392 | tf_op jit(solution)/shard_map/ppermute | solution.py:525
  176.3 19.7 %collective-permute-start.37 = (bf16[384,1024]{1,0:T(8,128)(2,1)S(1)}, bf16[384,1024]{1,0:T(8,128)(2,1)S(1)}, u32[]{:S(2)}, u32[]{:S(2)}) collective-permute-start(bf16[384,1024]{1,0:T(8,128)(2,1)S(1)} %get-tuple-element.269), channel_id=1, source_target_pairs={{0,1},{1,0},{2,3},{3,2},{4,5},{5,4},{6,7},{7,6},{8,9},{9,8},{10,11... | collective-permute-start | bytes 2359304 | tf_op jit(solution)/shard_map/ppermute | solution.py:528
  178.6 13.6 %collective-permute-start.39 = (bf16[96,1536]{1,0:T(8,128)(2,1)S(1)}, bf16[96,1536]{1,0:T(8,128)(2,1)S(1)}, u32[]{:S(2)}, u32[]{:S(2)}) collective-permute-start(bf16[96,1536]{1,0:T(8,128)(2,1)S(1)} %pad_maximum_fusion.2), channel_id=1, source_target_pairs={{0,8},{2,10},{4,12},{6,14},{8,0},{10,2},{12,4},{14,6},{16,24},{18,... | collective-permute-start | bytes 884744 | tf_op jit(solution)/shard_map/ppermute | solution.py:525
  197.6 11.3 %collective-permute-start.41 = (bf16[192,1024]{1,0:T(8,128)(2,1)S(1)}, bf16[192,1024]{1,0:T(8,128)(2,1)S(1)}, u32[]{:S(2)}, u32[]{:S(2)}) collective-permute-start(bf16[192,1024]{1,0:T(8,128)(2,1)S(1)} %add_convert_fusion), channel_id=1, source_target_pairs={{0,4},{2,6},{4,0},{6,2},{8,12},{10,14},{12,8},{14,10},{16,20},{18,... | collective-permute-start | bytes 1179656 | tf_op jit(solution)/shard_map/ppermute | solution.py:525
  209.4 24.2 %collective-permute-start.46 = (bf16[96,1920]{1,0:T(8,128)(2,1)S(1)}, bf16[96,1920]{1,0:T(8,128)(2,1)S(1)}, u32[]{:S(2)}, u32[]{:S(2)}) collective-permute-start(bf16[96,1920]{1,0:T(8,128)(2,1)S(1)} %pad_maximum_fusion.1), channel_id=1, source_target_pairs={{0,8},{2,10},{4,12},{6,14},{8,0},{10,2},{12,4},{14,6},{16,24},{18,... | collective-permute-start | bytes 1105928 | tf_op jit(solution)/shard_map/ppermute | solution.py:525
  211.1 22.5 %collective-permute-start.45 = (bf16[384,1152]{1,0:T(8,128)(2,1)S(1)}, bf16[384,1152]{1,0:T(8,128)(2,1)S(1)}, u32[]{:S(2)}, u32[]{:S(2)}) collective-permute-start(bf16[384,1152]{1,0:T(8,128)(2,1)S(1)} %keep_grads.6), channel_id=1, source_target_pairs={{0,1},{1,0},{2,3},{3,2},{4,5},{5,4},{6,7},{7,6},{8,9},{9,8},{10,11... | collective-permute-start | bytes 2654216 | tf_op jit(solution)/shard_map/ppermute | solution.py:528
  212.6 21.0 %collective-permute-start.44 = (f32[6912]{0:T(1024)S(1)}, f32[6912]{0:T(1024)S(1)}, u32[]{:S(2)}, u32[]{:S(2)}) collective-permute-start(f32[6912]{0:T(1024)S(1)} %pad_maximum_fusion.5), channel_id=1, source_target_pairs={{0,1},{1,0},{2,3},{3,2},{4,5},{5,4},{6,7},{7,6},{8,9},{9,8},{10,11... | collective-permute-start | bytes 82952 | tf_op jit(solution)/shard_map/ppermute | solution.py:528
  234.4 12.6 %collective-permute-start.54 = (bf16[48,1920]{1,0:T(8,128)(2,1)S(1)}, bf16[48,1920]{1,0:T(8,128)(2,1)S(1)}, u32[]{:S(2)}, u32[]{:S(2)}) collective-permute-start(bf16[48,1920]{1,0:T(8,128)(2,1)S(1)} %add_convert_fusion.2), channel_id=1, source_target_pairs={{0,16},{2,18},{4,20},{6,22},{8,24},{10,26},{12,28},{14,30},{16,0},... | collective-permute-start | bytes 552968 | tf_op jit(solution)/shard_map/ppermute | solution.py:525
  240.1 15.0 %collective-permute-start.53 = (f32[6912]{0:T(1024)S(1)}, f32[6912]{0:T(1024)S(1)}, u32[]{:S(2)}, u32[]{:S(2)}) collective-permute-start(f32[6912]{0:T(1024)S(1)} %add.105), channel_id=1, source_target_pairs={{0,24},{2,26},{4,28},{6,30},{8,16},{10,18},{12,20},{14,22},{16,8},... | collective-permute-start | bytes 82952 | tf_op jit(solution)/shard_map/ppermute | solution.py:525
  242.1 13.0 %collective-permute-start.52 = (f32[6912]{0:T(1024)S(1)}, f32[6912]{0:T(1024)S(1)}, u32[]{:S(2)}, u32[]{:S(2)}) collective-permute-start(f32[6912]{0:T(1024)S(1)} %add.105), channel_id=1, source_target_pairs={{0,16},{2,18},{4,20},{6,22},{8,24},{10,26},{12,28},{14,30},{16,0},... | collective-permute-start | bytes 82952 | tf_op jit(solution)/shard_map/ppermute | solution.py:525
  242.4 12.7 %collective-permute-start.51 = (f32[6912]{0:T(1024)S(1)}, f32[6912]{0:T(1024)S(1)}, u32[]{:S(2)}, u32[]{:S(2)}) collective-permute-start(f32[6912]{0:T(1024)S(1)} %add.105), channel_id=1, source_target_pairs={{0,8},{2,10},{4,12},{6,14},{8,0},{10,2},{12,4},{14,6},{16,24},{18,... | collective-permute-start | bytes 82952 | tf_op jit(solution)/shard_map/ppermute | solution.py:525
  (81 other events, 771.0 us)

commit v4 on v3

--- a/solution.py
+++ b/solution.py
@@ -238,13 +238,14 @@
     )(lengths, qkv, context, d_context, lse)
 
 
-def in_vmem(kernel, name, limit, outs, *args, scratch=()):
+def in_vmem(kernel, name, limit, outs, *args, scratch=(), aliases=None):
     return pl.pallas_call(
         kernel,
         in_specs=[pl.BlockSpec(memory_space=pltpu.VMEM)] * len(args),
         out_specs=[pl.BlockSpec(memory_space=pltpu.VMEM)] * len(outs),
         out_shape=[jax.ShapeDtypeStruct(*out) for out in outs],
         scratch_shapes=[pltpu.VMEM(shape, bf16) for shape in scratch],
+        input_output_aliases=aliases or {},
         compiler_params=pltpu.CompilerParams(vmem_limit_bytes=limit << 20),
         cost_estimate=cost(COST[name]),
         name=name,
@@ -352,7 +353,8 @@
     shape = normal_one.shape
     outs = [(shape, bf16), (shape, f32), (shape, bf16), ((8, shape[1]), f32)]
     args = (own, other, *w_own, *w_other, normal_one, cotan, vectors, place)
-    return in_vmem(turn_kernel, "turn", 10, outs, *args, scratch=[(shape[1], own.shape[1])] * 2)
+    scratch = [(shape[1], own.shape[1])] * 2
+    return in_vmem(turn_kernel, "turn", 10, outs, *args, scratch=scratch, aliases={11: 2})
 
 
 def d_hidden_kernel(d_ffn_ref, *refs):
@@ -370,7 +372,9 @@
 
 def d_hidden(d_ffn, w, slope):
     outs = [(slope.shape, bf16), ((8, slope.shape[1]), f32)]
-    return in_vmem(d_hidden_kernel, "d_hidden", 8, outs, d_ffn, *w, slope, scratch=[(d_ffn.shape[1], slope.shape[1])])
+    args = (d_ffn, *w, slope)
+    scratch = [(d_ffn.shape[1], slope.shape[1])]
+    return in_vmem(d_hidden_kernel, "d_hidden", 8, outs, *args, scratch=scratch, aliases={5: 0})
 
 
 def d_attention_kernel(own_ref, other_ref, *refs):
@@ -397,7 +401,8 @@
     shape = d_before.shape
     outs = [(shape, f32), (shape, bf16), ((8, shape[1]), f32)]
     args = (own, other, *w_own, *w_other, d_before, normal, scale, vectors)
-    return in_vmem(d_attention_kernel, "d_attention", 10, outs, *args, scratch=[(shape[1], own.shape[1])] * 2)
+    scratch = [(shape[1], own.shape[1])] * 2
+    return in_vmem(d_attention_kernel, "d_attention", 10, outs, *args, scratch=scratch, aliases={10: 0})
 
 
 def d_context_kernel(d_attn_ref, *refs):
@@ -557,14 +562,11 @@
     def halve_rest(self, keep, away):
         for bit in self.bits[1:]:
             keep, away = self.halve([mine + theirs.astype(f32) for mine, theirs in zip(keep, away)], bit)
-        return keep[0] + away[0].astype(f32)
-
-    def total_far(self, array):
-        for steps in reversed(self.far):
-            parts = [array] + [self.flip(array, step) for step in steps[1:]]
-            while len(parts) > 1:
-                parts = [parts[i] + parts[i + 1] for i in range(0, len(parts), 2)]
-            array = parts[0]
+        return keep[0], away[0]
+
+    def total_rest(self, array):
+        for bit in self.bits[1:]:
+            array = array + self.flip(array, bit)
         return array
 
 
@@ -783,7 +785,7 @@
     pair_other = flip(send_other, 1)
     first_near = flip((first_low + received(first_across[upper:])).astype(bf16), 2)
     last_across = cross((last_cross + received(last_near[:, rest:])).astype(bf16))
-    sum_outer = exchange.halve_rest(keep_outer, lower_outer)
+    keep_outer, lower_outer = exchange.halve_rest(keep_outer, lower_outer)
 
     pair_other, d_proj_other = gate((pair_other, d_proj_other))
     triple = 3 * width
@@ -793,9 +795,10 @@
         [((2 * upper, triple), bf16)],
     )
 
-    away_other, d_context_own, qkv_sums_other, first_near, last_across, sum_outer = gate(
-        (away_other, d_context_own, qkv_sums_other, first_near, last_across, sum_outer)
-    )
+    away_other, d_context_own, qkv_sums_other, first_near, last_across, keep_outer, lower_outer = gate(
+        (away_other, d_context_own, qkv_sums_other, first_near, last_across, keep_outer, lower_outer)
+    )
+    sum_outer = keep_outer + received(lower_outer)
     across_qkv = cross(away_other)
     whole = permuted(jnp.concatenate([sums_one[:3], sums_two[:3]]), ((1,), (1,))).reshape(-1)
     across_small = cross(jnp.concatenate([qkv_sums_other[0], qkv_sums_other[1], inner_sums_other[0], whole]))
@@ -812,7 +815,7 @@
     pair_own = flip(send_own, 1)
     small = jnp.concatenate([qkv_sums_own[0], qkv_sums_own[1], inner_sums_own[0], whole]) + across_small
     pair_small = flip(small, 1)
-    sum_mid = exchange.halve_rest(keep_mid, lower_mid)
+    keep_mid, lower_mid = exchange.halve_rest(keep_mid, lower_mid)
 
     pair_own, d_proj_own, small, pair_small = gate((pair_own, d_proj_own, small, pair_small))
     small = small + pair_small
@@ -825,11 +828,16 @@
 
     keep_qkv, away_qkv, small, near_small, early = gate((keep_qkv, away_qkv, small, near_small, early))
     near_qkv = flip(away_qkv, 2)
-    small = exchange.total_far(small + near_small)
+    small = small + near_small
+    pair_small = exchange.flip(small, exchange.bits[0])
     grad_tokens = d_inputs(d_summed, d_proj_own, d_proj_other, attn_own, attn_other, place16, 1, (early,))
 
-    keep_qkv, near_qkv, small, grad_tokens, sum_mid = gate((keep_qkv, near_qkv, small, grad_tokens, sum_mid))
+    keep_qkv, near_qkv, small, pair_small, grad_tokens, keep_mid, lower_mid = gate(
+        (keep_qkv, near_qkv, small, pair_small, grad_tokens, keep_mid, lower_mid)
+    )
+    sum_mid = keep_mid + received(lower_mid)
     sum_qkv = exchange.scatter_far(keep_qkv + received(near_qkv))
+    small = exchange.total_rest(small + pair_small)
 
     inner_width = bias_inner.shape[0]
     cuts = np.cumsum([width, width, inner_width] + [model] * 6)

time: 276 us -> 272 us (0.986)
    ppermute x46 -> x45, waiting for transfers between devices: 38.2 us -> 33.6 us  [flip(): return lax.ppermute(array, 'fsdp', [(i, i ^ bit) for i in range(self.fsdp)])]
    ppermute x46 -> x45, starting transfers between devices: 39.3 us -> 38.2 us  [flip(): return lax.ppermute(array, 'fsdp', [(i, i ^ bit) for i in range(self.fsdp)])]
  transfers between devices with their start and end apart: 58 -> 57, of which waited for: 22 -> 24; matrix products, arithmetic and copies ran while one was open for 5% -> 6% of each run, Pallas kernels for 43% -> 44%
where the time goes in v4:
time: 272 us; the launch traced here: 266 us
  Pallas kernels  138 us (51%)
  starting transfers between devices  51.7 us (19%)
  waiting for transfers between devices  44.8 us (16%)
  local copies, waits for them, and re-layouts  13.6 us (5%)
  other arithmetic  9.97 us (4%)
  matrix products  6.25 us (2%)
    pallas_call x20, Pallas kernels, in_vmem(): pl.pallas_call(kernel, in_specs=[pl.BlockSpec(memory_space=pltpu.VMEM)] *...  76.2 us
    ppermute x45, starting transfers between devices, flip(): return lax.ppermute(array, 'fsdp', [(i, i ^ bit) for i in range(self.fsdp)])  38.2 us
    ppermute x45, waiting for transfers between devices, flip(): return lax.ppermute(array, 'fsdp', [(i, i ^ bit) for i in range(self.fsdp)])  33.6 us
    pallas_call x2, Pallas kernels, attend_forward(): pl.pallas_call(functools.partial(attend_forward_kernel, pairs), grid_spec...  24.4 us
    pallas_call x2, Pallas kernels, attend_backward(): pl.pallas_call(functools.partial(attend_backward_kernel, pairs), grid_spe...  21.2 us
    pallas_call x2, Pallas kernels, d_inputs(): pl.pallas_call(d_inputs_kernel, grid=(steps,), in_specs=[tile(model), til...  16.3 us
    ppermute x11, starting transfers between devices, cross(): return lax.ppermute(array, 'tp', [(0, 1), (1, 0)])  11.2 us
    ppermute x11, waiting for transfers between devices, cross(): return lax.ppermute(array, 'tp', [(0, 1), (1, 0)])  11.2 us
  transfers between devices with their start and end apart: 57, of which 24 were waited for; matrix products, arithmetic and copies ran while one was open for 6% of the time, Pallas kernels for 44%

profile of v4, /device:TPU:0, one launch (start us, length us, event | category | flops | bytes accessed | tf_op | source)
XLA Modules:
  0.0 266.4 jit_solution(5447996083907733087)
XLA Ops:
  4.4 5.1 %collective-permute-start.2 = (bf16[48,1536]{1,0:T(8,128)(2,1)S(1)}, bf16[48,1536]{1,0:T(8,128)(2,1)}, u32[]{:S(2)}, u32[]{:S(2)}) collective-permute-start(bf16[48,1536]{1,0:T(8,128)(2,1)S(1)} %pad_maximum_fusion.3.refs_0_), channel_id=1, source_target_pairs={{0,24},{2,26},{4,28},{6,30},{8,16},{10,18},{12,20},{14,22},{16,8},... | collective-permute-start | bytes 442376 | tf_op jit(solution)/shard_map/ppermute | solution.py:530
  16.1 6.0 %collective-permute-done.1.refs_2_ = bf16[48,1536]{1,0:T(8,128)(2,1)} collective-permute-done((bf16[48,1536]{1,0:T(8,128)(2,1)S(1)}, bf16[48,1536]{1,0:T(8,128)(2,1)}, u32[]{:S(2)}, u32[]{:S(2)}) %collective-permute-start.1) | collective-permute-done | bytes 147488 | tf_op jit(solution)/shard_map/ppermute | solution.py:530
  26.4 2.5 collective-permute-start.8
  30.8 2.9 %fusion.6.refs_9_ = bf16[1024,768]{1,0:T(8,128)(2,1)S(1)} fusion(bf16[1024,768]{1,0:T(8,128)(2,1)} %param.21, s32[768]{0:T(1024)S(1)} %add.86), kind=kOutput, calls=%fused_computation.12 | convolution fusion | flops 1209335808 | bytes 3148800 | tf_op jit(solution)/shard_map/dot_general | solution.py:40
  34.9 5.1 %collective-permute-done.7.refs_2_ = bf16[48,1536]{1,0:T(8,128)(2,1)S(1)} collective-permute-done((bf16[48,1536]{1,0:T(8,128)(2,1)S(1)}, bf16[48,1536]{1,0:T(8,128)(2,1)S(1)}, u32[]{:S(2)}, u32[]{:S(2)}) %collective-permute-start.7) | collective-permute-done | bytes 147488 | tf_op jit(solution)/shard_map/ppermute | solution.py:530
  42.2 2.9 %collective-permute-start.11 = (bf16[48,1536]{1,0:T(8,128)(2,1)S(1)}, bf16[48,1536]{1,0:T(8,128)(2,1)S(1)}, u32[]{:S(2)}, u32[]{:S(2)}) collective-permute-start(bf16[48,1536]{1,0:T(8,128)(2,1)S(1)} %convert_bitcast_fusion.refs_0_), channel_id=1, source_target_pairs={{0,8},{2,10},{4,12},{6,14},{8,0},{10,2},{12,4},{14,6},{16,24},{18,... | collective-permute-start | bytes 442376 | tf_op jit(solution)/shard_map/ppermute | solution.py:530
  46.3 12.8 %attend_forward.2 = (bf16[1024,1152]{1,0:T(8,128)(2,1)S(1)}, bf16[1024,384]{1,0:T(8,128)(2,1)S(1)}, f32[2,6,512]{2,1,0:T(8,128)S(1)}) custom-call(s32[2]{0:T(128)S(1)} %dynamic_slice.3.lengths_ref, bf16[1024,768]{1,0:T(8,128)(2,1)S(1)} %fusion.7.inputs_ref.refs_8_.left_ref.refs_0_, bf16[192,1536]{1,0:T(8,128)(2,1)S(1)} %join.3.a_ref.refs_0_, ...), custom_call_target="tpu_custom_call" | custom-call | flops 35100000256 | bytes 1024 | tf_op jit(solution)/shard_map/attend_forward/pallas_call | solution.py:146
  63.6 11.7 %attend_forward.3 = (bf16[1024,1152]{1,0:T(8,128)(2,1)S(1)}, bf16[1024,384]{1,0:T(8,128)(2,1)S(1)}, f32[2,6,512]{2,1,0:T(8,128)S(1)}) custom-call(s32[2]{0:T(128)S(1)} %dynamic_slice.3.lengths_ref, bf16[1024,768]{1,0:T(8,128)(2,1)S(1)} %fusion.7.inputs_ref.refs_8_.left_ref.refs_0_, bf16[192,1536]{1,0:T(8,128)(2,1)S(1)} %collective-permute-done.5.a_ref.refs_4_, ...), custom_call_target="tpu_custom_call" | custom-call | flops 35100000256 | bytes 1024 | tf_op jit(solution)/shard_map/attend_forward/pallas_call | solution.py:146
  79.8 4.6 %attention_out.1 = (f32[1024,768]{1,0:T(8,128)S(1)}, f32[1024,1]{1,0:T(8,128)S(1)}, bf16[1024,768]{1,0:T(8,128)(2,1)S(1)}) custom-call(bf16[1024,384]{1,0:T(8,128)(2,1)S(1)} %get-tuple-element.209.own_ref.refs_0_.refs_4_.context_ref, bf16[1024,384]{1,0:T(8,128)(2,1)S(1)} %get-tuple-element.210.other_ref.refs_1_.refs_5_.context_ref, ...), custom_call_target="tpu_custom_call" | custom-call | flops 10800000000 | bytes 1024 | tf_op jit(solution)/shard_map/attention_out/pallas_call | solution.py:242
  84.4 8.0 %hidden.2 = (bf16[1024,1536]{1,0:T(8,128)(2,1)S(1)}, bf16[1024,1536]{1,0:T(8,128)(2,1)S(1)}) custom-call(bf16[1024,768]{1,0:T(8,128)(2,1)S(1)} %get-tuple-element.254.normed_ref.left_ref.refs_0_, bf16[192,1536]{1,0:T(8,128)(2,1)S(1)} %join.4.refs_0_, bf16[192,1536]{1,0:T(8,128)(2,1)S(1)} %collective-permute-done.10.refs_1_, ...), custom_call_target="tpu_custom_call" | custom-call | flops 22950000640 | bytes 1024 | tf_op jit(solution)/shard_map/hidden/pallas_call | solution.py:242
  95.3 8.0 %hidden.3 = (bf16[1024,1536]{1,0:T(8,128)(2,1)S(1)}, bf16[1024,1536]{1,0:T(8,128)(2,1)S(1)}) custom-call(bf16[1024,768]{1,0:T(8,128)(2,1)S(1)} %get-tuple-element.254.normed_ref.left_ref.refs_0_, bf16[192,1536]{1,0:T(8,128)(2,1)S(1)} %collective-permute-done.16.refs_0_.refs_4_, bf16[192,1536]{1,0:T(8,128)(2,1)S(1)} %collective-permute-done.20.refs_1_.refs_5_, ...), custom_call_target="tpu_custom_call" | custom-call | flops 22950000640 | bytes 1024 | tf_op jit(solution)/shard_map/hidden/pallas_call | solution.py:242
  103.3 5.5 %collective-permute-done.24.refs_5_.refs_1_ = bf16[192,1536]{1,0:T(8,128)(2,1)S(1)} collective-permute-done((bf16[192,1536]{1,0:T(8,128)(2,1)S(1)}, bf16[192,1536]{1,0:T(8,128)(2,1)S(1)}, u32[]{:S(2)}, u32[]{:S(2)}) %collective-permute-start.24) | collective-permute-done | bytes 589856 | tf_op jit(solution)/shard_map/ppermute | solution.py:533
  111.7 13.7 %turn.1 = (bf16[1024,768]{1,0:T(8,128)(2,1)}, f32[1024,768]{1,0:T(8,128)S(1)}, bf16[1024,768]{1,0:T(8,128)(2,1)S(1)}, f32[8,768]{1,0:T(8,128)S(1)}) custom-call(bf16[1024,1536]{1,0:T(8,128)(2,1)S(1)} %get-tuple-element.215.own_ref.refs_0_.refs_1_, ...), custom_call_target="tpu_custom_call", output_to_operand_aliasing={{2}: (11, {})} | custom-call | flops 35100000256 | bytes 1024 | tf_op jit(solution)/shard_map/turn/pallas_call | solution.py:242
  125.3 2.6 send_grads.5
  128.2 3.7 %d_hidden.2 = (bf16[1024,1536]{1,0:T(8,128)(2,1)S(1)}, f32[8,1536]{1,0:T(8,128)S(1)}) custom-call(bf16[1024,768]{1,0:T(8,128)(2,1)S(1)} %get-tuple-element.242.left_ref.d_ffn_ref.refs_0_, bf16[192,1536]{1,0:T(8,128)(2,1)S(1)} %join.5.refs_0_, bf16[192,1536]{1,0:T(8,128)(2,1)S(1)} %collective-permute-done.17.refs_1_, ...), custom_call_target="tpu_custom_call", output_to_operand_aliasing={{0}: (5, {})} | custom-call | flops 9720000512 | bytes 1024 | tf_op jit(solution)/shard_map/d_hidden/pallas_call | solution.py:242
  132.6 3.6 %keep_grads.4 = (f32[192,1536]{1,0:T(8,128)S(1)}, bf16[192,1536]{1,0:T(8,128)(2,1)}, bf16[192,1536]{1,0:T(8,128)(2,1)}, bf16[192,1536]{1,0:T(8,128)(2,1)}) custom-call(bf16[1024,768]{1,0:T(8,128)(2,1)S(1)} %get-tuple-element.242.left_ref.d_ffn_ref.refs_0_, bf16[1024,1536]{1,0:T(8,128)(2,1)S(1)} %get-tuple-element.215.own_ref.refs_0_.refs_1_, ...), custom_call_target="tpu_custom_call" | custom-call | flops 9450000384 | bytes 1024 | tf_op jit(solution)/shard_map/keep_grads/pallas_call | solution.py:242
  137.5 2.2 collective-permute-start.36
  139.7 3.7 %d_hidden.3 = (bf16[1024,1536]{1,0:T(8,128)(2,1)S(1)}, f32[8,1536]{1,0:T(8,128)S(1)}) custom-call(bf16[1024,768]{1,0:T(8,128)(2,1)S(1)} %get-tuple-element.242.left_ref.d_ffn_ref.refs_0_, bf16[192,1536]{1,0:T(8,128)(2,1)S(1)} %collective-permute-done.21.refs_4_.refs_0_, ...), custom_call_target="tpu_custom_call", output_to_operand_aliasing={{0}: (5, {})} | custom-call | flops 9720000512 | bytes 1024 | tf_op jit(solution)/shard_map/d_hidden/pallas_call | solution.py:242
  143.4 4.1 %send_grads.6 = bf16[384,3072]{1,0:T(8,128)(2,1)} custom-call(bf16[1024,768]{1,0:T(8,128)(2,1)S(1)} %get-tuple-element.254.normed_ref.left_ref.refs_0_, bf16[1024,1536]{1,0:T(8,128)(2,1)S(1)} %get-tuple-element.235.refs_0_.own_ref.refs_2_, bf16[1024,1536]{1,0:T(8,128)(2,1)S(1)} %get-tuple-element.245.refs_1_.other_ref.refs_3_), custom_call_target="tpu_custom_call" | custom-call | flops 18000000 | bytes 1024 | tf_op jit(solution)/shard_map/send_grads/pallas_call | solution.py:242
  147.5 7.4 %d_attention.1 = (f32[1024,768]{1,0:T(8,128)S(1)}, bf16[1024,768]{1,0:T(8,128)(2,1)S(1)}, f32[8,768]{1,0:T(8,128)S(1)}) custom-call(bf16[1024,1536]{1,0:T(8,128)(2,1)S(1)} %get-tuple-element.235.refs_0_.own_ref.refs_2_, bf16[1024,1536]{1,0:T(8,128)(2,1)S(1)} %get-tuple-element.245.refs_1_.other_ref.refs_3_, ...), custom_call_target="tpu_custom_call", output_to_operand_aliasing={{0}: (10, {})} | custom-call | flops 27000000512 | bytes 1024 | tf_op jit(solution)/shard_map/d_attention/pallas_call | solution.py:242
  165.4 3.8 %d_context.1 = (bf16[1024,384]{1,0:T(8,128)(2,1)S(1)}, bf16[1024,384]{1,0:T(8,128)(2,1)S(1)}) custom-call(bf16[1024,768]{1,0:T(8,128)(2,1)S(1)} %copy-done.39, bf16[192,1536]{1,0:T(8,128)(2,1)S(1)} %copy-done.17, bf16[192,1536]{1,0:T(8,128)(2,1)} %collective-permute-done.4.b_ref.refs_1_, bf16[192,1536]{1,0:T(8,128)(2,1)S(1)} %copy-done.21, ...), custom_call_target="tpu_custom_call" | custom-call | flops 5400000000 | bytes 1024 | tf_op jit(solution)/shard_map/d_context/pallas_call | solution.py:242
  169.3 5.2 %keep_grads.5 = (f32[192,1024]{1,0:T(8,128)S(1)}, f32[192,1024]{1,0:T(8,128)S(1)}, bf16[384,1024]{1,0:T(8,128)(2,1)S(1)}, f32[192,896]{1,0:T(8,128)S(1)}, f32[19...) custom-call(bf16[1024,768]{1,0:T(8,128)(2,1)S(1)} %copy-done.36, bf16[1024,768]{1,0:T(8,128)(2,1)S(1)} %copy-done.39, ...), custom_call_target="tpu_custom_call" | custom-call | flops 9450000384 | bytes 1024 | tf_op jit(solution)/shard_map/keep_grads/pallas_call | solution.py:242
  179.3 10.6 %attend_backward.2 = (bf16[1024,1152]{1,0:T(8,128)(2,1)S(1)}, f32[8,384]{1,0:T(8,128)S(1)}) custom-call(s32[2]{0:T(128)S(1)} %copy-done.43, bf16[1024,1152]{1,0:T(8,128)(2,1)S(1)} %copy-done.34, bf16[1024,384]{1,0:T(8,128)(2,1)S(1)} %copy-done.11, bf16[1024,384]{1,0:T(8,128)(2,1)S(1)} %get-tuple-element.269.d_context_ref, ...), custom_call_target="tpu_custom_call" | custom-call | flops 18000000 | bytes 1024 | tf_op jit(solution)/shard_map/attend_backward/pallas_call | solution.py:218
  192.5 2.6 collective-permute-done.37
  199.7 4.1 %collective-permute-done.43 = bf16[48,1536]{1,0:T(8,128)(2,1)S(1)} collective-permute-done((bf16[48,1536]{1,0:T(8,128)(2,1)S(1)}, bf16[48,1536]{1,0:T(8,128)(2,1)S(1)}, u32[]{:S(2)}, u32[]{:S(2)}) %collective-permute-start.43) | collective-permute-done | bytes 147488 | tf_op jit(solution)/shard_map/ppermute | solution.py:530
  203.8 2.7 collective-permute-done.42
  212.3 10.6 %attend_backward.3 = (bf16[1024,1152]{1,0:T(8,128)(2,1)S(1)}, f32[8,384]{1,0:T(8,128)S(1)}) custom-call(s32[2]{0:T(128)S(1)} %copy-done.43, bf16[1024,1152]{1,0:T(8,128)(2,1)S(1)} %copy-done.32, bf16[1024,384]{1,0:T(8,128)(2,1)S(1)} %copy-done.8, bf16[1024,384]{1,0:T(8,128)(2,1)S(1)} %get-tuple-element.292.d_context_ref, ...), custom_call_target="tpu_custom_call" | custom-call | flops 18000000 | bytes 1024 | tf_op jit(solution)/shard_map/attend_backward/pallas_call | solution.py:218
  224.3 8.2 %d_inputs.2.refs_9_ = f32[1024,768]{1,0:T(8,128)} custom-call(f32[1024,768]{1,0:T(8,128)S(1)} %get-tuple-element.301.d_summed_ref, bf16[1024,1152]{1,0:T(8,128)(2,1)S(1)} %get-tuple-element.311.refs_0_.own_ref.refs_1_, bf16[1024,1152]{1,0:T(8,128)(2,1)S(1)} %get-tuple-element.280.refs_0_.refs_1_.other_ref, bf16[192,1536]{1,0:T(8,128)(2,1)S(1)} %copy-done.17, ...), custom_call_target="tpu_custom_call" | custom-call | flops 18000000 | bytes 1024 | tf_op jit(solution)/shard_map/d_inputs/pallas_call | solution.py:455
  242.1 8.1 %d_inputs.3 = f32[1024,768]{1,0:T(8,128)} custom-call(f32[1024,768]{1,0:T(8,128)S(1)} %get-tuple-element.301.d_summed_ref, bf16[1024,1152]{1,0:T(8,128)(2,1)S(1)} %get-tuple-element.311.refs_0_.own_ref.refs_1_, bf16[1024,1152]{1,0:T(8,128)(2,1)S(1)} %get-tuple-element.280.refs_0_.refs_1_.other_ref, ...), custom_call_target="tpu_custom_call", output_to_operand_aliasing={{}: (12, {})} | custom-call | flops 18000000 | bytes 1024 | tf_op jit(solution)/shard_map/d_inputs/pallas_call | solution.py:455
  255.4 2.0 collective-permute-start.55
  259.4 2.6 collective-permute-done.55
  262.0 3.5 %collective-permute-done.54 = bf16[48,1152]{1,0:T(8,128)(2,1)S(1)} collective-permute-done((bf16[48,1152]{1,0:T(8,128)(2,1)S(1)}, bf16[48,1152]{1,0:T(8,128)(2,1)S(1)}, u32[]{:S(2)}, u32[]{:S(2)}) %collective-permute-start.54) | collective-permute-done | bytes 110624 | tf_op jit(solution)/shard_map/ppermute | solution.py:530
  (292 shorter events, 84.5 us)
Async XLA Ops:
  4.4 11.7 %collective-permute-start.2 = (bf16[48,1536]{1,0:T(8,128)(2,1)S(1)}, bf16[48,1536]{1,0:T(8,128)(2,1)}, u32[]{:S(2)}, u32[]{:S(2)}) collective-permute-start(bf16[48,1536]{1,0:T(8,128)(2,1)S(1)} %pad_maximum_fusion.3.refs_0_), channel_id=1, source_target_pairs={{0,24},{2,26},{4,28},{6,30},{8,16},{10,18},{12,20},{14,22},{16,8},... | collective-permute-start | bytes 442376 | tf_op jit(solution)/shard_map/ppermute | solution.py:530
  9.5 12.6 %collective-permute-start.1 = (bf16[48,1536]{1,0:T(8,128)(2,1)S(1)}, bf16[48,1536]{1,0:T(8,128)(2,1)}, u32[]{:S(2)}, u32[]{:S(2)}) collective-permute-start(bf16[48,1536]{1,0:T(8,128)(2,1)S(1)} %pad_maximum_fusion.3.refs_0_), channel_id=1, source_target_pairs={{0,16},{2,18},{4,20},{6,22},{8,24},{10,26},{12,28},{14,30},{16,0},... | collective-permute-start | bytes 442376 | tf_op jit(solution)/shard_map/ppermute | solution.py:530
  9.5 12.6 %collective-permute-start = (bf16[48,1536]{1,0:T(8,128)(2,1)S(1)}, bf16[48,1536]{1,0:T(8,128)(2,1)}, u32[]{:S(2)}, u32[]{:S(2)}) collective-permute-start(bf16[48,1536]{1,0:T(8,128)(2,1)S(1)} %pad_maximum_fusion.3.refs_0_), channel_id=1, source_target_pairs={{0,8},{2,10},{4,12},{6,14},{8,0},{10,2},{12,4},{14,6},{16,24},{18,... | collective-permute-start | bytes 442376 | tf_op jit(solution)/shard_map/ppermute | solution.py:530
  23.2 16.8 %collective-permute-start.5 = (bf16[192,1536]{1,0:T(8,128)(2,1)S(1)}, bf16[192,1536]{1,0:T(8,128)(2,1)S(1)}, u32[]{:S(2)}, u32[]{:S(2)}) collective-permute-start(bf16[192,1536]{1,0:T(8,128)(2,1)S(1)} %join.3.a_ref.refs_0_), channel_id=1, source_target_pairs={{0,1},{1,0},{2,3},{3,2},{4,5},{5,4},{6,7},{7,6},{8,9},{9,8},{10,11... | collective-permute-start | bytes 1769480 | tf_op jit(solution)/shard_map/ppermute | solution.py:533
  24.8 15.3 %collective-permute-start.4 = (bf16[192,1536]{1,0:T(8,128)(2,1)S(1)}, bf16[192,1536]{1,0:T(8,128)(2,1)}, u32[]{:S(2)}, u32[]{:S(2)}) collective-permute-start(bf16[192,1536]{1,0:T(8,128)(2,1)S(1)} %join.3.a_ref.refs_0_), channel_id=1, source_target_pairs={{0,4},{2,6},{4,0},{6,2},{8,12},{10,14},{12,8},{14,10},{16,20},{18,... | collective-permute-start | bytes 1769480 | tf_op jit(solution)/shard_map/ppermute | solution.py:530
  28.9 11.1 %collective-permute-start.7 = (bf16[48,1536]{1,0:T(8,128)(2,1)S(1)}, bf16[48,1536]{1,0:T(8,128)(2,1)S(1)}, u32[]{:S(2)}, u32[]{:S(2)}) collective-permute-start(bf16[48,1536]{1,0:T(8,128)(2,1)S(1)} %convert_element_type.97.refs_0_), channel_id=1, source_target_pairs={{0,16},{2,18},{4,20},{6,22},{8,24},{10,26},{12,28},{14,30},{16,0},... | collective-permute-start | bytes 442376 | tf_op jit(solution)/shard_map/ppermute | solution.py:530
  28.9 11.1 %collective-permute-start.6 = (bf16[48,1536]{1,0:T(8,128)(2,1)S(1)}, bf16[48,1536]{1,0:T(8,128)(2,1)S(1)}, u32[]{:S(2)}, u32[]{:S(2)}) collective-permute-start(bf16[48,1536]{1,0:T(8,128)(2,1)S(1)} %convert_element_type.97.refs_0_), channel_id=1, source_target_pairs={{0,8},{2,10},{4,12},{6,14},{8,0},{10,2},{12,4},{14,6},{16,24},{18,... | collective-permute-start | bytes 442376 | tf_op jit(solution)/shard_map/ppermute | solution.py:530
  40.7 18.4 %collective-permute-start.13 = (bf16[48,1536]{1,0:T(8,128)(2,1)S(1)}, bf16[48,1536]{1,0:T(8,128)(2,1)S(1)}, u32[]{:S(2)}, u32[]{:S(2)}) collective-permute-start(bf16[48,1536]{1,0:T(8,128)(2,1)S(1)} %convert_bitcast_fusion.refs_0_), channel_id=1, source_target_pairs={{0,24},{2,26},{4,28},{6,30},{8,16},{10,18},{12,20},{14,22},{16,8},... | collective-permute-start | bytes 442376 | tf_op jit(solution)/shard_map/ppermute | solution.py:530
  42.2 16.9 %collective-permute-start.12 = (bf16[48,1536]{1,0:T(8,128)(2,1)S(1)}, bf16[48,1536]{1,0:T(8,128)(2,1)S(1)}, u32[]{:S(2)}, u32[]{:S(2)}) collective-permute-start(bf16[48,1536]{1,0:T(8,128)(2,1)S(1)} %convert_bitcast_fusion.refs_0_), channel_id=1, source_target_pairs={{0,16},{2,18},{4,20},{6,22},{8,24},{10,26},{12,28},{14,30},{16,0},... | collective-permute-start | bytes 442376 | tf_op jit(solution)/shard_map/ppermute | solution.py:530
  42.2 16.9 %collective-permute-start.11 = (bf16[48,1536]{1,0:T(8,128)(2,1)S(1)}, bf16[48,1536]{1,0:T(8,128)(2,1)S(1)}, u32[]{:S(2)}, u32[]{:S(2)}) collective-permute-start(bf16[48,1536]{1,0:T(8,128)(2,1)S(1)} %convert_bitcast_fusion.refs_0_), channel_id=1, source_target_pairs={{0,8},{2,10},{4,12},{6,14},{8,0},{10,2},{12,4},{14,6},{16,24},{18,... | collective-permute-start | bytes 442376 | tf_op jit(solution)/shard_map/ppermute | solution.py:530
  45.2 14.8 %collective-permute-start.9 = (bf16[192,1536]{1,0:T(8,128)(2,1)}, bf16[192,1536]{1,0:T(8,128)(2,1)S(1)}, u32[]{:S(2)}, u32[]{:S(2)}) collective-permute-start(bf16[192,1536]{1,0:T(8,128)(2,1)} %collective-permute-done.4.b_ref.refs_1_), channel_id=1, source_target_pairs={{0,1},{1,0},{2,3},{3,2},{4,5},{5,4},{6,7},{7,6},{8,9},{9,8},{10,11... | collective-permute-start | bytes 1769480 | tf_op jit(solution)/shard_map/ppermute | solution.py:533
  45.8 14.2 %collective-permute-start.10 = (bf16[192,1536]{1,0:T(8,128)(2,1)S(1)}, bf16[192,1536]{1,0:T(8,128)(2,1)S(1)}, u32[]{:S(2)}, u32[]{:S(2)}) collective-permute-start(bf16[192,1536]{1,0:T(8,128)(2,1)S(1)} %join.4.refs_0_), channel_id=1, source_target_pairs={{0,4},{2,6},{4,0},{6,2},{8,12},{10,14},{12,8},{14,10},{16,20},{18,... | collective-permute-start | bytes 1769480 | tf_op jit(solution)/shard_map/ppermute | solution.py:530
  60.6 15.4 %collective-permute-start.17 = (bf16[192,1536]{1,0:T(8,128)(2,1)S(1)}, bf16[192,1536]{1,0:T(8,128)(2,1)S(1)}, u32[]{:S(2)}, u32[]{:S(2)}) collective-permute-start(bf16[192,1536]{1,0:T(8,128)(2,1)S(1)} %join.5.refs_0_), channel_id=1, source_target_pairs={{0,4},{2,6},{4,0},{6,2},{8,12},{10,14},{12,8},{14,10},{16,20},{18,... | collective-permute-start | bytes 1769480 | tf_op jit(solution)/shard_map/ppermute | solution.py:530
  62.1 14.4 %collective-permute-start.16 = (bf16[192,1536]{1,0:T(8,128)(2,1)S(1)}, bf16[192,1536]{1,0:T(8,128)(2,1)S(1)}, u32[]{:S(2)}, u32[]{:S(2)}) collective-permute-start(bf16[192,1536]{1,0:T(8,128)(2,1)S(1)} %join.4.refs_0_), channel_id=1, source_target_pairs={{0,1},{1,0},{2,3},{3,2},{4,5},{5,4},{6,7},{7,6},{8,9},{9,8},{10,11... | collective-permute-start | bytes 1769480 | tf_op jit(solution)/shard_map/ppermute | solution.py:533
  76.5 16.0 %collective-permute-start.20 = (bf16[192,1536]{1,0:T(8,128)(2,1)S(1)}, bf16[192,1536]{1,0:T(8,128)(2,1)S(1)}, u32[]{:S(2)}, u32[]{:S(2)}) collective-permute-start(bf16[192,1536]{1,0:T(8,128)(2,1)S(1)} %collective-permute-done.16.refs_0_.refs_4_), channel_id=1, source_target_pairs={{0,4},{2,6},{4,0},{6,2},{8,12},{10,14},{12,8},{14,10},{16,20},{18,... | collective-permute-start | bytes 1769480 | tf_op jit(solution)/shard_map/ppermute | solution.py:530
  77.7 14.7 %collective-permute-start.21 = (bf16[192,1536]{1,0:T(8,128)(2,1)S(1)}, bf16[192,1536]{1,0:T(8,128)(2,1)S(1)}, u32[]{:S(2)}, u32[]{:S(2)}) collective-permute-start(bf16[192,1536]{1,0:T(8,128)(2,1)S(1)} %join.5.refs_0_), channel_id=1, source_target_pairs={{0,1},{1,0},{2,3},{3,2},{4,5},{5,4},{6,7},{7,6},{8,9},{9,8},{10,11... | collective-permute-start | bytes 1769480 | tf_op jit(solution)/shard_map/ppermute | solution.py:533
  93.0 16.8 %collective-permute-start.28 = (bf16[192,1536]{1,0:T(8,128)(2,1)S(1)}, bf16[192,1536]{1,0:T(8,128)(2,1)S(1)}, u32[]{:S(2)}, u32[]{:S(2)}) collective-permute-start(bf16[192,1536]{1,0:T(8,128)(2,1)S(1)} %collective-permute-done.17.refs_1_), channel_id=1, source_target_pairs={{0,2},{2,0},{4,6},{6,4},{8,10},{10,8},{12,14},{14,12},{16,18},{18,... | collective-permute-start | bytes 1769480 | tf_op jit(solution)/shard_map/ppermute | solution.py:530
  93.2 15.7 %collective-permute-start.24 = (bf16[192,1536]{1,0:T(8,128)(2,1)S(1)}, bf16[192,1536]{1,0:T(8,128)(2,1)S(1)}, u32[]{:S(2)}, u32[]{:S(2)}) collective-permute-start(bf16[192,1536]{1,0:T(8,128)(2,1)S(1)} %collective-permute-done.17.refs_1_), channel_id=1, source_target_pairs={{0,1},{1,0},{2,3},{3,2},{4,5},{5,4},{6,7},{7,6},{8,9},{9,8},{10,11... | collective-permute-start | bytes 1769480 | tf_op jit(solution)/shard_map/ppermute | solution.py:533
  93.8 16.0 %collective-permute-start.27 = (bf16[192,1536]{1,0:T(8,128)(2,1)S(1)}, bf16[192,1536]{1,0:T(8,128)(2,1)S(1)}, u32[]{:S(2)}, u32[]{:S(2)}) collective-permute-start(bf16[192,1536]{1,0:T(8,128)(2,1)S(1)} %join.5.refs_0_), channel_id=1, source_target_pairs={{0,2},{2,0},{4,6},{6,4},{8,10},{10,8},{12,14},{14,12},{16,18},{18,... | collective-permute-start | bytes 1769480 | tf_op jit(solution)/shard_map/ppermute | solution.py:530
  136.2 38.3 %collective-permute-start.34 = (bf16[192,1536]{1,0:T(8,128)(2,1)}, bf16[192,1536]{1,0:T(8,128)(2,1)}, u32[]{:S(2)}, u32[]{:S(2)}) collective-permute-start(bf16[192,1536]{1,0:T(8,128)(2,1)} %get-tuple-element.266), channel_id=1, source_target_pairs={{0,4},{2,6},{4,0},{6,2},{8,12},{10,14},{12,8},{14,10},{16,20},{18,... | collective-permute-start | bytes 1769480 | tf_op jit(solution)/shard_map/ppermute | solution.py:530
  136.9 37.6 %collective-permute-start.35 = (bf16[192,1536]{1,0:T(8,128)(2,1)}, bf16[192,1536]{1,0:T(8,128)(2,1)}, u32[]{:S(2)}, u32[]{:S(2)}) collective-permute-start(bf16[192,1536]{1,0:T(8,128)(2,1)} %get-tuple-element.267), channel_id=1, source_target_pairs={{0,1},{1,0},{2,3},{3,2},{4,5},{5,4},{6,7},{7,6},{8,9},{9,8},{10,11... | collective-permute-start | bytes 1769480 | tf_op jit(solution)/shard_map/ppermute | solution.py:533
  137.5 37.1 %collective-permute-start.36 = (bf16[192,1536]{1,0:T(8,128)(2,1)}, bf16[192,1536]{1,0:T(8,128)(2,1)}, u32[]{:S(2)}, u32[]{:S(2)}) collective-permute-start(bf16[192,1536]{1,0:T(8,128)(2,1)} %get-tuple-element.268), channel_id=1, source_target_pairs={{0,5},{1,4},{2,7},{3,6},{4,1},{5,0},{6,3},{7,2},{8,13},{9,12},{10,... | collective-permute-start | bytes 1769480 | tf_op jit(solution)/shard_map/ppermute | solution.py:537
  147.5 21.8 %collective-permute-start.33 = (bf16[384,3072]{1,0:T(8,128)(2,1)}, bf16[384,3072]{1,0:T(8,128)(2,1)}, u32[]{:S(2)}, u32[]{:S(2)}) collective-permute-start(bf16[384,3072]{1,0:T(8,128)(2,1)} %send_grads.6), channel_id=1, source_target_pairs={{0,2},{2,0},{4,6},{6,4},{8,10},{10,8},{12,14},{14,12},{16,18},{18,... | collective-permute-start | bytes 7077896 | tf_op jit(solution)/shard_map/ppermute | solution.py:530
  174.6 17.9 %collective-permute-start.38 = (bf16[192,1792]{1,0:T(8,128)(2,1)S(1)}, bf16[192,1792]{1,0:T(8,128)(2,1)S(1)}, u32[]{:S(2)}, u32[]{:S(2)}) collective-permute-start(bf16[192,1792]{1,0:T(8,128)(2,1)S(1)} %get-tuple-element.273), channel_id=1, source_target_pairs={{0,4},{2,6},{4,0},{6,2},{8,12},{10,14},{12,8},{14,10},{16,20},{18,... | collective-permute-start | bytes 2064392 | tf_op jit(solution)/shard_map/ppermute | solution.py:530
  175.4 19.7 %collective-permute-start.37 = (bf16[384,1024]{1,0:T(8,128)(2,1)S(1)}, bf16[384,1024]{1,0:T(8,128)(2,1)S(1)}, u32[]{:S(2)}, u32[]{:S(2)}) collective-permute-start(bf16[384,1024]{1,0:T(8,128)(2,1)S(1)} %get-tuple-element.272), channel_id=1, source_target_pairs={{0,1},{1,0},{2,3},{3,2},{4,5},{5,4},{6,7},{7,6},{8,9},{9,8},{10,11... | collective-permute-start | bytes 2359304 | tf_op jit(solution)/shard_map/ppermute | solution.py:533
  177.7 13.6 %collective-permute-start.39 = (bf16[96,1536]{1,0:T(8,128)(2,1)S(1)}, bf16[96,1536]{1,0:T(8,128)(2,1)S(1)}, u32[]{:S(2)}, u32[]{:S(2)}) collective-permute-start(bf16[96,1536]{1,0:T(8,128)(2,1)S(1)} %pad_maximum_fusion.2), channel_id=1, source_target_pairs={{0,8},{2,10},{4,12},{6,14},{8,0},{10,2},{12,4},{14,6},{16,24},{18,... | collective-permute-start | bytes 884744 | tf_op jit(solution)/shard_map/ppermute | solution.py:530
  196.7 11.3 %collective-permute-start.41 = (bf16[192,1024]{1,0:T(8,128)(2,1)S(1)}, bf16[192,1024]{1,0:T(8,128)(2,1)S(1)}, u32[]{:S(2)}, u32[]{:S(2)}) collective-permute-start(bf16[192,1024]{1,0:T(8,128)(2,1)S(1)} %add_convert_fusion), channel_id=1, source_target_pairs={{0,4},{2,6},{4,0},{6,2},{8,12},{10,14},{12,8},{14,10},{16,20},{18,... | collective-permute-start | bytes 1179656 | tf_op jit(solution)/shard_map/ppermute | solution.py:530
  208.4 24.2 %collective-permute-start.46 = (bf16[96,1920]{1,0:T(8,128)(2,1)S(1)}, bf16[96,1920]{1,0:T(8,128)(2,1)S(1)}, u32[]{:S(2)}, u32[]{:S(2)}) collective-permute-start(bf16[96,1920]{1,0:T(8,128)(2,1)S(1)} %pad_maximum_fusion.1), channel_id=1, source_target_pairs={{0,8},{2,10},{4,12},{6,14},{8,0},{10,2},{12,4},{14,6},{16,24},{18,... | collective-permute-start | bytes 1105928 | tf_op jit(solution)/shard_map/ppermute | solution.py:530
  210.2 22.5 %collective-permute-start.45 = (bf16[384,1152]{1,0:T(8,128)(2,1)S(1)}, bf16[384,1152]{1,0:T(8,128)(2,1)S(1)}, u32[]{:S(2)}, u32[]{:S(2)}) collective-permute-start(bf16[384,1152]{1,0:T(8,128)(2,1)S(1)} %keep_grads.6), channel_id=1, source_target_pairs={{0,1},{1,0},{2,3},{3,2},{4,5},{5,4},{6,7},{7,6},{8,9},{9,8},{10,11... | collective-permute-start | bytes 2654216 | tf_op jit(solution)/shard_map/ppermute | solution.py:533
  211.7 21.0 %collective-permute-start.44 = (f32[6912]{0:T(1024)S(1)}, f32[6912]{0:T(1024)S(1)}, u32[]{:S(2)}, u32[]{:S(2)}) collective-permute-start(f32[6912]{0:T(1024)S(1)} %pad_maximum_fusion.5), channel_id=1, source_target_pairs={{0,1},{1,0},{2,3},{3,2},{4,5},{5,4},{6,7},{7,6},{8,9},{9,8},{10,11... | collective-permute-start | bytes 82952 | tf_op jit(solution)/shard_map/ppermute | solution.py:533
  234.2 16.0 %collective-permute-start.52 = (bf16[48,1920]{1,0:T(8,128)(2,1)S(1)}, bf16[48,1920]{1,0:T(8,128)(2,1)S(1)}, u32[]{:S(2)}, u32[]{:S(2)}) collective-permute-start(bf16[48,1920]{1,0:T(8,128)(2,1)S(1)} %add_convert_fusion.2), channel_id=1, source_target_pairs={{0,16},{2,18},{4,20},{6,22},{8,24},{10,26},{12,28},{14,30},{16,0},... | collective-permute-start | bytes 552968 | tf_op jit(solution)/shard_map/ppermute | solution.py:530
  239.2 11.0 %collective-permute-start.51 = (f32[6912]{0:T(1024)S(1)}, f32[6912]{0:T(1024)S(1)}, u32[]{:S(2)}, u32[]{:S(2)}) collective-permute-start(f32[6912]{0:T(1024)S(1)} %add.101), channel_id=1, source_target_pairs={{0,8},{2,10},{4,12},{6,14},{8,0},{10,2},{12,4},{14,6},{16,24},{18,... | collective-permute-start | bytes 82952 | tf_op jit(solution)/shard_map/ppermute | solution.py:530
  (80 other events, 747.4 us)

commit v5 on v4

--- a/solution.py
+++ b/solution.py
@@ -24,9 +24,10 @@
     turn=39,
     d_hidden=10.8,
     d_attention=30,
-    d_context=6,
+    d_context=20,
     d_inputs=0.02,
     join=3,
+    order=3,
     send_grads=0.02,
     keep_grads=10.5,
 )
@@ -282,6 +283,47 @@
     return in_vmem(join_kernel, "join", 8, [((len(arrays) * rows, width), arrays[0].dtype)], *arrays)[0]
 
 
+def exact_dot(dot, vectors, place):
+    parts, left = [], vectors
+    for _ in range(3):
+        part = left.astype(bf16).astype(f32)
+        parts.append(part)
+        left = left - part
+    count = vectors.shape[0]
+    result = dot(jnp.concatenate(parts, axis=0).astype(bf16), place)
+    return result[:count] + result[count : 2 * count] + result[2 * count :]
+
+
+def order_kernel(rows_ref, vectors_ref, place_ref, out_ref, ordered_ref):
+    ordered_ref[...] = exact_dot(dot_nn, vectors_ref[...], place_ref[...])
+
+    def body(at):
+        out_ref[at] = dot_nn(rows_ref[at], place_ref[...]).astype(bf16)
+
+    tiles_of(rows_ref, body)
+
+
+def order(rows, vectors, place):
+    outs = [(rows.shape, bf16), (vectors.shape, f32)]
+    return in_vmem(order_kernel, "order", 8, outs, rows, vectors, place)
+
+
+def small_kernel(one_ref, two_ref, qkv_ref, inner_ref, place_ref, out_ref):
+    whole = exact_dot(dot_nt, jnp.concatenate([one_ref[...], two_ref[...]], axis=0), place_ref[...])
+    model = out_ref.shape[1]
+    rows = inner_ref.shape[1] // model
+    out_ref[...] = jnp.zeros_like(out_ref)
+    out_ref[0:1] = side(qkv_ref[0:1], qkv_ref[1:2])
+    for index in range(rows):
+        out_ref[1 + index : 2 + index] = inner_ref[0:1, index * model : (index + 1) * model]
+    out_ref[1 + rows : 4 + rows] = whole[:3]
+    out_ref[4 + rows : 7 + rows] = whole[8:11]
+
+
+def small_sums(one, two, qkv, inner, place):
+    return in_vmem(small_kernel, "order", 8, [((16, place.shape[0]), f32)], one, two, qkv, inner, place)[0]
+
+
 def attention_out_kernel(own_ref, other_ref, *refs):
     pieces, (inputs_ref, vectors_ref, normal_ref, scale_ref, normed_ref, weight_ref) = refs[:8], refs[8:]
     width = own_ref.shape[1]
@@ -608,13 +650,7 @@
     source = (here ^ masks) * block + inside
     place = jnp.arange(model, dtype=jnp.int32)[:, None] == source[None, :]
     place16 = place.astype(bf16)
-    place32 = place.astype(f32)
     lengths_here = lax.dynamic_slice_in_dim(lengths, lax.axis_index("tp") * seqs, seqs, 0)
-
-    def permuted(vectors, dims):
-        return lax.dot_general(
-            vectors, place32, ((dims), ((), ())), precision=lax.Precision.HIGHEST, preferred_element_type=f32
-        )
 
     zero = jnp.zeros((width,), f32)
 
@@ -632,7 +668,7 @@
     biases_other = cross(biases_own)
     inputs = dot_nn(tokens, place16).astype(bf16)
     shard_inner, shard_outer = w_inner.astype(bf16), w_outer.T.astype(bf16)
-    vectors = jnp.stack([bias_output, norm1_gain, norm1_bias, bias_outer, norm2_gain, norm2_bias])
+    vectors = jnp.stack([bias_output, norm1_gain, norm1_bias, bias_outer, norm2_gain, norm2_bias, bias_output, bias_output])
 
     far_attn, shard_inner, shard_outer, biases_other, cotangent, vectors, inputs = gate(
         (far_attn, shard_inner, shard_outer, biases_other, cotangent, vectors, inputs)
@@ -640,8 +676,7 @@
     far_attn = join(far_attn)
     near_attn, across_attn = flip(far_attn, 2), cross(far_attn)
     far_inner = exchange.gather_far(shard_inner)
-    cotan = dot_nn(cotangent, place16).astype(bf16)
-    vectors = permuted(vectors, ((1,), (0,)))
+    cotan, vectors = order(cotangent, vectors, place16)
 
     far_attn, near_attn, across_attn, far_inner, shard_outer, inputs = gate(
         (far_attn, near_attn, across_attn, far_inner, shard_outer, inputs), cotan, vectors
@@ -787,7 +822,10 @@
     last_across = cross((last_cross + received(last_near[:, rest:])).astype(bf16))
     keep_outer, lower_outer = exchange.halve_rest(keep_outer, lower_outer)
 
-    pair_other, d_proj_other = gate((pair_other, d_proj_other))
+    pair_other, d_proj_other, qkv_sums_other, sums_one, sums_two = gate(
+        (pair_other, d_proj_other, qkv_sums_other, sums_one, sums_two)
+    )
+    small_other = small_sums(sums_one, sums_two, qkv_sums_other, inner_sums_other, place16)
     triple = 3 * width
     (away_other,) = keep_grads(
         (inputs, d_proj_other, pair_other),
@@ -795,13 +833,12 @@
         [((2 * upper, triple), bf16)],
     )
 
-    away_other, d_context_own, qkv_sums_other, first_near, last_across, keep_outer, lower_outer = gate(
-        (away_other, d_context_own, qkv_sums_other, first_near, last_across, keep_outer, lower_outer)
+    away_other, d_context_own, small_other, first_near, last_across, keep_outer, lower_outer = gate(
+        (away_other, d_context_own, small_other, first_near, last_across, keep_outer, lower_outer)
     )
     sum_outer = keep_outer + received(lower_outer)
     across_qkv = cross(away_other)
-    whole = permuted(jnp.concatenate([sums_one[:3], sums_two[:3]]), ((1,), (1,))).reshape(-1)
-    across_small = cross(jnp.concatenate([qkv_sums_other[0], qkv_sums_other[1], inner_sums_other[0], whole]))
+    across_small = cross(small_other)
     first_keep = first_keep + received(first_across[:upper]) + received(first_near)
     last_keep = last_keep + received(last_near[:, :rest]) + received(last_across)
     keep_mid, lower_mid = exchange.halve_first(jnp.concatenate([first_keep, last_keep], axis=1))
@@ -813,7 +850,7 @@
         (send_own, d_proj_own, qkv_sums_own, across_small, across_qkv, early, keep_mid, lower_mid)
     )
     pair_own = flip(send_own, 1)
-    small = jnp.concatenate([qkv_sums_own[0], qkv_sums_own[1], inner_sums_own[0], whole]) + across_small
+    small = across_small + small_sums(sums_one, sums_two, qkv_sums_own, inner_sums_own, place16)
     pair_small = flip(small, 1)
     keep_mid, lower_mid = exchange.halve_rest(keep_mid, lower_mid)
 
@@ -839,9 +876,10 @@
     sum_qkv = exchange.scatter_far(keep_qkv + received(near_qkv))
     small = exchange.total_rest(small + pair_small)
 
-    inner_width = bias_inner.shape[0]
-    cuts = np.cumsum([width, width, inner_width] + [model] * 6)
-    query_bias, value_bias, inner_bias_sum, *rest = jnp.split(small, cuts[:-1])
+    query_bias, value_bias = small[0, :width], small[0, width:]
+    rows = inner_width // model
+    inner_bias_sum = small[1 : 1 + rows].reshape(-1)
+    rest = [small[1 + rows + index] for index in range(6)]
 
     return (
         mixed,

time: 272 us -> 260 us (0.956)
  local copies, waits for them, and re-layouts: 13.6 us -> 6.19 us
  matrix products: 6.25 us -> 1.44 us
  waiting for transfers between devices: 44.8 us -> 48.9 us
    unnamed x110 -> x48, local copies, waits for them, and re-layouts: 9.17 us -> 1.84 us
    ppermute x1, waiting for transfers between devices: 0.01 us -> 3.22 us  [flip_cross(): return lax.ppermute(array, ('fsdp', 'tp'), pairs)]
    dot_general x2 -> x1, matrix products: 4.3 us -> 1.44 us  [dot_nn(): lax.dot_general(left, right, (((1,), (0,)), ((), ())), preferred_element_...]
    pallas_call x20 -> x23, Pallas kernels: 76.2 us -> 75.1 us  [in_vmem(): pl.pallas_call(kernel, in_specs=[pl.BlockSpec(memory_space=pltpu.VMEM)] *...]
  transfers between devices with their start and end apart: 57 -> 57, of which waited for: 24 -> 24; matrix products, arithmetic and copies ran while one was open for 6% -> 4% of each run, Pallas kernels for 44% -> 46%
where the time goes in v5:
time: 260 us; the launch traced here: 256 us
  Pallas kernels  137 us (53%)
  starting transfers between devices  52.5 us (20%)
  waiting for transfers between devices  48.9 us (19%)
  other arithmetic  8.63 us (3%)
  local copies, waits for them, and re-layouts  6.19 us (2%)
    pallas_call x23, Pallas kernels, in_vmem(): pl.pallas_call(kernel, in_specs=[pl.BlockSpec(memory_space=pltpu.VMEM)] *...  75.1 us
    ppermute x45, starting transfers between devices, flip(): return lax.ppermute(array, 'fsdp', [(i, i ^ bit) for i in range(self.fsdp)])  38.8 us
    ppermute x45, waiting for transfers between devices, flip(): return lax.ppermute(array, 'fsdp', [(i, i ^ bit) for i in range(self.fsdp)])  33.7 us
    pallas_call x2, Pallas kernels, attend_forward(): pl.pallas_call(functools.partial(attend_forward_kernel, pairs), grid_spec...  24.2 us
    pallas_call x2, Pallas kernels, attend_backward(): pl.pallas_call(functools.partial(attend_backward_kernel, pairs), grid_spe...  21.3 us
    pallas_call x2, Pallas kernels, d_inputs(): pl.pallas_call(d_inputs_kernel, grid=(steps,), in_specs=[tile(model), til...  16.4 us
    ppermute x11, waiting for transfers between devices, cross(): return lax.ppermute(array, 'tp', [(0, 1), (1, 0)])  11.9 us
    ppermute x11, starting transfers between devices, cross(): return lax.ppermute(array, 'tp', [(0, 1), (1, 0)])  11.4 us
  transfers between devices with their start and end apart: 57, of which 24 were waited for; matrix products, arithmetic and copies ran while one was open for 4% of the time, Pallas kernels for 46%

profile of v5, /device:TPU:0, one launch (start us, length us, event | category | flops | bytes accessed | tf_op | source)
XLA Modules:
  0.0 256.4 jit_solution(1841571318812915655)
XLA Ops:
  4.4 5.1 %collective-permute-start.2 = (bf16[48,1536]{1,0:T(8,128)(2,1)S(1)}, bf16[48,1536]{1,0:T(8,128)(2,1)}, u32[]{:S(2)}, u32[]{:S(2)}) collective-permute-start(bf16[48,1536]{1,0:T(8,128)(2,1)S(1)} %pad_maximum_fusion.3.refs_0_), channel_id=1, source_target_pairs={{0,24},{2,26},{4,28},{6,30},{8,16},{10,18},{12,20},{14,22},{16,8},... | collective-permute-start | bytes 442376 | tf_op jit(solution)/shard_map/ppermute | solution.py:572
  16.1 6.0 %collective-permute-done.1.refs_2_ = bf16[48,1536]{1,0:T(8,128)(2,1)} collective-permute-done((bf16[48,1536]{1,0:T(8,128)(2,1)S(1)}, bf16[48,1536]{1,0:T(8,128)(2,1)}, u32[]{:S(2)}, u32[]{:S(2)}) %collective-permute-start.1) | collective-permute-done | bytes 147488 | tf_op jit(solution)/shard_map/ppermute | solution.py:572
  26.8 2.6 %collective-permute-start.8 = (bf16[48,1536]{1,0:T(8,128)(2,1)S(1)}, bf16[48,1536]{1,0:T(8,128)(2,1)S(1)}, u32[]{:S(2)}, u32[]{:S(2)}) collective-permute-start(bf16[48,1536]{1,0:T(8,128)(2,1)S(1)} %convert_element_type.93.refs_0_), channel_id=1, source_target_pairs={{0,24},{2,26},{4,28},{6,30},{8,16},{10,18},{12,20},{14,22},{16,8},... | collective-permute-start | bytes 442376 | tf_op jit(solution)/shard_map/ppermute | solution.py:572
  32.6 2.7 %order.3 = (bf16[1024,768]{1,0:T(8,128)(2,1)S(1)}, f32[8,768]{1,0:T(8,128)S(1)}) custom-call(bf16[1024,768]{1,0:T(8,128)(2,1)S(1)} %copy-done.4, f32[8,768]{1,0:T(8,128)S(1)} %stack.29.vectors_ref, bf16[768,768]{1,0:T(8,128)(2,1)S(1)} %fusion.place_ref.refs_11_.refs_8_), custom_call_target="tpu_custom_call" | custom-call | flops 2700000000 | bytes 1024 | tf_op jit(solution)/shard_map/order/pallas_call | solution.py:243
  35.4 5.1 %collective-permute-done.7.refs_2_ = bf16[48,1536]{1,0:T(8,128)(2,1)S(1)} collective-permute-done((bf16[48,1536]{1,0:T(8,128)(2,1)S(1)}, bf16[48,1536]{1,0:T(8,128)(2,1)S(1)}, u32[]{:S(2)}, u32[]{:S(2)}) %collective-permute-start.7) | collective-permute-done | bytes 147488 | tf_op jit(solution)/shard_map/ppermute | solution.py:572
  42.6 2.9 %collective-permute-start.11 = (bf16[48,1536]{1,0:T(8,128)(2,1)S(1)}, bf16[48,1536]{1,0:T(8,128)(2,1)S(1)}, u32[]{:S(2)}, u32[]{:S(2)}) collective-permute-start(bf16[48,1536]{1,0:T(8,128)(2,1)S(1)} %convert_bitcast_fusion.refs_0_), channel_id=1, source_target_pairs={{0,8},{2,10},{4,12},{6,14},{8,0},{10,2},{12,4},{14,6},{16,24},{18,... | collective-permute-start | bytes 442376 | tf_op jit(solution)/shard_map/ppermute | solution.py:572
  46.7 12.6 %attend_forward.2 = (bf16[1024,1152]{1,0:T(8,128)(2,1)S(1)}, bf16[1024,384]{1,0:T(8,128)(2,1)S(1)}, f32[2,6,512]{2,1,0:T(8,128)S(1)}) custom-call(s32[2]{0:T(128)S(1)} %dynamic_slice.3.lengths_ref, bf16[1024,768]{1,0:T(8,128)(2,1)S(1)} %fusion.3.inputs_ref.refs_8_.left_ref.refs_0_, bf16[192,1536]{1,0:T(8,128)(2,1)S(1)} %join.3.a_ref.refs_0_, ...), custom_call_target="tpu_custom_call" | custom-call | flops 35100000256 | bytes 1024 | tf_op jit(solution)/shard_map/attend_forward/pallas_call | solution.py:147
  63.3 11.7 %attend_forward.3 = (bf16[1024,1152]{1,0:T(8,128)(2,1)S(1)}, bf16[1024,384]{1,0:T(8,128)(2,1)S(1)}, f32[2,6,512]{2,1,0:T(8,128)S(1)}) custom-call(s32[2]{0:T(128)S(1)} %dynamic_slice.3.lengths_ref, bf16[1024,768]{1,0:T(8,128)(2,1)S(1)} %fusion.3.inputs_ref.refs_8_.left_ref.refs_0_, bf16[192,1536]{1,0:T(8,128)(2,1)S(1)} %collective-permute-done.5.a_ref.refs_4_, ...), custom_call_target="tpu_custom_call" | custom-call | flops 35100000256 | bytes 1024 | tf_op jit(solution)/shard_map/attend_forward/pallas_call | solution.py:147
  80.1 4.6 %attention_out.1 = (f32[1024,768]{1,0:T(8,128)S(1)}, f32[1024,1]{1,0:T(8,128)S(1)}, bf16[1024,768]{1,0:T(8,128)(2,1)S(1)}) custom-call(bf16[1024,384]{1,0:T(8,128)(2,1)S(1)} %get-tuple-element.216.own_ref.refs_0_.refs_4_.context_ref, bf16[1024,384]{1,0:T(8,128)(2,1)S(1)} %get-tuple-element.217.other_ref.refs_1_.refs_5_.context_ref, ...), custom_call_target="tpu_custom_call" | custom-call | flops 10800000000 | bytes 1024 | tf_op jit(solution)/shard_map/attention_out/pallas_call | solution.py:243
  84.7 8.0 %hidden.2 = (bf16[1024,1536]{1,0:T(8,128)(2,1)S(1)}, bf16[1024,1536]{1,0:T(8,128)(2,1)S(1)}) custom-call(bf16[1024,768]{1,0:T(8,128)(2,1)S(1)} %get-tuple-element.261.normed_ref.left_ref.refs_0_, bf16[192,1536]{1,0:T(8,128)(2,1)S(1)} %join.4.refs_0_, bf16[192,1536]{1,0:T(8,128)(2,1)S(1)} %collective-permute-done.10.refs_1_, ...), custom_call_target="tpu_custom_call" | custom-call | flops 22950000640 | bytes 1024 | tf_op jit(solution)/shard_map/hidden/pallas_call | solution.py:243
  95.6 8.0 %hidden.3 = (bf16[1024,1536]{1,0:T(8,128)(2,1)S(1)}, bf16[1024,1536]{1,0:T(8,128)(2,1)S(1)}) custom-call(bf16[1024,768]{1,0:T(8,128)(2,1)S(1)} %get-tuple-element.261.normed_ref.left_ref.refs_0_, bf16[192,1536]{1,0:T(8,128)(2,1)S(1)} %collective-permute-done.16.refs_0_.refs_4_, bf16[192,1536]{1,0:T(8,128)(2,1)S(1)} %collective-permute-done.20.refs_1_.refs_5_, ...), custom_call_target="tpu_custom_call" | custom-call | flops 22950000640 | bytes 1024 | tf_op jit(solution)/shard_map/hidden/pallas_call | solution.py:243
  103.6 5.5 %collective-permute-done.24.refs_5_.refs_1_ = bf16[192,1536]{1,0:T(8,128)(2,1)S(1)} collective-permute-done((bf16[192,1536]{1,0:T(8,128)(2,1)S(1)}, bf16[192,1536]{1,0:T(8,128)(2,1)S(1)}, u32[]{:S(2)}, u32[]{:S(2)}) %collective-permute-start.24) | collective-permute-done | bytes 589856 | tf_op jit(solution)/shard_map/ppermute | solution.py:575
  112.0 13.5 %turn.1 = (bf16[1024,768]{1,0:T(8,128)(2,1)}, f32[1024,768]{1,0:T(8,128)S(1)}, bf16[1024,768]{1,0:T(8,128)(2,1)S(1)}, f32[8,768]{1,0:T(8,128)S(1)}) custom-call(bf16[1024,1536]{1,0:T(8,128)(2,1)S(1)} %get-tuple-element.222.own_ref.refs_0_.refs_1_, ...), custom_call_target="tpu_custom_call", output_to_operand_aliasing={{2}: (11, {})} | custom-call | flops 35100000256 | bytes 1024 | tf_op jit(solution)/shard_map/turn/pallas_call | solution.py:243
  125.5 2.6 %send_grads.5 = bf16[384,3072]{1,0:T(8,128)(2,1)S(1)} custom-call(bf16[1024,768]{1,0:T(8,128)(2,1)S(1)} %get-tuple-element.249.left_ref.d_ffn_ref.refs_0_, bf16[1024,1536]{1,0:T(8,128)(2,1)S(1)} %get-tuple-element.222.own_ref.refs_0_.refs_1_, bf16[1024,1536]{1,0:T(8,128)(2,1)S(1)} %get-tuple-element.229.other_ref.refs_1_.refs_2_), custom_call_target="tpu_custom_call" | custom-call | flops 18000000 | bytes 1024 | tf_op jit(solution)/shard_map/send_grads/pallas_call | solution.py:243
  128.3 3.7 %d_hidden.2 = (bf16[1024,1536]{1,0:T(8,128)(2,1)S(1)}, f32[8,1536]{1,0:T(8,128)S(1)}) custom-call(bf16[1024,768]{1,0:T(8,128)(2,1)S(1)} %get-tuple-element.249.left_ref.d_ffn_ref.refs_0_, bf16[192,1536]{1,0:T(8,128)(2,1)S(1)} %join.5.refs_0_, bf16[192,1536]{1,0:T(8,128)(2,1)S(1)} %collective-permute-done.17.refs_1_, ...), custom_call_target="tpu_custom_call", output_to_operand_aliasing={{0}: (5, {})} | custom-call | flops 9720000512 | bytes 1024 | tf_op jit(solution)/shard_map/d_hidden/pallas_call | solution.py:243
  132.7 2.6 %keep_grads.4 = (f32[192,1536]{1,0:T(8,128)S(1)}, bf16[192,1536]{1,0:T(8,128)(2,1)S(1)}, bf16[192,1536]{1,0:T(8,128)(2,1)S(1)}, bf16[192,1536]{1,0:T(8,128)(2,1)S(1)}) custom-call(bf16[1024,768]{1,0:T(8,128)(2,1)S(1)} %get-tuple-element.249.left_ref.d_ffn_ref.refs_0_, bf16[1024,1536]{1,0:T(8,128)(2,1)S(1)} %get-tuple-element.222.own_ref.refs_0_.refs_1_, ...), custom_call_target="tpu_custom_call" | custom-call | flops 9450000384 | bytes 1024 | tf_op jit(solution)/shard_map/keep_grads/pallas_call | solution.py:243
  136.6 2.2 collective-permute-start.36
  138.9 3.7 %d_hidden.3 = (bf16[1024,1536]{1,0:T(8,128)(2,1)S(1)}, f32[8,1536]{1,0:T(8,128)S(1)}) custom-call(bf16[1024,768]{1,0:T(8,128)(2,1)S(1)} %get-tuple-element.249.left_ref.d_ffn_ref.refs_0_, bf16[192,1536]{1,0:T(8,128)(2,1)S(1)} %collective-permute-done.21.refs_4_.refs_0_, ...), custom_call_target="tpu_custom_call", output_to_operand_aliasing={{0}: (5, {})} | custom-call | flops 9720000512 | bytes 1024 | tf_op jit(solution)/shard_map/d_hidden/pallas_call | solution.py:243
  142.6 2.6 %send_grads.6 = bf16[384,3072]{1,0:T(8,128)(2,1)S(1)} custom-call(bf16[1024,768]{1,0:T(8,128)(2,1)S(1)} %get-tuple-element.261.normed_ref.left_ref.refs_0_, bf16[1024,1536]{1,0:T(8,128)(2,1)S(1)} %get-tuple-element.242.refs_0_.own_ref.refs_2_, bf16[1024,1536]{1,0:T(8,128)(2,1)S(1)} %get-tuple-element.252.refs_1_.other_ref.refs_3_), custom_call_target="tpu_custom_call" | custom-call | flops 18000000 | bytes 1024 | tf_op jit(solution)/shard_map/send_grads/pallas_call | solution.py:243
  145.4 7.4 %d_attention.1 = (f32[1024,768]{1,0:T(8,128)S(1)}, bf16[1024,768]{1,0:T(8,128)(2,1)S(1)}, f32[8,768]{1,0:T(8,128)S(1)}) custom-call(bf16[1024,1536]{1,0:T(8,128)(2,1)S(1)} %get-tuple-element.242.refs_0_.own_ref.refs_2_, bf16[1024,1536]{1,0:T(8,128)(2,1)S(1)} %get-tuple-element.252.refs_1_.other_ref.refs_3_, ...), custom_call_target="tpu_custom_call", output_to_operand_aliasing={{0}: (10, {})} | custom-call | flops 27000000512 | bytes 1024 | tf_op jit(solution)/shard_map/d_attention/pallas_call | solution.py:243
  154.3 3.5 %d_context.1 = (bf16[1024,384]{1,0:T(8,128)(2,1)S(1)}, bf16[1024,384]{1,0:T(8,128)(2,1)S(1)}) custom-call(bf16[1024,768]{1,0:T(8,128)(2,1)S(1)} %get-tuple-element.262.left_ref.d_attn_ref.refs_1_, bf16[192,1536]{1,0:T(8,128)(2,1)S(1)} %join.3.a_ref.refs_0_, bf16[192,1536]{1,0:T(8,128)(2,1)} %collective-permute-done.4.b_ref.refs_1_, ...), custom_call_target="tpu_custom_call" | custom-call | flops 17999998976 | bytes 1024 | tf_op jit(solution)/shard_map/d_context/pallas_call | solution.py:243
  157.9 3.5 %keep_grads.5 = (f32[192,1024]{1,0:T(8,128)S(1)}, f32[192,1024]{1,0:T(8,128)S(1)}, bf16[384,1024]{1,0:T(8,128)(2,1)S(1)}, f32[192,896]{1,0:T(8,128)S(1)}, f32[19...) custom-call(bf16[1024,768]{1,0:T(8,128)(2,1)S(1)} %get-tuple-element.261.normed_ref.left_ref.refs_0_, ...), custom_call_target="tpu_custom_call" | custom-call | flops 9450000384 | bytes 1024 | tf_op jit(solution)/shard_map/keep_grads/pallas_call | solution.py:243
  161.4 3.2 %collective-permute-done.36 = bf16[192,1536]{1,0:T(8,128)(2,1)S(1)} collective-permute-done((bf16[192,1536]{1,0:T(8,128)(2,1)S(1)}, bf16[192,1536]{1,0:T(8,128)(2,1)S(1)}, u32[]{:S(2)}, u32[]{:S(2)}) %collective-permute-start.36) | collective-permute-done | bytes 589856 | tf_op jit(solution)/shard_map/ppermute | solution.py:579
  166.8 10.6 %attend_backward.2 = (bf16[1024,1152]{1,0:T(8,128)(2,1)S(1)}, f32[8,384]{1,0:T(8,128)S(1)}) custom-call(s32[2]{0:T(128)S(1)} %copy-done.3, bf16[1024,1152]{1,0:T(8,128)(2,1)S(1)} %get-tuple-element.236.qkv_ref, bf16[1024,384]{1,0:T(8,128)(2,1)S(1)} %get-tuple-element.217.other_ref.refs_1_.refs_5_.context_ref, ...), custom_call_target="tpu_custom_call" | custom-call | flops 18000000 | bytes 1024 | tf_op jit(solution)/shard_map/attend_backward/pallas_call | solution.py:219
  180.9 2.4 collective-permute-done.37
  188.2 2.6 %collective-permute-done.43 = bf16[48,1536]{1,0:T(8,128)(2,1)S(1)} collective-permute-done((bf16[48,1536]{1,0:T(8,128)(2,1)S(1)}, bf16[48,1536]{1,0:T(8,128)(2,1)S(1)}, u32[]{:S(2)}, u32[]{:S(2)}) %collective-permute-start.43) | collective-permute-done | bytes 147488 | tf_op jit(solution)/shard_map/ppermute | solution.py:572
  190.8 3.7 %collective-permute-done.42 = bf16[192,896]{1,0:T(8,128)(2,1)S(1)} collective-permute-done((bf16[192,896]{1,0:T(8,128)(2,1)S(1)}, bf16[192,896]{1,0:T(8,128)(2,1)S(1)}, u32[]{:S(2)}, u32[]{:S(2)}) %collective-permute-start.42) | collective-permute-done | bytes 344096 | tf_op jit(solution)/shard_map/ppermute | solution.py:575
  200.3 10.6 %attend_backward.3 = (bf16[1024,1152]{1,0:T(8,128)(2,1)S(1)}, f32[8,384]{1,0:T(8,128)S(1)}) custom-call(s32[2]{0:T(128)S(1)} %copy-done.3, bf16[1024,1152]{1,0:T(8,128)(2,1)S(1)} %get-tuple-element.235.qkv_ref, bf16[1024,384]{1,0:T(8,128)(2,1)S(1)} %get-tuple-element.216.own_ref.refs_0_.refs_4_.context_ref, ...), custom_call_target="tpu_custom_call" | custom-call | flops 18000000 | bytes 1024 | tf_op jit(solution)/shard_map/attend_backward/pallas_call | solution.py:219
  212.4 8.3 %d_inputs.2.refs_9_ = f32[1024,768]{1,0:T(8,128)} custom-call(f32[1024,768]{1,0:T(8,128)S(1)} %get-tuple-element.311.d_summed_ref, bf16[1024,1152]{1,0:T(8,128)(2,1)S(1)} %get-tuple-element.321.refs_0_.own_ref.refs_1_, bf16[1024,1152]{1,0:T(8,128)(2,1)S(1)} %get-tuple-element.290.refs_0_.refs_1_.other_ref, bf16[192,1536]{1,0:T(8,128)(2,1)S(1)} %join.3.a_ref.refs_0_, ...), custom_call_target="tpu_custom_call" | custom-call | flops 18000000 | bytes 1024 | tf_op jit(solution)/shard_map/d_inputs/pallas_call | solution.py:497
  231.3 8.1 %d_inputs.3 = f32[1024,768]{1,0:T(8,128)} custom-call(f32[1024,768]{1,0:T(8,128)S(1)} %get-tuple-element.311.d_summed_ref, bf16[1024,1152]{1,0:T(8,128)(2,1)S(1)} %get-tuple-element.321.refs_0_.own_ref.refs_1_, bf16[1024,1152]{1,0:T(8,128)(2,1)S(1)} %get-tuple-element.290.refs_0_.refs_1_.other_ref, ...), custom_call_target="tpu_custom_call", output_to_operand_aliasing={{}: (12, {})} | custom-call | flops 18000000 | bytes 1024 | tf_op jit(solution)/shard_map/d_inputs/pallas_call | solution.py:497
  244.3 2.3 collective-permute-start.55
  251.2 4.2 %collective-permute-done.54 = bf16[48,1152]{1,0:T(8,128)(2,1)S(1)} collective-permute-done((bf16[48,1152]{1,0:T(8,128)(2,1)S(1)}, bf16[48,1152]{1,0:T(8,128)(2,1)S(1)}, u32[]{:S(2)}, u32[]{:S(2)}) %collective-permute-start.54) | collective-permute-done | bytes 110624 | tf_op jit(solution)/shard_map/ppermute | solution.py:572
  (223 shorter events, 78.5 us)
Async XLA Ops:
  4.4 11.7 %collective-permute-start.2 = (bf16[48,1536]{1,0:T(8,128)(2,1)S(1)}, bf16[48,1536]{1,0:T(8,128)(2,1)}, u32[]{:S(2)}, u32[]{:S(2)}) collective-permute-start(bf16[48,1536]{1,0:T(8,128)(2,1)S(1)} %pad_maximum_fusion.3.refs_0_), channel_id=1, source_target_pairs={{0,24},{2,26},{4,28},{6,30},{8,16},{10,18},{12,20},{14,22},{16,8},... | collective-permute-start | bytes 442376 | tf_op jit(solution)/shard_map/ppermute | solution.py:572
  9.5 12.6 %collective-permute-start.1 = (bf16[48,1536]{1,0:T(8,128)(2,1)S(1)}, bf16[48,1536]{1,0:T(8,128)(2,1)}, u32[]{:S(2)}, u32[]{:S(2)}) collective-permute-start(bf16[48,1536]{1,0:T(8,128)(2,1)S(1)} %pad_maximum_fusion.3.refs_0_), channel_id=1, source_target_pairs={{0,16},{2,18},{4,20},{6,22},{8,24},{10,26},{12,28},{14,30},{16,0},... | collective-permute-start | bytes 442376 | tf_op jit(solution)/shard_map/ppermute | solution.py:572
  9.5 12.6 %collective-permute-start = (bf16[48,1536]{1,0:T(8,128)(2,1)S(1)}, bf16[48,1536]{1,0:T(8,128)(2,1)}, u32[]{:S(2)}, u32[]{:S(2)}) collective-permute-start(bf16[48,1536]{1,0:T(8,128)(2,1)S(1)} %pad_maximum_fusion.3.refs_0_), channel_id=1, source_target_pairs={{0,8},{2,10},{4,12},{6,14},{8,0},{10,2},{12,4},{14,6},{16,24},{18,... | collective-permute-start | bytes 442376 | tf_op jit(solution)/shard_map/ppermute | solution.py:572
  23.2 17.3 %collective-permute-start.5 = (bf16[192,1536]{1,0:T(8,128)(2,1)S(1)}, bf16[192,1536]{1,0:T(8,128)(2,1)S(1)}, u32[]{:S(2)}, u32[]{:S(2)}) collective-permute-start(bf16[192,1536]{1,0:T(8,128)(2,1)S(1)} %join.3.a_ref.refs_0_), channel_id=1, source_target_pairs={{0,1},{1,0},{2,3},{3,2},{4,5},{5,4},{6,7},{7,6},{8,9},{9,8},{10,11... | collective-permute-start | bytes 1769480 | tf_op jit(solution)/shard_map/ppermute | solution.py:575
  24.7 15.7 %collective-permute-start.4 = (bf16[192,1536]{1,0:T(8,128)(2,1)S(1)}, bf16[192,1536]{1,0:T(8,128)(2,1)}, u32[]{:S(2)}, u32[]{:S(2)}) collective-permute-start(bf16[192,1536]{1,0:T(8,128)(2,1)S(1)} %join.3.a_ref.refs_0_), channel_id=1, source_target_pairs={{0,4},{2,6},{4,0},{6,2},{8,12},{10,14},{12,8},{14,10},{16,20},{18,... | collective-permute-start | bytes 1769480 | tf_op jit(solution)/shard_map/ppermute | solution.py:572
  29.3 11.1 %collective-permute-start.7 = (bf16[48,1536]{1,0:T(8,128)(2,1)S(1)}, bf16[48,1536]{1,0:T(8,128)(2,1)S(1)}, u32[]{:S(2)}, u32[]{:S(2)}) collective-permute-start(bf16[48,1536]{1,0:T(8,128)(2,1)S(1)} %convert_element_type.93.refs_0_), channel_id=1, source_target_pairs={{0,16},{2,18},{4,20},{6,22},{8,24},{10,26},{12,28},{14,30},{16,0},... | collective-permute-start | bytes 442376 | tf_op jit(solution)/shard_map/ppermute | solution.py:572
  29.3 11.1 %collective-permute-start.6 = (bf16[48,1536]{1,0:T(8,128)(2,1)S(1)}, bf16[48,1536]{1,0:T(8,128)(2,1)S(1)}, u32[]{:S(2)}, u32[]{:S(2)}) collective-permute-start(bf16[48,1536]{1,0:T(8,128)(2,1)S(1)} %convert_element_type.93.refs_0_), channel_id=1, source_target_pairs={{0,8},{2,10},{4,12},{6,14},{8,0},{10,2},{12,4},{14,6},{16,24},{18,... | collective-permute-start | bytes 442376 | tf_op jit(solution)/shard_map/ppermute | solution.py:572
  41.1 18.2 %collective-permute-start.13 = (bf16[48,1536]{1,0:T(8,128)(2,1)S(1)}, bf16[48,1536]{1,0:T(8,128)(2,1)S(1)}, u32[]{:S(2)}, u32[]{:S(2)}) collective-permute-start(bf16[48,1536]{1,0:T(8,128)(2,1)S(1)} %convert_bitcast_fusion.refs_0_), channel_id=1, source_target_pairs={{0,24},{2,26},{4,28},{6,30},{8,16},{10,18},{12,20},{14,22},{16,8},... | collective-permute-start | bytes 442376 | tf_op jit(solution)/shard_map/ppermute | solution.py:572
  42.6 16.7 %collective-permute-start.12 = (bf16[48,1536]{1,0:T(8,128)(2,1)S(1)}, bf16[48,1536]{1,0:T(8,128)(2,1)S(1)}, u32[]{:S(2)}, u32[]{:S(2)}) collective-permute-start(bf16[48,1536]{1,0:T(8,128)(2,1)S(1)} %convert_bitcast_fusion.refs_0_), channel_id=1, source_target_pairs={{0,16},{2,18},{4,20},{6,22},{8,24},{10,26},{12,28},{14,30},{16,0},... | collective-permute-start | bytes 442376 | tf_op jit(solution)/shard_map/ppermute | solution.py:572
  42.6 16.7 %collective-permute-start.11 = (bf16[48,1536]{1,0:T(8,128)(2,1)S(1)}, bf16[48,1536]{1,0:T(8,128)(2,1)S(1)}, u32[]{:S(2)}, u32[]{:S(2)}) collective-permute-start(bf16[48,1536]{1,0:T(8,128)(2,1)S(1)} %convert_bitcast_fusion.refs_0_), channel_id=1, source_target_pairs={{0,8},{2,10},{4,12},{6,14},{8,0},{10,2},{12,4},{14,6},{16,24},{18,... | collective-permute-start | bytes 442376 | tf_op jit(solution)/shard_map/ppermute | solution.py:572
  45.6 14.8 %collective-permute-start.9 = (bf16[192,1536]{1,0:T(8,128)(2,1)}, bf16[192,1536]{1,0:T(8,128)(2,1)S(1)}, u32[]{:S(2)}, u32[]{:S(2)}) collective-permute-start(bf16[192,1536]{1,0:T(8,128)(2,1)} %collective-permute-done.4.b_ref.refs_1_), channel_id=1, source_target_pairs={{0,1},{1,0},{2,3},{3,2},{4,5},{5,4},{6,7},{7,6},{8,9},{9,8},{10,11... | collective-permute-start | bytes 1769480 | tf_op jit(solution)/shard_map/ppermute | solution.py:575
  46.2 14.2 %collective-permute-start.10 = (bf16[192,1536]{1,0:T(8,128)(2,1)S(1)}, bf16[192,1536]{1,0:T(8,128)(2,1)S(1)}, u32[]{:S(2)}, u32[]{:S(2)}) collective-permute-start(bf16[192,1536]{1,0:T(8,128)(2,1)S(1)} %join.4.refs_0_), channel_id=1, source_target_pairs={{0,4},{2,6},{4,0},{6,2},{8,12},{10,14},{12,8},{14,10},{16,20},{18,... | collective-permute-start | bytes 1769480 | tf_op jit(solution)/shard_map/ppermute | solution.py:572
  61.0 15.3 %collective-permute-start.17 = (bf16[192,1536]{1,0:T(8,128)(2,1)S(1)}, bf16[192,1536]{1,0:T(8,128)(2,1)S(1)}, u32[]{:S(2)}, u32[]{:S(2)}) collective-permute-start(bf16[192,1536]{1,0:T(8,128)(2,1)S(1)} %join.5.refs_0_), channel_id=1, source_target_pairs={{0,4},{2,6},{4,0},{6,2},{8,12},{10,14},{12,8},{14,10},{16,20},{18,... | collective-permute-start | bytes 1769480 | tf_op jit(solution)/shard_map/ppermute | solution.py:572
  61.6 15.0 %collective-permute-start.16 = (bf16[192,1536]{1,0:T(8,128)(2,1)S(1)}, bf16[192,1536]{1,0:T(8,128)(2,1)S(1)}, u32[]{:S(2)}, u32[]{:S(2)}) collective-permute-start(bf16[192,1536]{1,0:T(8,128)(2,1)S(1)} %join.4.refs_0_), channel_id=1, source_target_pairs={{0,1},{1,0},{2,3},{3,2},{4,5},{5,4},{6,7},{7,6},{8,9},{9,8},{10,11... | collective-permute-start | bytes 1769480 | tf_op jit(solution)/shard_map/ppermute | solution.py:575
  76.6 16.1 %collective-permute-start.20 = (bf16[192,1536]{1,0:T(8,128)(2,1)S(1)}, bf16[192,1536]{1,0:T(8,128)(2,1)S(1)}, u32[]{:S(2)}, u32[]{:S(2)}) collective-permute-start(bf16[192,1536]{1,0:T(8,128)(2,1)S(1)} %collective-permute-done.16.refs_0_.refs_4_), channel_id=1, source_target_pairs={{0,4},{2,6},{4,0},{6,2},{8,12},{10,14},{12,8},{14,10},{16,20},{18,... | collective-permute-start | bytes 1769480 | tf_op jit(solution)/shard_map/ppermute | solution.py:572
  78.1 14.7 %collective-permute-start.21 = (bf16[192,1536]{1,0:T(8,128)(2,1)S(1)}, bf16[192,1536]{1,0:T(8,128)(2,1)S(1)}, u32[]{:S(2)}, u32[]{:S(2)}) collective-permute-start(bf16[192,1536]{1,0:T(8,128)(2,1)S(1)} %join.5.refs_0_), channel_id=1, source_target_pairs={{0,1},{1,0},{2,3},{3,2},{4,5},{5,4},{6,7},{7,6},{8,9},{9,8},{10,11... | collective-permute-start | bytes 1769480 | tf_op jit(solution)/shard_map/ppermute | solution.py:575
  93.3 16.3 %collective-permute-start.28 = (bf16[192,1536]{1,0:T(8,128)(2,1)S(1)}, bf16[192,1536]{1,0:T(8,128)(2,1)S(1)}, u32[]{:S(2)}, u32[]{:S(2)}) collective-permute-start(bf16[192,1536]{1,0:T(8,128)(2,1)S(1)} %collective-permute-done.17.refs_1_), channel_id=1, source_target_pairs={{0,2},{2,0},{4,6},{6,4},{8,10},{10,8},{12,14},{14,12},{16,18},{18,... | collective-permute-start | bytes 1769480 | tf_op jit(solution)/shard_map/ppermute | solution.py:572
  93.5 15.7 %collective-permute-start.24 = (bf16[192,1536]{1,0:T(8,128)(2,1)S(1)}, bf16[192,1536]{1,0:T(8,128)(2,1)S(1)}, u32[]{:S(2)}, u32[]{:S(2)}) collective-permute-start(bf16[192,1536]{1,0:T(8,128)(2,1)S(1)} %collective-permute-done.17.refs_1_), channel_id=1, source_target_pairs={{0,1},{1,0},{2,3},{3,2},{4,5},{5,4},{6,7},{7,6},{8,9},{9,8},{10,11... | collective-permute-start | bytes 1769480 | tf_op jit(solution)/shard_map/ppermute | solution.py:575
  94.0 15.6 %collective-permute-start.27 = (bf16[192,1536]{1,0:T(8,128)(2,1)S(1)}, bf16[192,1536]{1,0:T(8,128)(2,1)S(1)}, u32[]{:S(2)}, u32[]{:S(2)}) collective-permute-start(bf16[192,1536]{1,0:T(8,128)(2,1)S(1)} %join.5.refs_0_), channel_id=1, source_target_pairs={{0,2},{2,0},{4,6},{6,4},{8,10},{10,8},{12,14},{14,12},{16,18},{18,... | collective-permute-start | bytes 1769480 | tf_op jit(solution)/shard_map/ppermute | solution.py:572
  135.3 26.0 %collective-permute-start.34 = (bf16[192,1536]{1,0:T(8,128)(2,1)S(1)}, bf16[192,1536]{1,0:T(8,128)(2,1)S(1)}, u32[]{:S(2)}, u32[]{:S(2)}) collective-permute-start(bf16[192,1536]{1,0:T(8,128)(2,1)S(1)} %get-tuple-element.273), channel_id=1, source_target_pairs={{0,4},{2,6},{4,0},{6,2},{8,12},{10,14},{12,8},{14,10},{16,20},{18,... | collective-permute-start | bytes 1769480 | tf_op jit(solution)/shard_map/ppermute | solution.py:572
  136.0 25.4 %collective-permute-start.35 = (bf16[192,1536]{1,0:T(8,128)(2,1)S(1)}, bf16[192,1536]{1,0:T(8,128)(2,1)S(1)}, u32[]{:S(2)}, u32[]{:S(2)}) collective-permute-start(bf16[192,1536]{1,0:T(8,128)(2,1)S(1)} %get-tuple-element.274), channel_id=1, source_target_pairs={{0,1},{1,0},{2,3},{3,2},{4,5},{5,4},{6,7},{7,6},{8,9},{9,8},{10,11... | collective-permute-start | bytes 1769480 | tf_op jit(solution)/shard_map/ppermute | solution.py:575
  136.6 27.9 %collective-permute-start.36 = (bf16[192,1536]{1,0:T(8,128)(2,1)S(1)}, bf16[192,1536]{1,0:T(8,128)(2,1)S(1)}, u32[]{:S(2)}, u32[]{:S(2)}) collective-permute-start(bf16[192,1536]{1,0:T(8,128)(2,1)S(1)} %get-tuple-element.275), channel_id=1, source_target_pairs={{0,5},{1,4},{2,7},{3,6},{4,1},{5,0},{6,3},{7,2},{8,13},{9,12},{10,... | collective-permute-start | bytes 1769480 | tf_op jit(solution)/shard_map/ppermute | solution.py:579
  145.2 12.6 %collective-permute-start.33 = (bf16[384,3072]{1,0:T(8,128)(2,1)S(1)}, bf16[384,3072]{1,0:T(8,128)(2,1)S(1)}, u32[]{:S(2)}, u32[]{:S(2)}) collective-permute-start(bf16[384,3072]{1,0:T(8,128)(2,1)S(1)} %send_grads.6), channel_id=1, source_target_pairs={{0,2},{2,0},{4,6},{6,4},{8,10},{10,8},{12,14},{14,12},{16,18},{18,... | collective-permute-start | bytes 7077896 | tf_op jit(solution)/shard_map/ppermute | solution.py:572
  164.6 16.3 %collective-permute-start.38 = (bf16[192,1792]{1,0:T(8,128)(2,1)S(1)}, bf16[192,1792]{1,0:T(8,128)(2,1)S(1)}, u32[]{:S(2)}, u32[]{:S(2)}) collective-permute-start(bf16[192,1792]{1,0:T(8,128)(2,1)S(1)} %get-tuple-element.280), channel_id=1, source_target_pairs={{0,4},{2,6},{4,0},{6,2},{8,12},{10,14},{12,8},{14,10},{16,20},{18,... | collective-permute-start | bytes 2064392 | tf_op jit(solution)/shard_map/ppermute | solution.py:572
  165.2 18.2 %collective-permute-start.37 = (bf16[384,1024]{1,0:T(8,128)(2,1)S(1)}, bf16[384,1024]{1,0:T(8,128)(2,1)S(1)}, u32[]{:S(2)}, u32[]{:S(2)}) collective-permute-start(bf16[384,1024]{1,0:T(8,128)(2,1)S(1)} %get-tuple-element.279), channel_id=1, source_target_pairs={{0,1},{1,0},{2,3},{3,2},{4,5},{5,4},{6,7},{7,6},{8,9},{9,8},{10,11... | collective-permute-start | bytes 2359304 | tf_op jit(solution)/shard_map/ppermute | solution.py:575
  166.2 12.6 %collective-permute-start.39 = (bf16[96,1536]{1,0:T(8,128)(2,1)S(1)}, bf16[96,1536]{1,0:T(8,128)(2,1)S(1)}, u32[]{:S(2)}, u32[]{:S(2)}) collective-permute-start(bf16[96,1536]{1,0:T(8,128)(2,1)S(1)} %pad_maximum_fusion.2), channel_id=1, source_target_pairs={{0,8},{2,10},{4,12},{6,14},{8,0},{10,2},{12,4},{14,6},{16,24},{18,... | collective-permute-start | bytes 884744 | tf_op jit(solution)/shard_map/ppermute | solution.py:572
  184.7 11.3 %collective-permute-start.41 = (bf16[192,1024]{1,0:T(8,128)(2,1)S(1)}, bf16[192,1024]{1,0:T(8,128)(2,1)S(1)}, u32[]{:S(2)}, u32[]{:S(2)}) collective-permute-start(bf16[192,1024]{1,0:T(8,128)(2,1)S(1)} %add_convert_fusion), channel_id=1, source_target_pairs={{0,4},{2,6},{4,0},{6,2},{8,12},{10,14},{12,8},{14,10},{16,20},{18,... | collective-permute-start | bytes 1179656 | tf_op jit(solution)/shard_map/ppermute | solution.py:572
  196.4 24.4 %collective-permute-start.45 = (bf16[384,1152]{1,0:T(8,128)(2,1)S(1)}, bf16[384,1152]{1,0:T(8,128)(2,1)S(1)}, u32[]{:S(2)}, u32[]{:S(2)}) collective-permute-start(bf16[384,1152]{1,0:T(8,128)(2,1)S(1)} %keep_grads.6), channel_id=1, source_target_pairs={{0,1},{1,0},{2,3},{3,2},{4,5},{5,4},{6,7},{7,6},{8,9},{9,8},{10,11... | collective-permute-start | bytes 2654216 | tf_op jit(solution)/shard_map/ppermute | solution.py:575
  197.9 22.8 %collective-permute-start.46 = (bf16[96,1920]{1,0:T(8,128)(2,1)S(1)}, bf16[96,1920]{1,0:T(8,128)(2,1)S(1)}, u32[]{:S(2)}, u32[]{:S(2)}) collective-permute-start(bf16[96,1920]{1,0:T(8,128)(2,1)S(1)} %pad_maximum_fusion.1), channel_id=1, source_target_pairs={{0,8},{2,10},{4,12},{6,14},{8,0},{10,2},{12,4},{14,6},{16,24},{18,... | collective-permute-start | bytes 1105928 | tf_op jit(solution)/shard_map/ppermute | solution.py:572
  199.7 21.0 %collective-permute-start.44 = (f32[16,768]{1,0:T(8,128)S(1)}, f32[16,768]{1,0:T(8,128)S(1)}, u32[]{:S(2)}, u32[]{:S(2)}) collective-permute-start(f32[16,768]{1,0:T(8,128)S(1)} %order.4), channel_id=1, source_target_pairs={{0,1},{1,0},{2,3},{3,2},{4,5},{5,4},{6,7},{7,6},{8,9},{9,8},{10,11... | collective-permute-start | bytes 147464 | tf_op jit(solution)/shard_map/ppermute | solution.py:575
  222.7 16.6 %collective-permute-start.52 = (bf16[48,1920]{1,0:T(8,128)(2,1)S(1)}, bf16[48,1920]{1,0:T(8,128)(2,1)S(1)}, u32[]{:S(2)}, u32[]{:S(2)}) collective-permute-start(bf16[48,1920]{1,0:T(8,128)(2,1)S(1)} %add_convert_fusion.2), channel_id=1, source_target_pairs={{0,16},{2,18},{4,20},{6,22},{8,24},{10,26},{12,28},{14,30},{16,0},... | collective-permute-start | bytes 552968 | tf_op jit(solution)/shard_map/ppermute | solution.py:572
  228.0 11.4 %collective-permute-start.51 = (f32[16,768]{1,0:T(8,128)S(1)}, f32[16,768]{1,0:T(8,128)S(1)}, u32[]{:S(2)}, u32[]{:S(2)}) collective-permute-start(f32[16,768]{1,0:T(8,128)S(1)} %add.101), channel_id=1, source_target_pairs={{0,8},{2,10},{4,12},{6,14},{8,0},{10,2},{12,4},{14,6},{16,24},{18,... | collective-permute-start | bytes 147464 | tf_op jit(solution)/shard_map/ppermute | solution.py:572
  (49 other events, 324.6 us)

commit v6 on v5

--- a/solution.py
+++ b/solution.py
@@ -711,7 +711,7 @@
     across_inner, corner_inner, far_outer, near_outer, across_outer, normed16, hidden_own = gate(
         (across_inner, corner_inner, far_outer, near_outer, across_outer, normed16, hidden_own)
     )
-    corner_outer = cross(near_outer)
+    corner_outer = flip(across_outer, 2)
     pair_across_inner, pair_corner_inner = flip(across_inner, 1), flip(corner_inner, 1)
     pair_far_outer, pair_near_outer = flip(far_outer, 1), flip(near_outer, 1)
     inner_other = (across_inner, corner_inner, pair_across_inner, pair_corner_inner)

time: 260 us -> 260 us (level)
    ppermute x11 -> x10, waiting for transfers between devices: 11.9 us -> 6.46 us  [cross(): return lax.ppermute(array, 'tp', [(0, 1), (1, 0)])]
    ppermute x45 -> x46, waiting for transfers between devices: 33.7 us -> 38.5 us  [flip(): return lax.ppermute(array, 'fsdp', [(i, i ^ bit) for i in range(self.fsdp)])]
    ppermute x45 -> x46, starting transfers between devices: 38.8 us -> 39.7 us  [flip(): return lax.ppermute(array, 'fsdp', [(i, i ^ bit) for i in range(self.fsdp)])]
    ppermute x11 -> x10, starting transfers between devices: 11.4 us -> 10.6 us  [cross(): return lax.ppermute(array, 'tp', [(0, 1), (1, 0)])]
where the time goes in v6:
time: 260 us; the launch traced here: 256 us
  Pallas kernels  137 us (53%)
  starting transfers between devices  52.7 us (20%)
  waiting for transfers between devices  48.2 us (19%)
  other arithmetic  8.63 us (3%)
  local copies, waits for them, and re-layouts  6.18 us (2%)
    pallas_call x23, Pallas kernels, in_vmem(): pl.pallas_call(kernel, in_specs=[pl.BlockSpec(memory_space=pltpu.VMEM)] *...  75.1 us
    ppermute x46, starting transfers between devices, flip(): return lax.ppermute(array, 'fsdp', [(i, i ^ bit) for i in range(self.fsdp)])  39.7 us
    ppermute x46, waiting for transfers between devices, flip(): return lax.ppermute(array, 'fsdp', [(i, i ^ bit) for i in range(self.fsdp)])  38.5 us
    pallas_call x2, Pallas kernels, attend_forward(): pl.pallas_call(functools.partial(attend_forward_kernel, pairs), grid_spec...  24.2 us
    pallas_call x2, Pallas kernels, attend_backward(): pl.pallas_call(functools.partial(attend_backward_kernel, pairs), grid_spe...  21.2 us
    pallas_call x2, Pallas kernels, d_inputs(): pl.pallas_call(d_inputs_kernel, grid=(steps,), in_specs=[tile(model), til...  16.4 us
    ppermute x10, starting transfers between devices, cross(): return lax.ppermute(array, 'tp', [(0, 1), (1, 0)])  10.6 us
    ppermute x10, waiting for transfers between devices, cross(): return lax.ppermute(array, 'tp', [(0, 1), (1, 0)])  6.46 us
  transfers between devices with their start and end apart: 57, of which 24 were waited for; matrix products, arithmetic and copies ran while one was open for 4% of the time, Pallas kernels for 46%

profile of v6, /device:TPU:0, one launch (start us, length us, event | category | flops | bytes accessed | tf_op | source)
XLA Modules:
  0.0 255.9 jit_solution(10529017853443186836)
XLA Ops:
  4.4 5.1 %collective-permute-start.2 = (bf16[48,1536]{1,0:T(8,128)(2,1)S(1)}, bf16[48,1536]{1,0:T(8,128)(2,1)}, u32[]{:S(2)}, u32[]{:S(2)}) collective-permute-start(bf16[48,1536]{1,0:T(8,128)(2,1)S(1)} %pad_maximum_fusion.3.refs_0_), channel_id=1, source_target_pairs={{0,24},{2,26},{4,28},{6,30},{8,16},{10,18},{12,20},{14,22},{16,8},... | collective-permute-start | bytes 442376 | tf_op jit(solution)/shard_map/ppermute | solution.py:572
  16.1 6.0 %collective-permute-done.1.refs_2_ = bf16[48,1536]{1,0:T(8,128)(2,1)} collective-permute-done((bf16[48,1536]{1,0:T(8,128)(2,1)S(1)}, bf16[48,1536]{1,0:T(8,128)(2,1)}, u32[]{:S(2)}, u32[]{:S(2)}) %collective-permute-start.1) | collective-permute-done | bytes 147488 | tf_op jit(solution)/shard_map/ppermute | solution.py:572
  26.8 2.6 %collective-permute-start.8 = (bf16[48,1536]{1,0:T(8,128)(2,1)S(1)}, bf16[48,1536]{1,0:T(8,128)(2,1)S(1)}, u32[]{:S(2)}, u32[]{:S(2)}) collective-permute-start(bf16[48,1536]{1,0:T(8,128)(2,1)S(1)} %convert_element_type.93.refs_0_), channel_id=1, source_target_pairs={{0,24},{2,26},{4,28},{6,30},{8,16},{10,18},{12,20},{14,22},{16,8},... | collective-permute-start | bytes 442376 | tf_op jit(solution)/shard_map/ppermute | solution.py:572
  32.6 2.7 %order.3 = (bf16[1024,768]{1,0:T(8,128)(2,1)S(1)}, f32[8,768]{1,0:T(8,128)S(1)}) custom-call(bf16[1024,768]{1,0:T(8,128)(2,1)S(1)} %copy-done.4, f32[8,768]{1,0:T(8,128)S(1)} %stack.29.vectors_ref, bf16[768,768]{1,0:T(8,128)(2,1)S(1)} %fusion.place_ref.refs_11_.refs_8_), custom_call_target="tpu_custom_call" | custom-call | flops 2700000000 | bytes 1024 | tf_op jit(solution)/shard_map/order/pallas_call | solution.py:243
  35.4 5.1 %collective-permute-done.7.refs_2_ = bf16[48,1536]{1,0:T(8,128)(2,1)S(1)} collective-permute-done((bf16[48,1536]{1,0:T(8,128)(2,1)S(1)}, bf16[48,1536]{1,0:T(8,128)(2,1)S(1)}, u32[]{:S(2)}, u32[]{:S(2)}) %collective-permute-start.7) | collective-permute-done | bytes 147488 | tf_op jit(solution)/shard_map/ppermute | solution.py:572
  42.6 2.9 %collective-permute-start.11 = (bf16[48,1536]{1,0:T(8,128)(2,1)S(1)}, bf16[48,1536]{1,0:T(8,128)(2,1)S(1)}, u32[]{:S(2)}, u32[]{:S(2)}) collective-permute-start(bf16[48,1536]{1,0:T(8,128)(2,1)S(1)} %convert_bitcast_fusion.refs_0_), channel_id=1, source_target_pairs={{0,8},{2,10},{4,12},{6,14},{8,0},{10,2},{12,4},{14,6},{16,24},{18,... | collective-permute-start | bytes 442376 | tf_op jit(solution)/shard_map/ppermute | solution.py:572
  46.7 12.6 %attend_forward.2 = (bf16[1024,1152]{1,0:T(8,128)(2,1)S(1)}, bf16[1024,384]{1,0:T(8,128)(2,1)S(1)}, f32[2,6,512]{2,1,0:T(8,128)S(1)}) custom-call(s32[2]{0:T(128)S(1)} %dynamic_slice.3.lengths_ref, bf16[1024,768]{1,0:T(8,128)(2,1)S(1)} %fusion.3.inputs_ref.refs_8_.left_ref.refs_0_, bf16[192,1536]{1,0:T(8,128)(2,1)S(1)} %join.3.a_ref.refs_0_, ...), custom_call_target="tpu_custom_call" | custom-call | flops 35100000256 | bytes 1024 | tf_op jit(solution)/shard_map/attend_forward/pallas_call | solution.py:147
  63.3 11.7 %attend_forward.3 = (bf16[1024,1152]{1,0:T(8,128)(2,1)S(1)}, bf16[1024,384]{1,0:T(8,128)(2,1)S(1)}, f32[2,6,512]{2,1,0:T(8,128)S(1)}) custom-call(s32[2]{0:T(128)S(1)} %dynamic_slice.3.lengths_ref, bf16[1024,768]{1,0:T(8,128)(2,1)S(1)} %fusion.3.inputs_ref.refs_8_.left_ref.refs_0_, bf16[192,1536]{1,0:T(8,128)(2,1)S(1)} %collective-permute-done.5.a_ref.refs_4_, ...), custom_call_target="tpu_custom_call" | custom-call | flops 35100000256 | bytes 1024 | tf_op jit(solution)/shard_map/attend_forward/pallas_call | solution.py:147
  80.1 4.6 %attention_out.1 = (f32[1024,768]{1,0:T(8,128)S(1)}, f32[1024,1]{1,0:T(8,128)S(1)}, bf16[1024,768]{1,0:T(8,128)(2,1)S(1)}) custom-call(bf16[1024,384]{1,0:T(8,128)(2,1)S(1)} %get-tuple-element.216.own_ref.refs_0_.refs_4_.context_ref, bf16[1024,384]{1,0:T(8,128)(2,1)S(1)} %get-tuple-element.217.other_ref.refs_1_.refs_5_.context_ref, ...), custom_call_target="tpu_custom_call" | custom-call | flops 10800000000 | bytes 1024 | tf_op jit(solution)/shard_map/attention_out/pallas_call | solution.py:243
  84.7 8.0 %hidden.2 = (bf16[1024,1536]{1,0:T(8,128)(2,1)S(1)}, bf16[1024,1536]{1,0:T(8,128)(2,1)S(1)}) custom-call(bf16[1024,768]{1,0:T(8,128)(2,1)S(1)} %get-tuple-element.261.normed_ref.left_ref.refs_0_, bf16[192,1536]{1,0:T(8,128)(2,1)S(1)} %join.4.refs_0_, bf16[192,1536]{1,0:T(8,128)(2,1)S(1)} %collective-permute-done.10.refs_1_, ...), custom_call_target="tpu_custom_call" | custom-call | flops 22950000640 | bytes 1024 | tf_op jit(solution)/shard_map/hidden/pallas_call | solution.py:243
  95.6 8.0 %hidden.3 = (bf16[1024,1536]{1,0:T(8,128)(2,1)S(1)}, bf16[1024,1536]{1,0:T(8,128)(2,1)S(1)}) custom-call(bf16[1024,768]{1,0:T(8,128)(2,1)S(1)} %get-tuple-element.261.normed_ref.left_ref.refs_0_, bf16[192,1536]{1,0:T(8,128)(2,1)S(1)} %collective-permute-done.16.refs_0_.refs_4_, bf16[192,1536]{1,0:T(8,128)(2,1)S(1)} %collective-permute-done.20.refs_1_.refs_5_, ...), custom_call_target="tpu_custom_call" | custom-call | flops 22950000640 | bytes 1024 | tf_op jit(solution)/shard_map/hidden/pallas_call | solution.py:243
  103.6 5.1 %collective-permute-done.24.refs_5_.refs_1_ = bf16[192,1536]{1,0:T(8,128)(2,1)S(1)} collective-permute-done((bf16[192,1536]{1,0:T(8,128)(2,1)S(1)}, bf16[192,1536]{1,0:T(8,128)(2,1)S(1)}, u32[]{:S(2)}, u32[]{:S(2)}) %collective-permute-start.24) | collective-permute-done | bytes 589856 | tf_op jit(solution)/shard_map/ppermute | solution.py:572
  111.5 13.5 %turn.1 = (bf16[1024,768]{1,0:T(8,128)(2,1)}, f32[1024,768]{1,0:T(8,128)S(1)}, bf16[1024,768]{1,0:T(8,128)(2,1)S(1)}, f32[8,768]{1,0:T(8,128)S(1)}) custom-call(bf16[1024,1536]{1,0:T(8,128)(2,1)S(1)} %get-tuple-element.222.own_ref.refs_0_.refs_1_, ...), custom_call_target="tpu_custom_call", output_to_operand_aliasing={{2}: (11, {})} | custom-call | flops 35100000256 | bytes 1024 | tf_op jit(solution)/shard_map/turn/pallas_call | solution.py:243
  125.0 2.6 %send_grads.5 = bf16[384,3072]{1,0:T(8,128)(2,1)S(1)} custom-call(bf16[1024,768]{1,0:T(8,128)(2,1)S(1)} %get-tuple-element.249.left_ref.d_ffn_ref.refs_0_, bf16[1024,1536]{1,0:T(8,128)(2,1)S(1)} %get-tuple-element.222.own_ref.refs_0_.refs_1_, bf16[1024,1536]{1,0:T(8,128)(2,1)S(1)} %get-tuple-element.228.other_ref.refs_1_.refs_2_), custom_call_target="tpu_custom_call" | custom-call | flops 18000000 | bytes 1024 | tf_op jit(solution)/shard_map/send_grads/pallas_call | solution.py:243
  127.9 3.7 %d_hidden.2 = (bf16[1024,1536]{1,0:T(8,128)(2,1)S(1)}, f32[8,1536]{1,0:T(8,128)S(1)}) custom-call(bf16[1024,768]{1,0:T(8,128)(2,1)S(1)} %get-tuple-element.249.left_ref.d_ffn_ref.refs_0_, bf16[192,1536]{1,0:T(8,128)(2,1)S(1)} %join.5.refs_0_, bf16[192,1536]{1,0:T(8,128)(2,1)S(1)} %collective-permute-done.17.refs_1_, ...), custom_call_target="tpu_custom_call", output_to_operand_aliasing={{0}: (5, {})} | custom-call | flops 9720000512 | bytes 1024 | tf_op jit(solution)/shard_map/d_hidden/pallas_call | solution.py:243
  132.3 2.6 %keep_grads.4 = (f32[192,1536]{1,0:T(8,128)S(1)}, bf16[192,1536]{1,0:T(8,128)(2,1)S(1)}, bf16[192,1536]{1,0:T(8,128)(2,1)S(1)}, bf16[192,1536]{1,0:T(8,128)(2,1)S(1)}) custom-call(bf16[1024,768]{1,0:T(8,128)(2,1)S(1)} %get-tuple-element.249.left_ref.d_ffn_ref.refs_0_, bf16[1024,1536]{1,0:T(8,128)(2,1)S(1)} %get-tuple-element.222.own_ref.refs_0_.refs_1_, ...), custom_call_target="tpu_custom_call" | custom-call | flops 9450000384 | bytes 1024 | tf_op jit(solution)/shard_map/keep_grads/pallas_call | solution.py:243
  136.1 2.3 collective-permute-start.36
  138.4 3.7 %d_hidden.3 = (bf16[1024,1536]{1,0:T(8,128)(2,1)S(1)}, f32[8,1536]{1,0:T(8,128)S(1)}) custom-call(bf16[1024,768]{1,0:T(8,128)(2,1)S(1)} %get-tuple-element.249.left_ref.d_ffn_ref.refs_0_, bf16[192,1536]{1,0:T(8,128)(2,1)S(1)} %collective-permute-done.21.refs_4_.refs_0_, ...), custom_call_target="tpu_custom_call", output_to_operand_aliasing={{0}: (5, {})} | custom-call | flops 9720000512 | bytes 1024 | tf_op jit(solution)/shard_map/d_hidden/pallas_call | solution.py:243
  142.2 2.6 %send_grads.6 = bf16[384,3072]{1,0:T(8,128)(2,1)S(1)} custom-call(bf16[1024,768]{1,0:T(8,128)(2,1)S(1)} %get-tuple-element.261.normed_ref.left_ref.refs_0_, bf16[1024,1536]{1,0:T(8,128)(2,1)S(1)} %get-tuple-element.242.refs_0_.own_ref.refs_2_, bf16[1024,1536]{1,0:T(8,128)(2,1)S(1)} %get-tuple-element.252.refs_1_.other_ref.refs_3_), custom_call_target="tpu_custom_call" | custom-call | flops 18000000 | bytes 1024 | tf_op jit(solution)/shard_map/send_grads/pallas_call | solution.py:243
  144.9 7.4 %d_attention.1 = (f32[1024,768]{1,0:T(8,128)S(1)}, bf16[1024,768]{1,0:T(8,128)(2,1)S(1)}, f32[8,768]{1,0:T(8,128)S(1)}) custom-call(bf16[1024,1536]{1,0:T(8,128)(2,1)S(1)} %get-tuple-element.242.refs_0_.own_ref.refs_2_, bf16[1024,1536]{1,0:T(8,128)(2,1)S(1)} %get-tuple-element.252.refs_1_.other_ref.refs_3_, ...), custom_call_target="tpu_custom_call", output_to_operand_aliasing={{0}: (10, {})} | custom-call | flops 27000000512 | bytes 1024 | tf_op jit(solution)/shard_map/d_attention/pallas_call | solution.py:243
  153.9 3.5 %d_context.1 = (bf16[1024,384]{1,0:T(8,128)(2,1)S(1)}, bf16[1024,384]{1,0:T(8,128)(2,1)S(1)}) custom-call(bf16[1024,768]{1,0:T(8,128)(2,1)S(1)} %get-tuple-element.262.left_ref.d_attn_ref.refs_1_, bf16[192,1536]{1,0:T(8,128)(2,1)S(1)} %join.3.a_ref.refs_0_, bf16[192,1536]{1,0:T(8,128)(2,1)} %collective-permute-done.4.b_ref.refs_1_, ...), custom_call_target="tpu_custom_call" | custom-call | flops 17999998976 | bytes 1024 | tf_op jit(solution)/shard_map/d_context/pallas_call | solution.py:243
  157.4 3.5 %keep_grads.5 = (f32[192,1024]{1,0:T(8,128)S(1)}, f32[192,1024]{1,0:T(8,128)S(1)}, bf16[384,1024]{1,0:T(8,128)(2,1)S(1)}, f32[192,896]{1,0:T(8,128)S(1)}, f32[19...) custom-call(bf16[1024,768]{1,0:T(8,128)(2,1)S(1)} %get-tuple-element.261.normed_ref.left_ref.refs_0_, ...), custom_call_target="tpu_custom_call" | custom-call | flops 9450000384 | bytes 1024 | tf_op jit(solution)/shard_map/keep_grads/pallas_call | solution.py:243
  160.9 3.2 %collective-permute-done.36 = bf16[192,1536]{1,0:T(8,128)(2,1)S(1)} collective-permute-done((bf16[192,1536]{1,0:T(8,128)(2,1)S(1)}, bf16[192,1536]{1,0:T(8,128)(2,1)S(1)}, u32[]{:S(2)}, u32[]{:S(2)}) %collective-permute-start.36) | collective-permute-done | bytes 589856 | tf_op jit(solution)/shard_map/ppermute | solution.py:579
  166.3 10.6 %attend_backward.2 = (bf16[1024,1152]{1,0:T(8,128)(2,1)S(1)}, f32[8,384]{1,0:T(8,128)S(1)}) custom-call(s32[2]{0:T(128)S(1)} %copy-done.3, bf16[1024,1152]{1,0:T(8,128)(2,1)S(1)} %get-tuple-element.236.qkv_ref, bf16[1024,384]{1,0:T(8,128)(2,1)S(1)} %get-tuple-element.217.other_ref.refs_1_.refs_5_.context_ref, ...), custom_call_target="tpu_custom_call" | custom-call | flops 18000000 | bytes 1024 | tf_op jit(solution)/shard_map/attend_backward/pallas_call | solution.py:219
  180.5 2.4 collective-permute-done.37
  187.7 2.6 %collective-permute-done.43 = bf16[48,1536]{1,0:T(8,128)(2,1)S(1)} collective-permute-done((bf16[48,1536]{1,0:T(8,128)(2,1)S(1)}, bf16[48,1536]{1,0:T(8,128)(2,1)S(1)}, u32[]{:S(2)}, u32[]{:S(2)}) %collective-permute-start.43) | collective-permute-done | bytes 147488 | tf_op jit(solution)/shard_map/ppermute | solution.py:572
  190.3 3.7 %collective-permute-done.42 = bf16[192,896]{1,0:T(8,128)(2,1)S(1)} collective-permute-done((bf16[192,896]{1,0:T(8,128)(2,1)S(1)}, bf16[192,896]{1,0:T(8,128)(2,1)S(1)}, u32[]{:S(2)}, u32[]{:S(2)}) %collective-permute-start.42) | collective-permute-done | bytes 344096 | tf_op jit(solution)/shard_map/ppermute | solution.py:575
  199.9 10.6 %attend_backward.3 = (bf16[1024,1152]{1,0:T(8,128)(2,1)S(1)}, f32[8,384]{1,0:T(8,128)S(1)}) custom-call(s32[2]{0:T(128)S(1)} %copy-done.3, bf16[1024,1152]{1,0:T(8,128)(2,1)S(1)} %get-tuple-element.235.qkv_ref, bf16[1024,384]{1,0:T(8,128)(2,1)S(1)} %get-tuple-element.216.own_ref.refs_0_.refs_4_.context_ref, ...), custom_call_target="tpu_custom_call" | custom-call | flops 18000000 | bytes 1024 | tf_op jit(solution)/shard_map/attend_backward/pallas_call | solution.py:219
  211.9 8.3 %d_inputs.2.refs_9_ = f32[1024,768]{1,0:T(8,128)} custom-call(f32[1024,768]{1,0:T(8,128)S(1)} %get-tuple-element.311.d_summed_ref, bf16[1024,1152]{1,0:T(8,128)(2,1)S(1)} %get-tuple-element.321.refs_0_.own_ref.refs_1_, bf16[1024,1152]{1,0:T(8,128)(2,1)S(1)} %get-tuple-element.290.refs_0_.refs_1_.other_ref, bf16[192,1536]{1,0:T(8,128)(2,1)S(1)} %join.3.a_ref.refs_0_, ...), custom_call_target="tpu_custom_call" | custom-call | flops 18000000 | bytes 1024 | tf_op jit(solution)/shard_map/d_inputs/pallas_call | solution.py:497
  230.8 8.1 %d_inputs.3 = f32[1024,768]{1,0:T(8,128)} custom-call(f32[1024,768]{1,0:T(8,128)S(1)} %get-tuple-element.311.d_summed_ref, bf16[1024,1152]{1,0:T(8,128)(2,1)S(1)} %get-tuple-element.321.refs_0_.own_ref.refs_1_, bf16[1024,1152]{1,0:T(8,128)(2,1)S(1)} %get-tuple-element.290.refs_0_.refs_1_.other_ref, ...), custom_call_target="tpu_custom_call", output_to_operand_aliasing={{}: (12, {})} | custom-call | flops 18000000 | bytes 1024 | tf_op jit(solution)/shard_map/d_inputs/pallas_call | solution.py:497
  243.8 2.3 collective-permute-start.55
  250.7 4.2 %collective-permute-done.54 = bf16[48,1152]{1,0:T(8,128)(2,1)S(1)} collective-permute-done((bf16[48,1152]{1,0:T(8,128)(2,1)S(1)}, bf16[48,1152]{1,0:T(8,128)(2,1)S(1)}, u32[]{:S(2)}, u32[]{:S(2)}) %collective-permute-start.54) | collective-permute-done | bytes 110624 | tf_op jit(solution)/shard_map/ppermute | solution.py:572
  (223 shorter events, 78.4 us)
Async XLA Ops:
  4.4 11.7 %collective-permute-start.2 = (bf16[48,1536]{1,0:T(8,128)(2,1)S(1)}, bf16[48,1536]{1,0:T(8,128)(2,1)}, u32[]{:S(2)}, u32[]{:S(2)}) collective-permute-start(bf16[48,1536]{1,0:T(8,128)(2,1)S(1)} %pad_maximum_fusion.3.refs_0_), channel_id=1, source_target_pairs={{0,24},{2,26},{4,28},{6,30},{8,16},{10,18},{12,20},{14,22},{16,8},... | collective-permute-start | bytes 442376 | tf_op jit(solution)/shard_map/ppermute | solution.py:572
  9.5 12.6 %collective-permute-start.1 = (bf16[48,1536]{1,0:T(8,128)(2,1)S(1)}, bf16[48,1536]{1,0:T(8,128)(2,1)}, u32[]{:S(2)}, u32[]{:S(2)}) collective-permute-start(bf16[48,1536]{1,0:T(8,128)(2,1)S(1)} %pad_maximum_fusion.3.refs_0_), channel_id=1, source_target_pairs={{0,16},{2,18},{4,20},{6,22},{8,24},{10,26},{12,28},{14,30},{16,0},... | collective-permute-start | bytes 442376 | tf_op jit(solution)/shard_map/ppermute | solution.py:572
  9.5 12.6 %collective-permute-start = (bf16[48,1536]{1,0:T(8,128)(2,1)S(1)}, bf16[48,1536]{1,0:T(8,128)(2,1)}, u32[]{:S(2)}, u32[]{:S(2)}) collective-permute-start(bf16[48,1536]{1,0:T(8,128)(2,1)S(1)} %pad_maximum_fusion.3.refs_0_), channel_id=1, source_target_pairs={{0,8},{2,10},{4,12},{6,14},{8,0},{10,2},{12,4},{14,6},{16,24},{18,... | collective-permute-start | bytes 442376 | tf_op jit(solution)/shard_map/ppermute | solution.py:572
  23.2 17.3 %collective-permute-start.5 = (bf16[192,1536]{1,0:T(8,128)(2,1)S(1)}, bf16[192,1536]{1,0:T(8,128)(2,1)S(1)}, u32[]{:S(2)}, u32[]{:S(2)}) collective-permute-start(bf16[192,1536]{1,0:T(8,128)(2,1)S(1)} %join.3.a_ref.refs_0_), channel_id=1, source_target_pairs={{0,1},{1,0},{2,3},{3,2},{4,5},{5,4},{6,7},{7,6},{8,9},{9,8},{10,11... | collective-permute-start | bytes 1769480 | tf_op jit(solution)/shard_map/ppermute | solution.py:575
  24.7 15.7 %collective-permute-start.4 = (bf16[192,1536]{1,0:T(8,128)(2,1)S(1)}, bf16[192,1536]{1,0:T(8,128)(2,1)}, u32[]{:S(2)}, u32[]{:S(2)}) collective-permute-start(bf16[192,1536]{1,0:T(8,128)(2,1)S(1)} %join.3.a_ref.refs_0_), channel_id=1, source_target_pairs={{0,4},{2,6},{4,0},{6,2},{8,12},{10,14},{12,8},{14,10},{16,20},{18,... | collective-permute-start | bytes 1769480 | tf_op jit(solution)/shard_map/ppermute | solution.py:572
  29.3 11.1 %collective-permute-start.7 = (bf16[48,1536]{1,0:T(8,128)(2,1)S(1)}, bf16[48,1536]{1,0:T(8,128)(2,1)S(1)}, u32[]{:S(2)}, u32[]{:S(2)}) collective-permute-start(bf16[48,1536]{1,0:T(8,128)(2,1)S(1)} %convert_element_type.93.refs_0_), channel_id=1, source_target_pairs={{0,16},{2,18},{4,20},{6,22},{8,24},{10,26},{12,28},{14,30},{16,0},... | collective-permute-start | bytes 442376 | tf_op jit(solution)/shard_map/ppermute | solution.py:572
  29.3 11.1 %collective-permute-start.6 = (bf16[48,1536]{1,0:T(8,128)(2,1)S(1)}, bf16[48,1536]{1,0:T(8,128)(2,1)S(1)}, u32[]{:S(2)}, u32[]{:S(2)}) collective-permute-start(bf16[48,1536]{1,0:T(8,128)(2,1)S(1)} %convert_element_type.93.refs_0_), channel_id=1, source_target_pairs={{0,8},{2,10},{4,12},{6,14},{8,0},{10,2},{12,4},{14,6},{16,24},{18,... | collective-permute-start | bytes 442376 | tf_op jit(solution)/shard_map/ppermute | solution.py:572
  41.1 18.2 %collective-permute-start.13 = (bf16[48,1536]{1,0:T(8,128)(2,1)S(1)}, bf16[48,1536]{1,0:T(8,128)(2,1)S(1)}, u32[]{:S(2)}, u32[]{:S(2)}) collective-permute-start(bf16[48,1536]{1,0:T(8,128)(2,1)S(1)} %convert_bitcast_fusion.refs_0_), channel_id=1, source_target_pairs={{0,24},{2,26},{4,28},{6,30},{8,16},{10,18},{12,20},{14,22},{16,8},... | collective-permute-start | bytes 442376 | tf_op jit(solution)/shard_map/ppermute | solution.py:572
  42.6 16.7 %collective-permute-start.12 = (bf16[48,1536]{1,0:T(8,128)(2,1)S(1)}, bf16[48,1536]{1,0:T(8,128)(2,1)S(1)}, u32[]{:S(2)}, u32[]{:S(2)}) collective-permute-start(bf16[48,1536]{1,0:T(8,128)(2,1)S(1)} %convert_bitcast_fusion.refs_0_), channel_id=1, source_target_pairs={{0,16},{2,18},{4,20},{6,22},{8,24},{10,26},{12,28},{14,30},{16,0},... | collective-permute-start | bytes 442376 | tf_op jit(solution)/shard_map/ppermute | solution.py:572
  42.6 16.7 %collective-permute-start.11 = (bf16[48,1536]{1,0:T(8,128)(2,1)S(1)}, bf16[48,1536]{1,0:T(8,128)(2,1)S(1)}, u32[]{:S(2)}, u32[]{:S(2)}) collective-permute-start(bf16[48,1536]{1,0:T(8,128)(2,1)S(1)} %convert_bitcast_fusion.refs_0_), channel_id=1, source_target_pairs={{0,8},{2,10},{4,12},{6,14},{8,0},{10,2},{12,4},{14,6},{16,24},{18,... | collective-permute-start | bytes 442376 | tf_op jit(solution)/shard_map/ppermute | solution.py:572
  45.6 14.8 %collective-permute-start.9 = (bf16[192,1536]{1,0:T(8,128)(2,1)}, bf16[192,1536]{1,0:T(8,128)(2,1)S(1)}, u32[]{:S(2)}, u32[]{:S(2)}) collective-permute-start(bf16[192,1536]{1,0:T(8,128)(2,1)} %collective-permute-done.4.b_ref.refs_1_), channel_id=1, source_target_pairs={{0,1},{1,0},{2,3},{3,2},{4,5},{5,4},{6,7},{7,6},{8,9},{9,8},{10,11... | collective-permute-start | bytes 1769480 | tf_op jit(solution)/shard_map/ppermute | solution.py:575
  46.2 14.2 %collective-permute-start.10 = (bf16[192,1536]{1,0:T(8,128)(2,1)S(1)}, bf16[192,1536]{1,0:T(8,128)(2,1)S(1)}, u32[]{:S(2)}, u32[]{:S(2)}) collective-permute-start(bf16[192,1536]{1,0:T(8,128)(2,1)S(1)} %join.4.refs_0_), channel_id=1, source_target_pairs={{0,4},{2,6},{4,0},{6,2},{8,12},{10,14},{12,8},{14,10},{16,20},{18,... | collective-permute-start | bytes 1769480 | tf_op jit(solution)/shard_map/ppermute | solution.py:572
  61.0 15.3 %collective-permute-start.17 = (bf16[192,1536]{1,0:T(8,128)(2,1)S(1)}, bf16[192,1536]{1,0:T(8,128)(2,1)S(1)}, u32[]{:S(2)}, u32[]{:S(2)}) collective-permute-start(bf16[192,1536]{1,0:T(8,128)(2,1)S(1)} %join.5.refs_0_), channel_id=1, source_target_pairs={{0,4},{2,6},{4,0},{6,2},{8,12},{10,14},{12,8},{14,10},{16,20},{18,... | collective-permute-start | bytes 1769480 | tf_op jit(solution)/shard_map/ppermute | solution.py:572
  61.6 15.0 %collective-permute-start.16 = (bf16[192,1536]{1,0:T(8,128)(2,1)S(1)}, bf16[192,1536]{1,0:T(8,128)(2,1)S(1)}, u32[]{:S(2)}, u32[]{:S(2)}) collective-permute-start(bf16[192,1536]{1,0:T(8,128)(2,1)S(1)} %join.4.refs_0_), channel_id=1, source_target_pairs={{0,1},{1,0},{2,3},{3,2},{4,5},{5,4},{6,7},{7,6},{8,9},{9,8},{10,11... | collective-permute-start | bytes 1769480 | tf_op jit(solution)/shard_map/ppermute | solution.py:575
  76.6 16.1 %collective-permute-start.20 = (bf16[192,1536]{1,0:T(8,128)(2,1)S(1)}, bf16[192,1536]{1,0:T(8,128)(2,1)S(1)}, u32[]{:S(2)}, u32[]{:S(2)}) collective-permute-start(bf16[192,1536]{1,0:T(8,128)(2,1)S(1)} %collective-permute-done.16.refs_0_.refs_4_), channel_id=1, source_target_pairs={{0,4},{2,6},{4,0},{6,2},{8,12},{10,14},{12,8},{14,10},{16,20},{18,... | collective-permute-start | bytes 1769480 | tf_op jit(solution)/shard_map/ppermute | solution.py:572
  78.1 14.7 %collective-permute-start.21 = (bf16[192,1536]{1,0:T(8,128)(2,1)S(1)}, bf16[192,1536]{1,0:T(8,128)(2,1)S(1)}, u32[]{:S(2)}, u32[]{:S(2)}) collective-permute-start(bf16[192,1536]{1,0:T(8,128)(2,1)S(1)} %join.5.refs_0_), channel_id=1, source_target_pairs={{0,1},{1,0},{2,3},{3,2},{4,5},{5,4},{6,7},{7,6},{8,9},{9,8},{10,11... | collective-permute-start | bytes 1769480 | tf_op jit(solution)/shard_map/ppermute | solution.py:575
  93.3 15.4 %collective-permute-start.24 = (bf16[192,1536]{1,0:T(8,128)(2,1)S(1)}, bf16[192,1536]{1,0:T(8,128)(2,1)S(1)}, u32[]{:S(2)}, u32[]{:S(2)}) collective-permute-start(bf16[192,1536]{1,0:T(8,128)(2,1)S(1)} %collective-permute-done.21.refs_4_.refs_0_), channel_id=1, source_target_pairs={{0,4},{2,6},{4,0},{6,2},{8,12},{10,14},{12,8},{14,10},{16,20},{18,... | collective-permute-start | bytes 1769480 | tf_op jit(solution)/shard_map/ppermute | solution.py:572
  94.0 15.2 %collective-permute-start.27 = (bf16[192,1536]{1,0:T(8,128)(2,1)S(1)}, bf16[192,1536]{1,0:T(8,128)(2,1)S(1)}, u32[]{:S(2)}, u32[]{:S(2)}) collective-permute-start(bf16[192,1536]{1,0:T(8,128)(2,1)S(1)} %join.5.refs_0_), channel_id=1, source_target_pairs={{0,2},{2,0},{4,6},{6,4},{8,10},{10,8},{12,14},{14,12},{16,18},{18,... | collective-permute-start | bytes 1769480 | tf_op jit(solution)/shard_map/ppermute | solution.py:572
  94.0 15.2 %collective-permute-start.28 = (bf16[192,1536]{1,0:T(8,128)(2,1)S(1)}, bf16[192,1536]{1,0:T(8,128)(2,1)S(1)}, u32[]{:S(2)}, u32[]{:S(2)}) collective-permute-start(bf16[192,1536]{1,0:T(8,128)(2,1)S(1)} %collective-permute-done.17.refs_1_), channel_id=1, source_target_pairs={{0,2},{2,0},{4,6},{6,4},{8,10},{10,8},{12,14},{14,12},{16,18},{18,... | collective-permute-start | bytes 1769480 | tf_op jit(solution)/shard_map/ppermute | solution.py:572
  134.9 26.0 %collective-permute-start.34 = (bf16[192,1536]{1,0:T(8,128)(2,1)S(1)}, bf16[192,1536]{1,0:T(8,128)(2,1)S(1)}, u32[]{:S(2)}, u32[]{:S(2)}) collective-permute-start(bf16[192,1536]{1,0:T(8,128)(2,1)S(1)} %get-tuple-element.273), channel_id=1, source_target_pairs={{0,4},{2,6},{4,0},{6,2},{8,12},{10,14},{12,8},{14,10},{16,20},{18,... | collective-permute-start | bytes 1769480 | tf_op jit(solution)/shard_map/ppermute | solution.py:572
  135.6 25.4 %collective-permute-start.35 = (bf16[192,1536]{1,0:T(8,128)(2,1)S(1)}, bf16[192,1536]{1,0:T(8,128)(2,1)S(1)}, u32[]{:S(2)}, u32[]{:S(2)}) collective-permute-start(bf16[192,1536]{1,0:T(8,128)(2,1)S(1)} %get-tuple-element.274), channel_id=1, source_target_pairs={{0,1},{1,0},{2,3},{3,2},{4,5},{5,4},{6,7},{7,6},{8,9},{9,8},{10,11... | collective-permute-start | bytes 1769480 | tf_op jit(solution)/shard_map/ppermute | solution.py:575
  136.1 28.0 %collective-permute-start.36 = (bf16[192,1536]{1,0:T(8,128)(2,1)S(1)}, bf16[192,1536]{1,0:T(8,128)(2,1)S(1)}, u32[]{:S(2)}, u32[]{:S(2)}) collective-permute-start(bf16[192,1536]{1,0:T(8,128)(2,1)S(1)} %get-tuple-element.275), channel_id=1, source_target_pairs={{0,5},{1,4},{2,7},{3,6},{4,1},{5,0},{6,3},{7,2},{8,13},{9,12},{10,... | collective-permute-start | bytes 1769480 | tf_op jit(solution)/shard_map/ppermute | solution.py:579
  144.8 12.6 %collective-permute-start.33 = (bf16[384,3072]{1,0:T(8,128)(2,1)S(1)}, bf16[384,3072]{1,0:T(8,128)(2,1)S(1)}, u32[]{:S(2)}, u32[]{:S(2)}) collective-permute-start(bf16[384,3072]{1,0:T(8,128)(2,1)S(1)} %send_grads.6), channel_id=1, source_target_pairs={{0,2},{2,0},{4,6},{6,4},{8,10},{10,8},{12,14},{14,12},{16,18},{18,... | collective-permute-start | bytes 7077896 | tf_op jit(solution)/shard_map/ppermute | solution.py:572
  164.2 16.3 %collective-permute-start.38 = (bf16[192,1792]{1,0:T(8,128)(2,1)S(1)}, bf16[192,1792]{1,0:T(8,128)(2,1)S(1)}, u32[]{:S(2)}, u32[]{:S(2)}) collective-permute-start(bf16[192,1792]{1,0:T(8,128)(2,1)S(1)} %get-tuple-element.280), channel_id=1, source_target_pairs={{0,4},{2,6},{4,0},{6,2},{8,12},{10,14},{12,8},{14,10},{16,20},{18,... | collective-permute-start | bytes 2064392 | tf_op jit(solution)/shard_map/ppermute | solution.py:572
  164.8 18.2 %collective-permute-start.37 = (bf16[384,1024]{1,0:T(8,128)(2,1)S(1)}, bf16[384,1024]{1,0:T(8,128)(2,1)S(1)}, u32[]{:S(2)}, u32[]{:S(2)}) collective-permute-start(bf16[384,1024]{1,0:T(8,128)(2,1)S(1)} %get-tuple-element.279), channel_id=1, source_target_pairs={{0,1},{1,0},{2,3},{3,2},{4,5},{5,4},{6,7},{7,6},{8,9},{9,8},{10,11... | collective-permute-start | bytes 2359304 | tf_op jit(solution)/shard_map/ppermute | solution.py:575
  165.7 12.6 %collective-permute-start.39 = (bf16[96,1536]{1,0:T(8,128)(2,1)S(1)}, bf16[96,1536]{1,0:T(8,128)(2,1)S(1)}, u32[]{:S(2)}, u32[]{:S(2)}) collective-permute-start(bf16[96,1536]{1,0:T(8,128)(2,1)S(1)} %pad_maximum_fusion.2), channel_id=1, source_target_pairs={{0,8},{2,10},{4,12},{6,14},{8,0},{10,2},{12,4},{14,6},{16,24},{18,... | collective-permute-start | bytes 884744 | tf_op jit(solution)/shard_map/ppermute | solution.py:572
  184.2 11.3 %collective-permute-start.41 = (bf16[192,1024]{1,0:T(8,128)(2,1)S(1)}, bf16[192,1024]{1,0:T(8,128)(2,1)S(1)}, u32[]{:S(2)}, u32[]{:S(2)}) collective-permute-start(bf16[192,1024]{1,0:T(8,128)(2,1)S(1)} %add_convert_fusion), channel_id=1, source_target_pairs={{0,4},{2,6},{4,0},{6,2},{8,12},{10,14},{12,8},{14,10},{16,20},{18,... | collective-permute-start | bytes 1179656 | tf_op jit(solution)/shard_map/ppermute | solution.py:572
  195.9 24.4 %collective-permute-start.45 = (bf16[384,1152]{1,0:T(8,128)(2,1)S(1)}, bf16[384,1152]{1,0:T(8,128)(2,1)S(1)}, u32[]{:S(2)}, u32[]{:S(2)}) collective-permute-start(bf16[384,1152]{1,0:T(8,128)(2,1)S(1)} %keep_grads.6), channel_id=1, source_target_pairs={{0,1},{1,0},{2,3},{3,2},{4,5},{5,4},{6,7},{7,6},{8,9},{9,8},{10,11... | collective-permute-start | bytes 2654216 | tf_op jit(solution)/shard_map/ppermute | solution.py:575
  197.5 22.7 %collective-permute-start.46 = (bf16[96,1920]{1,0:T(8,128)(2,1)S(1)}, bf16[96,1920]{1,0:T(8,128)(2,1)S(1)}, u32[]{:S(2)}, u32[]{:S(2)}) collective-permute-start(bf16[96,1920]{1,0:T(8,128)(2,1)S(1)} %pad_maximum_fusion.1), channel_id=1, source_target_pairs={{0,8},{2,10},{4,12},{6,14},{8,0},{10,2},{12,4},{14,6},{16,24},{18,... | collective-permute-start | bytes 1105928 | tf_op jit(solution)/shard_map/ppermute | solution.py:572
  199.3 21.0 %collective-permute-start.44 = (f32[16,768]{1,0:T(8,128)S(1)}, f32[16,768]{1,0:T(8,128)S(1)}, u32[]{:S(2)}, u32[]{:S(2)}) collective-permute-start(f32[16,768]{1,0:T(8,128)S(1)} %order.4), channel_id=1, source_target_pairs={{0,1},{1,0},{2,3},{3,2},{4,5},{5,4},{6,7},{7,6},{8,9},{9,8},{10,11... | collective-permute-start | bytes 147464 | tf_op jit(solution)/shard_map/ppermute | solution.py:575
  222.2 16.6 %collective-permute-start.52 = (bf16[48,1920]{1,0:T(8,128)(2,1)S(1)}, bf16[48,1920]{1,0:T(8,128)(2,1)S(1)}, u32[]{:S(2)}, u32[]{:S(2)}) collective-permute-start(bf16[48,1920]{1,0:T(8,128)(2,1)S(1)} %add_convert_fusion.2), channel_id=1, source_target_pairs={{0,16},{2,18},{4,20},{6,22},{8,24},{10,26},{12,28},{14,30},{16,0},... | collective-permute-start | bytes 552968 | tf_op jit(solution)/shard_map/ppermute | solution.py:572
  227.5 11.4 %collective-permute-start.51 = (f32[16,768]{1,0:T(8,128)S(1)}, f32[16,768]{1,0:T(8,128)S(1)}, u32[]{:S(2)}, u32[]{:S(2)}) collective-permute-start(f32[16,768]{1,0:T(8,128)S(1)} %add.101), channel_id=1, source_target_pairs={{0,8},{2,10},{4,12},{6,14},{8,0},{10,2},{12,4},{14,6},{16,24},{18,... | collective-permute-start | bytes 147464 | tf_op jit(solution)/shard_map/ppermute | solution.py:572
  (49 other events, 324.1 us)
